TPU v7x, 32 devices: a whole 2x2x4 slice. The times are simulated.
32 devices in a mesh: gx: 4 (over y, core), gy: 4 (over z), lev: 2 (over x).
Axes of the slice: x: 2, y: 2, z: 4, core: 2. Of those that a mesh axis runs over, the one named last changes fastest.
Arguments:
- east_wind: float32 [136, 128, 512], P('lev', 'gx', 'gy'), may hold values from -6 to 6
- north_wind: float32 [136, 128, 512], P('lev', 'gx', 'gy'), may hold values from -6 to 6
- height: float32 [136, 128, 512], P('lev', 'gx', 'gy'), may hold values from -6 to 6
- to_modes: float32 [136, 136], replicated, may hold values from -0.5 to 0.5
- to_levels: float32 [136, 136], replicated, may hold values from -0.5 to 0.5
- mode_coef: float32 [136], replicated, may hold values from 0.05 to 20
Outputs:
- east_next: float32 [136, 128, 512], P('lev', 'gx', 'gy')
- north_next: float32 [136, 128, 512], P('lev', 'gx', 'gy')
- height_next: float32 [136, 128, 512], P('lev', 'gx', 'gy')
All inputs are finite; a program needn't handle non-finite values.
Results may differ from a plain program's by a relative error of at most 0.000073.
Values sent between devices are 32-bit elements; how exact they have to be, the bound alone decides.
No kernel may reach another device: no remote copies, remote signals or barrier semaphores. Data moves between devices by JAX's collectives and lax.ppermute only.
A program may use at most 64 MiB of HBM per device.

v0:
```python
import jax
import jax.numpy as jnp
from jax import lax
from jax.sharding import PartitionSpec as P

SWEEPS = 6


def with_halo(value, sides, width):
    for axis, dim in sides:
        peers, length = (lax.axis_size(axis), value.shape[dim])
        up = [(i, (i + 1) % peers) for i in range(peers - 1)]
        down = [(j, i) for i, j in up]
        last = lax.slice_in_dim(value, length - width, length, axis=dim)
        initial = lax.slice_in_dim(value, 0, width, axis=dim)
        before = lax.ppermute(last, axis, up)
        after = lax.ppermute(initial, axis, down)
        value = jnp.concatenate([before, value, after], axis=dim)
    return value


def east_diff(padded):
    return (
        8.0 * (padded[..., 3:-1, 2:-2] - padded[..., 1:-3, 2:-2])
        - (padded[..., 4:, 2:-2] - padded[..., :-4, 2:-2])
    ) / 12.0


def north_diff(padded):
    return (
        8.0 * (padded[..., 2:-2, 3:-1] - padded[..., 2:-2, 1:-3])
        - (padded[..., 2:-2, 4:] - padded[..., 2:-2, :-4])
    ) / 12.0


def on_device(east_wind, north_wind, height, to_modes, to_levels, mode_coef):
    levels_dev = east_wind.shape[0]
    row_cells = east_wind.shape[1]
    col_cells = east_wind.shape[2]
    winds = jnp.stack([east_wind, north_wind])
    padded = with_halo(winds, (("gx", 2), ("gy", 3)), 2)
    diverge = east_diff(padded[0]) + north_diff(padded[1])
    source = height - diverge
    first_level = lax.axis_index("lev") * levels_dev
    stiff = lax.dynamic_slice_in_dim(mode_coef, first_level, levels_dev)[:, None, None]
    my_columns = lax.dynamic_slice_in_dim(to_modes, first_level, levels_dev, 1)
    flat_source = source.reshape(levels_dev, -1)
    block = my_columns
    modal = lax.psum_scatter(
        jnp.dot(
            block, flat_source, precision=lax.Precision.HIGHEST, preferred_element_type=jnp.float32
        ),
        "lev",
        scatter_dimension=0,
        tiled=True,
    ).reshape(levels_dev, row_cells, col_cells)
    denom = 1.0 + 4.0 * stiff
    solved = modal / denom
    for sweep_index in range(SWEEPS):
        edged = with_halo(solved, (("gx", 1), ("gy", 2)), 1)
        beside_all = (
            edged[:, 2:, 1:-1] + edged[:, :-2, 1:-1] + edged[:, 1:-1, 2:] + edged[:, 1:-1, :-2]
        )
        solved = (modal + stiff * beside_all) / denom
    my_rows = lax.dynamic_slice_in_dim(to_levels, first_level, levels_dev, 0)
    piece = lax.all_gather(solved, "lev", axis=0, tiled=True)
    block = my_rows
    flat_piece = piece.reshape(piece.shape[0], -1)
    summed = jnp.dot(
        block, flat_piece, precision=lax.Precision.HIGHEST, preferred_element_type=jnp.float32
    )
    height_next = summed.reshape(levels_dev, row_cells, col_cells)
    edged_height = with_halo(height_next, (("gx", 1), ("gy", 2)), 2)
    return (east_wind - east_diff(edged_height), north_wind - north_diff(edged_height), height_next)


def solution(mesh):
    return jax.shard_map(
        on_device,
        mesh=mesh,
        in_specs=(P("lev", "gx", "gy"), P("lev", "gx", "gy"), P("lev", "gx", "gy"), P(), P(), P()),
        out_specs=(P("lev", "gx", "gy"), P("lev", "gx", "gy"), P("lev", "gx", "gy")),
        check_vma=False,
    )
```

profile of v0, /device:TPU:1, one launch (start us, length us, event | category | flops | bytes accessed | tf_op | source)
XLA Modules:
  0.0 282.7 jit_solution(13165422543526540478)
XLA Ops:
  10.2 4.5 %collective-permute-start = (f32[2,68,2,128]{3,1,2,0:T(8,128)S(1)}, f32[2,68,2,128]{3,1,2,0:T(8,128)S(1)}, u32[]{:S(2)}, u32[]{:S(2)}) collective-permute-start(f32[2,68,2,128]{3,1,2,0:T(8,128)S(1)} %get-tuple-element.18), channel_id=1, source_target_pairs={{0,8},{8,16},{16,24},{1,9},{9,17},{17,25},{2,10},{10,18},{18,26},{... | collective-permute-start | bytes 417800 | tf_op jit(solution)/shard_map/ppermute | solution.py:16
  16.8 4.4 %collective-permute-done.1 = f32[2,68,2,128]{3,1,2,0:T(8,128)S(1)} collective-permute-done((f32[2,68,2,128]{3,1,2,0:T(8,128)S(1)}, f32[2,68,2,128]{3,1,2,0:T(8,128)S(1)}, u32[]{:S(2)}, u32[]{:S(2)}) %collective-permute-start.1) | collective-permute-done | bytes 139296 | tf_op jit(solution)/shard_map/ppermute | solution.py:17
  40.7 6.2 %pad_maximum_fusion = f32[2,68,36,132]{3,1,2,0:T(8,128)S(1)} fusion(f32[2,68,36,2]{3,1,2,0:T(8,128)} %copy.35, f32[2,68,2,128]{3,1,2,0:T(8,128)S(1)} %collective-permute-done.1, f32[1,68,32,128]{3,1,2,0:T(8,128)S(1)} %get-tuple-element.49, f32[1,68,32,128]{3,1,2,0:T(8,128)S(1)} %get-tuple-element.48, f32[2,68,2,128]{3,1,2,0:T(8,128)S(1)} %collective-permute-done, ...), kind=kLoop, calls=%fused_computation | loop fusion | flops 3231360 | bytes 5170176 | tf_op jit(solution)/shard_map/concatenate | solution.py:18
  53.3 30.1 %fusion = f32[72,4096]{1,0:T(8,128)S(1)} fusion(f32[136,4096]{1,0:T(8,128)S(1)} %fusion.62), kind=kCustom, calls=%all-reduce-scatter | all-reduce-scatter fusion | flops 589825 | bytes 3408384
  97.8 4.0 %collective-permute-start.7 = (f32[68,34,1]{0,2,1:T(1,128)S(1)}, f32[68,34,1]{0,2,1:T(1,128)S(1)}, u32[]{:S(2)}, u32[]{:S(2)}) collective-permute-start(f32[68,34,1]{0,2,1:T(1,128)S(1)} %get-tuple-element.31), channel_id=1, source_target_pairs={{0,2},{2,4},{4,6},{1,3},{3,5},{5,7},{8,10},{10,12},{12,14},{9,11},... | collective-permute-start | bytes 27752 | tf_op jit(solution)/shard_map/ppermute | solution.py:16
  102.6 3.7 %fusion.37 = f32[68,32,128]{0,2,1:T(8,128)S(1)} fusion(f32[68,32,128]{0,2,1:T(8,128)S(1)} %bitcast.34, f32[68,34,1]{0,2,1:T(1,128)S(1)} %collective-permute-done.7, f32[68,1,128]{0,2,1:T(8,128)S(1)} %collective-permute-done.4, f32[68,32,128]{0,2,1:T(8,128)S(1)} %broadcast_divide_fusion, f32[68,1,128]{0,2,1:T(8,128)S(1)} %collective-permute-done.5, ...), kind=kLoop, calls=%fused_computation.82 | loop fusion | flops 3899392 | bytes 3431008 | tf_op jit(solution)/shard_map/div | solution.py:64
  108.3 5.4 %collective-permute-start.9 = (f32[68,1,128]{0,2,1:T(8,128)S(1)}, f32[68,1,128]{0,2,1:T(8,128)S(1)}, u32[]{:S(2)}, u32[]{:S(2)}) collective-permute-start(f32[68,1,128]{0,2,1:T(8,128)S(1)} %get-tuple-element.40), channel_id=1, source_target_pairs={{0,8},{8,16},{16,24},{1,9},{9,17},{17,25},{2,10},{10,18},{18,26},{... | collective-permute-start | bytes 104456 | tf_op jit(solution)/shard_map/ppermute | solution.py:16
  116.3 4.8 %collective-permute-start.11 = (f32[68,34,1]{0,2,1:T(1,128)S(1)}, f32[68,34,1]{0,2,1:T(1,128)S(1)}, u32[]{:S(2)}, u32[]{:S(2)}) collective-permute-start(f32[68,34,1]{0,2,1:T(1,128)S(1)} %get-tuple-element.29), channel_id=1, source_target_pairs={{0,2},{2,4},{4,6},{1,3},{3,5},{5,7},{8,10},{10,12},{12,14},{9,11},... | collective-permute-start | bytes 27752 | tf_op jit(solution)/shard_map/ppermute | solution.py:16
  121.7 3.7 %fusion.31 = f32[68,32,128]{0,2,1:T(8,128)S(1)} fusion(f32[68,32,128]{0,2,1:T(8,128)S(1)} %bitcast.35, f32[68,34,1]{0,2,1:T(1,128)S(1)} %collective-permute-done.11, f32[68,1,128]{0,2,1:T(8,128)S(1)} %collective-permute-done.8, f32[68,32,128]{0,2,1:T(8,128)S(1)} %fusion.37, f32[68,1,128]{0,2,1:T(8,128)S(1)} %collective-permute-done.9, ...), kind=kLoop, calls=%fused_computation.68 | loop fusion | flops 3899392 | bytes 3431008 | tf_op jit(solution)/shard_map/div | solution.py:64
  127.4 5.1 %collective-permute-start.13 = (f32[68,1,128]{0,2,1:T(8,128)S(1)}, f32[68,1,128]{0,2,1:T(8,128)S(1)}, u32[]{:S(2)}, u32[]{:S(2)}) collective-permute-start(f32[68,1,128]{0,2,1:T(8,128)S(1)} %get-tuple-element.38), channel_id=1, source_target_pairs={{0,8},{8,16},{16,24},{1,9},{9,17},{17,25},{2,10},{10,18},{18,26},{... | collective-permute-start | bytes 104456 | tf_op jit(solution)/shard_map/ppermute | solution.py:16
  135.2 4.6 %collective-permute-start.15 = (f32[68,34,1]{0,2,1:T(1,128)S(1)}, f32[68,34,1]{0,2,1:T(1,128)S(1)}, u32[]{:S(2)}, u32[]{:S(2)}) collective-permute-start(f32[68,34,1]{0,2,1:T(1,128)S(1)} %get-tuple-element.27), channel_id=1, source_target_pairs={{0,2},{2,4},{4,6},{1,3},{3,5},{5,7},{8,10},{10,12},{12,14},{9,11},... | collective-permute-start | bytes 27752 | tf_op jit(solution)/shard_map/ppermute | solution.py:16
  140.6 3.7 %fusion.25 = f32[68,32,128]{0,2,1:T(8,128)S(1)} fusion(f32[68,32,128]{0,2,1:T(8,128)S(1)} %bitcast.36, f32[68,34,1]{0,2,1:T(1,128)S(1)} %collective-permute-done.15, f32[68,1,128]{0,2,1:T(8,128)S(1)} %collective-permute-done.12, f32[68,32,128]{0,2,1:T(8,128)S(1)} %fusion.31, f32[68,1,128]{0,2,1:T(8,128)S(1)} %collective-permute-done.13, ...), kind=kLoop, calls=%fused_computation.54 | loop fusion | flops 3899392 | bytes 3431008 | tf_op jit(solution)/shard_map/div | solution.py:64
  146.2 5.1 %collective-permute-start.17 = (f32[68,1,128]{0,2,1:T(8,128)S(1)}, f32[68,1,128]{0,2,1:T(8,128)S(1)}, u32[]{:S(2)}, u32[]{:S(2)}) collective-permute-start(f32[68,1,128]{0,2,1:T(8,128)S(1)} %get-tuple-element.36), channel_id=1, source_target_pairs={{0,8},{8,16},{16,24},{1,9},{9,17},{17,25},{2,10},{10,18},{18,26},{... | collective-permute-start | bytes 104456 | tf_op jit(solution)/shard_map/ppermute | solution.py:16
  154.0 4.6 %collective-permute-start.19 = (f32[68,34,1]{0,2,1:T(1,128)S(1)}, f32[68,34,1]{0,2,1:T(1,128)S(1)}, u32[]{:S(2)}, u32[]{:S(2)}) collective-permute-start(f32[68,34,1]{0,2,1:T(1,128)S(1)} %get-tuple-element.25), channel_id=1, source_target_pairs={{0,2},{2,4},{4,6},{1,3},{3,5},{5,7},{8,10},{10,12},{12,14},{9,11},... | collective-permute-start | bytes 27752 | tf_op jit(solution)/shard_map/ppermute | solution.py:16
  159.4 3.7 %fusion.19 = f32[68,32,128]{0,2,1:T(8,128)S(1)} fusion(f32[68,32,128]{0,2,1:T(8,128)S(1)} %bitcast.37, f32[68,34,1]{0,2,1:T(1,128)S(1)} %collective-permute-done.19, f32[68,1,128]{0,2,1:T(8,128)S(1)} %collective-permute-done.16, f32[68,32,128]{0,2,1:T(8,128)S(1)} %fusion.25, f32[68,1,128]{0,2,1:T(8,128)S(1)} %collective-permute-done.17, ...), kind=kLoop, calls=%fused_computation.40 | loop fusion | flops 3899392 | bytes 3431008 | tf_op jit(solution)/shard_map/div | solution.py:64
  165.1 5.1 %collective-permute-start.21 = (f32[68,1,128]{0,2,1:T(8,128)S(1)}, f32[68,1,128]{0,2,1:T(8,128)S(1)}, u32[]{:S(2)}, u32[]{:S(2)}) collective-permute-start(f32[68,1,128]{0,2,1:T(8,128)S(1)} %get-tuple-element.34), channel_id=1, source_target_pairs={{0,8},{8,16},{16,24},{1,9},{9,17},{17,25},{2,10},{10,18},{18,26},{... | collective-permute-start | bytes 104456 | tf_op jit(solution)/shard_map/ppermute | solution.py:16
  172.9 4.6 %collective-permute-start.23 = (f32[68,34,1]{0,2,1:T(1,128)S(1)}, f32[68,34,1]{0,2,1:T(1,128)S(1)}, u32[]{:S(2)}, u32[]{:S(2)}) collective-permute-start(f32[68,34,1]{0,2,1:T(1,128)S(1)} %get-tuple-element.23), channel_id=1, source_target_pairs={{0,2},{2,4},{4,6},{1,3},{3,5},{5,7},{8,10},{10,12},{12,14},{9,11},... | collective-permute-start | bytes 27752 | tf_op jit(solution)/shard_map/ppermute | solution.py:16
  183.9 5.1 %collective-permute-start.25 = (f32[68,1,128]{0,2,1:T(8,128)S(1)}, f32[68,1,128]{0,2,1:T(8,128)S(1)}, u32[]{:S(2)}, u32[]{:S(2)}) collective-permute-start(f32[68,1,128]{0,2,1:T(8,128)S(1)} %get-tuple-element.32), channel_id=1, source_target_pairs={{0,8},{8,16},{16,24},{1,9},{9,17},{17,25},{2,10},{10,18},{18,26},{... | collective-permute-start | bytes 104456 | tf_op jit(solution)/shard_map/ppermute | solution.py:16
  191.7 4.8 %collective-permute-start.27 = (f32[68,34,1]{0,2,1:T(1,128)S(1)}, f32[68,34,1]{0,2,1:T(1,128)S(1)}, u32[]{:S(2)}, u32[]{:S(2)}) collective-permute-start(f32[68,34,1]{0,2,1:T(1,128)S(1)} %get-tuple-element.21), channel_id=1, source_target_pairs={{0,2},{2,4},{4,6},{1,3},{3,5},{5,7},{8,10},{10,12},{12,14},{9,11},... | collective-permute-start | bytes 27752 | tf_op jit(solution)/shard_map/ppermute | solution.py:16
  197.1 4.6 %fusion.7 = f32[68,32,128]{0,2,1:T(8,128)} fusion(f32[68,32,128]{0,2,1:T(8,128)S(1)} %bitcast.39, f32[68,34,1]{0,2,1:T(1,128)S(1)} %collective-permute-done.27, f32[68,1,128]{0,2,1:T(8,128)S(1)} %collective-permute-done.24, f32[68,32,128]{0,2,1:T(8,128)S(1)} %fusion.13, f32[68,1,128]{0,2,1:T(8,128)S(1)} %collective-permute-done.25, ...), kind=kLoop, calls=%fused_computation.12 | loop fusion | flops 3899392 | bytes 3431008 | tf_op jit(solution)/shard_map/div | solution.py:64
  204.6 40.0 %all-gather.2.cloned.1.call-done = f32[136,32,128]{2,1,0:T(8,128)} async-done(((f32[68,32,128]{2,1,0:T(8,128)}), f32[136,32,128]{2,1,0:T(8,128)}) %all-gather.2.cloned.1.call-update) | async-done | bytes 2228240 | tf_op jit(solution)/shard_map/all_gather | solution.py:66
  244.6 4.2 %fusion.1 = f32[68,32,128]{2,0,1:T(8,128)S(1)} fusion(f32[136,136]{1,0:T(8,128)S(1)} %copy-done.3, s32[]{:T(128)S(6)} %select_n.2, f32[17,8,32,128]{3,2,1,0:T(8,128)} %bitcast.42), kind=kOutput, calls=%fused_computation.5 | convolution fusion | flops 454557696 | bytes 3416068 | tf_op jit(solution)/shard_map/dot_general | solution.py:69
  261.0 4.0 %collective-permute-start.31 = (f32[68,36,2]{0,2,1:T(2,128)S(1)}, f32[68,36,2]{0,2,1:T(2,128)S(1)}, u32[]{:S(2)}, u32[]{:S(2)}) collective-permute-start(f32[68,36,2]{0,2,1:T(2,128)S(1)} %copy.50), channel_id=1, source_target_pairs={{0,2},{2,4},{4,6},{1,3},{3,5},{5,7},{8,10},{10,12},{12,14},{9,11},... | collective-permute-start | bytes 58760 | tf_op jit(solution)/shard_map/ppermute | solution.py:16
  270.4 4.3 %fusion.50 = f32[68,32,128]{2,0,1:T(8,128)S(1)} fusion(f32[68,36,2]{2,0,1:T(8,128)} %copy.51, f32[68,2,128]{2,0,1:T(8,128)S(1)} %collective-permute-done.28, f32[68,32,128]{2,0,1:T(8,128)S(1)} %fusion.1, f32[68,2,128]{2,0,1:T(8,128)S(1)} %collective-permute-done.29, f32[68,36,2]{2,0,1:T(8,128)S(1)} %copy.49, f32[68,32,128]{2,1,0:T(8,128)} %param.7), kind=kLoop, calls=%fused_computation.108 | loop fusion | flops 5013504 | bytes 3520768 | tf_op jit(solution)/shard_map/sub | solution.py:74
  (112 shorter events, 97.3 us)
Async XLA Ops:
  7.2 237.4 %all-gather.2.cloned.1.call-start = ((), (), s32[]{:S(2)}) async-start(), calls=%async_computation | async-start | bytes 3342336 | tf_op jit(solution)/shard_map/all_gather | solution.py:66
  10.2 6.6 %collective-permute-start = (f32[2,68,2,128]{3,1,2,0:T(8,128)S(1)}, f32[2,68,2,128]{3,1,2,0:T(8,128)S(1)}, u32[]{:S(2)}, u32[]{:S(2)}) collective-permute-start(f32[2,68,2,128]{3,1,2,0:T(8,128)S(1)} %get-tuple-element.18), channel_id=1, source_target_pairs={{0,8},{8,16},{16,24},{1,9},{9,17},{17,25},{2,10},{10,18},{18,26},{... | collective-permute-start | bytes 417800 | tf_op jit(solution)/shard_map/ppermute | solution.py:16
  14.7 6.5 %collective-permute-start.1 = (f32[2,68,2,128]{3,1,2,0:T(8,128)S(1)}, f32[2,68,2,128]{3,1,2,0:T(8,128)S(1)}, u32[]{:S(2)}, u32[]{:S(2)}) collective-permute-start(f32[2,68,2,128]{3,1,2,0:T(8,128)S(1)} %get-tuple-element.19), channel_id=1, source_target_pairs={{8,0},{16,8},{24,16},{9,1},{17,9},{25,17},{10,2},{18,10},{26,18},{... | collective-permute-start | bytes 417800 | tf_op jit(solution)/shard_map/ppermute | solution.py:17
  27.2 8.6 %collective-permute-start.2 = (f32[2,68,36,2]{1,3,2,0:T(2,128)S(1)}, f32[2,68,36,2]{1,3,2,0:T(2,128)S(1)}, u32[]{:S(2)}, u32[]{:S(2)}) collective-permute-start(f32[2,68,36,2]{1,3,2,0:T(2,128)S(1)} %copy.32), channel_id=1, source_target_pairs={{0,2},{2,4},{4,6},{1,3},{3,5},{5,7},{8,10},{10,12},{12,14},{9,11},... | collective-permute-start | bytes 117512 | tf_op jit(solution)/shard_map/ppermute | solution.py:16
  89.5 5.6 %collective-permute-start.4 = (f32[68,1,128]{0,2,1:T(8,128)S(1)}, f32[68,1,128]{0,2,1:T(8,128)S(1)}, u32[]{:S(2)}, u32[]{:S(2)}) collective-permute-start(f32[68,1,128]{0,2,1:T(8,128)S(1)} %get-tuple-element.43), channel_id=1, source_target_pairs={{8,0},{16,8},{24,16},{9,1},{17,9},{25,17},{10,2},{18,10},{26,18},{... | collective-permute-start | bytes 104456 | tf_op jit(solution)/shard_map/ppermute | solution.py:17
  106.3 7.3 %collective-permute-start.8 = (f32[68,1,128]{0,2,1:T(8,128)S(1)}, f32[68,1,128]{0,2,1:T(8,128)S(1)}, u32[]{:S(2)}, u32[]{:S(2)}) collective-permute-start(f32[68,1,128]{0,2,1:T(8,128)S(1)} %get-tuple-element.41), channel_id=1, source_target_pairs={{8,0},{16,8},{24,16},{9,1},{17,9},{25,17},{10,2},{18,10},{26,18},{... | collective-permute-start | bytes 104456 | tf_op jit(solution)/shard_map/ppermute | solution.py:17
  108.3 6.7 %collective-permute-start.9 = (f32[68,1,128]{0,2,1:T(8,128)S(1)}, f32[68,1,128]{0,2,1:T(8,128)S(1)}, u32[]{:S(2)}, u32[]{:S(2)}) collective-permute-start(f32[68,1,128]{0,2,1:T(8,128)S(1)} %get-tuple-element.40), channel_id=1, source_target_pairs={{0,8},{8,16},{16,24},{1,9},{9,17},{17,25},{2,10},{10,18},{18,26},{... | collective-permute-start | bytes 104456 | tf_op jit(solution)/shard_map/ppermute | solution.py:16
  115.0 6.1 %collective-permute-start.10 = (f32[68,34,1]{0,2,1:T(1,128)S(1)}, f32[68,34,1]{0,2,1:T(1,128)S(1)}, u32[]{:S(2)}, u32[]{:S(2)}) collective-permute-start(f32[68,34,1]{0,2,1:T(1,128)S(1)} %get-tuple-element.28), channel_id=1, source_target_pairs={{2,0},{4,2},{6,4},{3,1},{5,3},{7,5},{10,8},{12,10},{14,12},{11,9},... | collective-permute-start | bytes 27752 | tf_op jit(solution)/shard_map/ppermute | solution.py:17
  116.3 5.4 %collective-permute-start.11 = (f32[68,34,1]{0,2,1:T(1,128)S(1)}, f32[68,34,1]{0,2,1:T(1,128)S(1)}, u32[]{:S(2)}, u32[]{:S(2)}) collective-permute-start(f32[68,34,1]{0,2,1:T(1,128)S(1)} %get-tuple-element.29), channel_id=1, source_target_pairs={{0,2},{2,4},{4,6},{1,3},{3,5},{5,7},{8,10},{10,12},{12,14},{9,11},... | collective-permute-start | bytes 27752 | tf_op jit(solution)/shard_map/ppermute | solution.py:16
  125.5 7.1 %collective-permute-start.12 = (f32[68,1,128]{0,2,1:T(8,128)S(1)}, f32[68,1,128]{0,2,1:T(8,128)S(1)}, u32[]{:S(2)}, u32[]{:S(2)}) collective-permute-start(f32[68,1,128]{0,2,1:T(8,128)S(1)} %get-tuple-element.39), channel_id=1, source_target_pairs={{8,0},{16,8},{24,16},{9,1},{17,9},{25,17},{10,2},{18,10},{26,18},{... | collective-permute-start | bytes 104456 | tf_op jit(solution)/shard_map/ppermute | solution.py:17
  127.4 6.4 %collective-permute-start.13 = (f32[68,1,128]{0,2,1:T(8,128)S(1)}, f32[68,1,128]{0,2,1:T(8,128)S(1)}, u32[]{:S(2)}, u32[]{:S(2)}) collective-permute-start(f32[68,1,128]{0,2,1:T(8,128)S(1)} %get-tuple-element.38), channel_id=1, source_target_pairs={{0,8},{8,16},{16,24},{1,9},{9,17},{17,25},{2,10},{10,18},{18,26},{... | collective-permute-start | bytes 104456 | tf_op jit(solution)/shard_map/ppermute | solution.py:16
  133.9 5.9 %collective-permute-start.14 = (f32[68,34,1]{0,2,1:T(1,128)S(1)}, f32[68,34,1]{0,2,1:T(1,128)S(1)}, u32[]{:S(2)}, u32[]{:S(2)}) collective-permute-start(f32[68,34,1]{0,2,1:T(1,128)S(1)} %get-tuple-element.26), channel_id=1, source_target_pairs={{2,0},{4,2},{6,4},{3,1},{5,3},{7,5},{10,8},{12,10},{14,12},{11,9},... | collective-permute-start | bytes 27752 | tf_op jit(solution)/shard_map/ppermute | solution.py:17
  144.3 7.1 %collective-permute-start.16 = (f32[68,1,128]{0,2,1:T(8,128)S(1)}, f32[68,1,128]{0,2,1:T(8,128)S(1)}, u32[]{:S(2)}, u32[]{:S(2)}) collective-permute-start(f32[68,1,128]{0,2,1:T(8,128)S(1)} %get-tuple-element.37), channel_id=1, source_target_pairs={{8,0},{16,8},{24,16},{9,1},{17,9},{25,17},{10,2},{18,10},{26,18},{... | collective-permute-start | bytes 104456 | tf_op jit(solution)/shard_map/ppermute | solution.py:17
  146.2 6.4 %collective-permute-start.17 = (f32[68,1,128]{0,2,1:T(8,128)S(1)}, f32[68,1,128]{0,2,1:T(8,128)S(1)}, u32[]{:S(2)}, u32[]{:S(2)}) collective-permute-start(f32[68,1,128]{0,2,1:T(8,128)S(1)} %get-tuple-element.36), channel_id=1, source_target_pairs={{0,8},{8,16},{16,24},{1,9},{9,17},{17,25},{2,10},{10,18},{18,26},{... | collective-permute-start | bytes 104456 | tf_op jit(solution)/shard_map/ppermute | solution.py:16
  152.7 5.9 %collective-permute-start.18 = (f32[68,34,1]{0,2,1:T(1,128)S(1)}, f32[68,34,1]{0,2,1:T(1,128)S(1)}, u32[]{:S(2)}, u32[]{:S(2)}) collective-permute-start(f32[68,34,1]{0,2,1:T(1,128)S(1)} %get-tuple-element.24), channel_id=1, source_target_pairs={{2,0},{4,2},{6,4},{3,1},{5,3},{7,5},{10,8},{12,10},{14,12},{11,9},... | collective-permute-start | bytes 27752 | tf_op jit(solution)/shard_map/ppermute | solution.py:17
  163.1 7.1 %collective-permute-start.20 = (f32[68,1,128]{0,2,1:T(8,128)S(1)}, f32[68,1,128]{0,2,1:T(8,128)S(1)}, u32[]{:S(2)}, u32[]{:S(2)}) collective-permute-start(f32[68,1,128]{0,2,1:T(8,128)S(1)} %get-tuple-element.35), channel_id=1, source_target_pairs={{8,0},{16,8},{24,16},{9,1},{17,9},{25,17},{10,2},{18,10},{26,18},{... | collective-permute-start | bytes 104456 | tf_op jit(solution)/shard_map/ppermute | solution.py:17
  165.1 6.4 %collective-permute-start.21 = (f32[68,1,128]{0,2,1:T(8,128)S(1)}, f32[68,1,128]{0,2,1:T(8,128)S(1)}, u32[]{:S(2)}, u32[]{:S(2)}) collective-permute-start(f32[68,1,128]{0,2,1:T(8,128)S(1)} %get-tuple-element.34), channel_id=1, source_target_pairs={{0,8},{8,16},{16,24},{1,9},{9,17},{17,25},{2,10},{10,18},{18,26},{... | collective-permute-start | bytes 104456 | tf_op jit(solution)/shard_map/ppermute | solution.py:16
  171.6 5.9 %collective-permute-start.22 = (f32[68,34,1]{0,2,1:T(1,128)S(1)}, f32[68,34,1]{0,2,1:T(1,128)S(1)}, u32[]{:S(2)}, u32[]{:S(2)}) collective-permute-start(f32[68,34,1]{0,2,1:T(1,128)S(1)} %get-tuple-element.22), channel_id=1, source_target_pairs={{2,0},{4,2},{6,4},{3,1},{5,3},{7,5},{10,8},{12,10},{14,12},{11,9},... | collective-permute-start | bytes 27752 | tf_op jit(solution)/shard_map/ppermute | solution.py:17
  182.0 7.1 %collective-permute-start.24 = (f32[68,1,128]{0,2,1:T(8,128)S(1)}, f32[68,1,128]{0,2,1:T(8,128)S(1)}, u32[]{:S(2)}, u32[]{:S(2)}) collective-permute-start(f32[68,1,128]{0,2,1:T(8,128)S(1)} %get-tuple-element.33), channel_id=1, source_target_pairs={{8,0},{16,8},{24,16},{9,1},{17,9},{25,17},{10,2},{18,10},{26,18},{... | collective-permute-start | bytes 104456 | tf_op jit(solution)/shard_map/ppermute | solution.py:17
  183.9 6.4 %collective-permute-start.25 = (f32[68,1,128]{0,2,1:T(8,128)S(1)}, f32[68,1,128]{0,2,1:T(8,128)S(1)}, u32[]{:S(2)}, u32[]{:S(2)}) collective-permute-start(f32[68,1,128]{0,2,1:T(8,128)S(1)} %get-tuple-element.32), channel_id=1, source_target_pairs={{0,8},{8,16},{16,24},{1,9},{9,17},{17,25},{2,10},{10,18},{18,26},{... | collective-permute-start | bytes 104456 | tf_op jit(solution)/shard_map/ppermute | solution.py:16
  190.4 6.1 %collective-permute-start.26 = (f32[68,34,1]{0,2,1:T(1,128)S(1)}, f32[68,34,1]{0,2,1:T(1,128)S(1)}, u32[]{:S(2)}, u32[]{:S(2)}) collective-permute-start(f32[68,34,1]{0,2,1:T(1,128)S(1)} %get-tuple-element.20), channel_id=1, source_target_pairs={{2,0},{4,2},{6,4},{3,1},{5,3},{7,5},{10,8},{12,10},{14,12},{11,9},... | collective-permute-start | bytes 27752 | tf_op jit(solution)/shard_map/ppermute | solution.py:17
  248.8 6.8 %collective-permute-start.28 = (f32[68,2,128]{2,0,1:T(8,128)S(1)}, f32[68,2,128]{2,0,1:T(8,128)S(1)}, u32[]{:S(2)}, u32[]{:S(2)}) collective-permute-start(f32[68,2,128]{2,0,1:T(8,128)S(1)} %get-tuple-element.46), channel_id=1, source_target_pairs={{8,0},{16,8},{24,16},{9,1},{17,9},{25,17},{10,2},{18,10},{26,18},{... | collective-permute-start | bytes 208904 | tf_op jit(solution)/shard_map/ppermute | solution.py:17
  259.2 9.0 %collective-permute-start.30 = (f32[68,36,2]{0,2,1:T(2,128)S(1)}, f32[68,36,2]{0,2,1:T(2,128)S(1)}, u32[]{:S(2)}, u32[]{:S(2)}) collective-permute-start(f32[68,36,2]{0,2,1:T(2,128)S(1)} %copy.48), channel_id=1, source_target_pairs={{2,0},{4,2},{6,4},{3,1},{5,3},{7,5},{10,8},{12,10},{14,12},{11,9},... | collective-permute-start | bytes 58760 | tf_op jit(solution)/shard_map/ppermute | solution.py:17
  261.0 7.8 %collective-permute-start.31 = (f32[68,36,2]{0,2,1:T(2,128)S(1)}, f32[68,36,2]{0,2,1:T(2,128)S(1)}, u32[]{:S(2)}, u32[]{:S(2)}) collective-permute-start(f32[68,36,2]{0,2,1:T(2,128)S(1)} %copy.50), channel_id=1, source_target_pairs={{0,2},{2,4},{4,6},{1,3},{3,5},{5,7},{8,10},{10,12},{12,14},{9,11},... | collective-permute-start | bytes 58760 | tf_op jit(solution)/shard_map/ppermute | solution.py:16
  (16 other events, 186.0 us)
Sparse Core Ops, SparseCore 0:
  204.7 39.8 all-gather.1
where the time goes:
time: 284 us; the launch traced here: 283 us
  starting transfers between devices  100 us (35%)
  waiting for transfers between devices  59 us (21%)
  other arithmetic  38.6 us (14%)
  local copies, waits for them, and re-layouts  33.3 us (12%)
  blocking collectives  30.1 us (11%)
  between operations  15.3 us (5%)
  matrix products  6.14 us (2%)
    ppermute x16, starting transfers between devices, with_halo(): before = lax.ppermute(last, axis, up)  71.1 us
    all_gather x1, waiting for transfers between devices, on_device(): piece = lax.all_gather(solved, 'lev', axis=0, tiled=True)  40 us
    unnamed x1, blocking collectives  30.1 us
    ppermute x16, starting transfers between devices, with_halo(): after = lax.ppermute(initial, axis, down)  27 us
    div x6, other arithmetic, on_device(): solved = (modal + stiff * beside_all) / denom  23.1 us
    ppermute x16, waiting for transfers between devices, with_halo(): before = lax.ppermute(last, axis, up)  12.8 us
    unnamed x21, local copies, waits for them, and re-layouts  6.77 us
    concatenate x3, other arithmetic, with_halo(): value = jnp.concatenate([before, value, after], axis=dim)  6.47 us
  transfers between devices with their start and end apart: 34, of which 17 were waited for; matrix products, arithmetic and copies ran while one was open for 4% of the time, Pallas kernels for 0%

commit v1 on v0

v1 whole, which is shorter than its diff:
```python
import functools

import jax
import jax.numpy as jnp
from jax import lax
from jax.experimental import pallas as pl
from jax.experimental.pallas import tpu as pltpu
from jax.sharding import PartitionSpec as P

SWEEPS = 6
HALO = SWEEPS + 2
TERMS = SWEEPS + 1
LANES = 128
VMEM = pl.BlockSpec(memory_space=pltpu.VMEM)
SMEM = pl.BlockSpec(memory_space=pltpu.SMEM)
F32 = jnp.float32
BF16 = jnp.bfloat16


def up_to(n, k):
    return (n + k - 1) // k * k


def lanes_of():
    return lax.broadcasted_iota(jnp.int32, (1, LANES), 1)


def call(body, outs, *args, specs=None, scratch=(), vmem=48 << 20, name):
    return pl.pallas_call(
        body,
        out_shape=outs,
        in_specs=specs or [VMEM] * len(args),
        out_specs=jax.tree.map(lambda _: VMEM, outs),
        scratch_shapes=list(scratch),
        compiler_params=pltpu.CompilerParams(vmem_limit_bytes=vmem),
        name=name,
    )(*args)


def row_of(ref, x):
    levels, rows, lanes = ref.shape
    return ref.reshape(levels * rows, lanes)[pl.ds(x, levels, stride=rows), :]


def set_row(ref, x, value):
    levels, rows, lanes = ref.shape
    ref.reshape(levels * rows, lanes)[pl.ds(x, levels, stride=rows), :] = value


def north_step(main, side):
    lane = lanes_of()
    one = pltpu.roll(jnp.where(lane < 1, side, main), LANES - 1, 1) - pltpu.roll(
        jnp.where(lane >= LANES - 1, side, main), 1, 1
    )
    two = pltpu.roll(jnp.where(lane < 2, side, main), LANES - 2, 1) - pltpu.roll(
        jnp.where(lane >= LANES - 2, side, main), 2, 1
    )
    return 8.0 * one - two


def wind_edges(u_ref, v_ref, lo_ref, hi_ref, cols_ref):
    levels, rows, _ = u_ref.shape
    lane = lanes_of()
    for i in range(2):
        lo_ref[i, :levels] = row_of(u_ref, i)
        hi_ref[i, :levels] = row_of(u_ref, rows - 2 + i)

    def body(x, packed):
        rolled = pltpu.roll(row_of(v_ref, x), 4 * x + 2, 1)
        return jnp.where(lane // 4 == x, rolled, packed)

    cols_ref[:levels] = lax.fori_loop(0, rows, body, jnp.zeros((levels, LANES), F32), unroll=4)


def source_rows(u_ref, v_ref, h_ref, ulo_ref, uhi_ref, vl_ref, vr_ref, edge_ref, mid_ref, lo_ref, hi_ref):
    levels, rows, _ = u_ref.shape
    lane = lanes_of()
    vside = jnp.where(lane % 4 < 2, vl_ref[:levels], vr_ref[:levels])
    pad = edge_ref.shape[1] - levels

    def at(x):
        if x < 0:
            return ulo_ref[2 + x, :levels]
        if x >= rows:
            return uhi_ref[x - rows, :levels]
        return row_of(u_ref, x)

    packs = {}
    for x in range(rows):
        v = row_of(v_ref, x)
        side = pltpu.roll(vside, (LANES - 4 * x - 2) % LANES, 1)
        dx = 8.0 * (at(x + 1) - at(x - 1)) - (at(x + 2) - at(x - 2))
        dy = north_step(v, side)
        s = row_of(h_ref, x) - (dx + dy) * (1.0 / 12.0)
        m, k = divmod(x, 8)
        if x < HALO:
            targets = [(edge_ref, x), (lo_ref, x)]
        elif x >= rows - HALO:
            targets = [(edge_ref, x - rows + 2 * HALO), (hi_ref, x - rows + HALO)]
        else:
            targets = [(mid_ref, x - HALO)]
            rolled = pltpu.roll(s, 16 * k + 8, 1)
            packs[m] = jnp.where(lane // 16 == k, rolled, packs[m]) if m in packs else rolled
            if k == 7:
                targets_pack = 2 * HALO + m - 1
                edge_ref[targets_pack, :levels] = packs[m]
                if pad:
                    edge_ref[targets_pack, levels:] = jnp.zeros((pad, LANES), F32)
        for ref, i in targets:
            ref[i, :levels] = s
            if pad:
                ref[i, levels:] = jnp.zeros((pad, LANES), F32)


def column_messages(edge_ref, below_ref, above_ref, right_ref, left_ref):
    lane = lanes_of()
    slot = lane % 16

    def pack(ref, base):
        packed = pltpu.roll(ref[base], 8, 1)
        for k in range(1, 8):
            packed = jnp.where(lane // 16 == k, pltpu.roll(ref[base + k], 16 * k + 8, 1), packed)
        return packed

    mids = edge_ref.shape[0] - 2 * HALO
    packs = [pack(below_ref, 0), pack(edge_ref, 0)]
    packs += [edge_ref[2 * HALO + i] for i in range(mids)]
    packs += [pack(edge_ref, HALO), pack(above_ref, 0)]
    for i in range(len(packs) // 2):
        even, odd = packs[2 * i], packs[2 * i + 1]
        right_ref[i] = jnp.where(slot < 8, even, pltpu.roll(odd, 8, 1))
        left_ref[i] = jnp.where(slot < 8, pltpu.roll(even, LANES - 8, 1), odd)


def weights(levels_ref, modes_ref, coef_ref, out_ref):
    levels = levels_ref.shape[0]
    lp = out_ref.shape[0] // TERMS
    kp = out_ref.shape[1] // 3
    groups = modes_ref.shape[1]
    coef = coef_ref[...]
    denom = 1.0 + 4.0 * coef
    scaled = levels_ref[...] / denom
    ratio = coef / denom
    out_ref[...] = jnp.zeros(out_ref.shape, BF16)
    for j in range(TERMS):
        m = jnp.dot(scaled, modes_ref[...], precision=lax.Precision.HIGHEST, preferred_element_type=F32)
        high = m.astype(BF16)
        low = (m - high.astype(F32)).astype(BF16)
        rows = pl.ds(j * lp, lp)
        out_ref[rows, :kp] = high
        out_ref[rows, kp : 2 * kp] = high
        out_ref[rows, 2 * kp :] = low
        scaled = scaled * ratio


def finish(place_ref, *refs, groups, limits):
    ins, refs = refs[: 7 * groups], refs[7 * groups :]
    u_ref, v_ref, east_ref, north_ref, height_ref, s_ref, t_ref, ga_ref, gb_ref = refs
    levels, rows, _ = u_ref.shape
    span = rows + 2 * HALO
    lp = ga_ref.shape[1]
    kp = s_ref.shape[2] // 3
    lane = lanes_of()
    slot = lane % 16
    sided = (lane < HALO) | (lane >= LANES - HALO)

    for g in range(groups):
        edge, mid, below, above, from_left, from_right, w = ins[7 * g : 7 * g + 7]
        for m in range(span // 8):
            zl, zr = from_left[m // 2], from_right[m // 2]
            if m % 2 == 0:
                side = jnp.where(slot < 8, zl, pltpu.roll(zr, 8, 1))
            else:
                side = jnp.where(slot < 8, pltpu.roll(zl, LANES - 8, 1), zr)
            if m == 0:
                ref, base = below, 0
            elif m == 1:
                ref, base = edge, 0
            elif m == span // 8 - 2:
                ref, base = edge, HALO
            elif m == span // 8 - 1:
                ref, base = above, 0
            else:
                ref, base = mid, 8 * (m - 2)

            for k in range(8):
                beside = jnp.where(sided, pltpu.roll(side, LANES - 16 * k - 8, 1), 0.0)
                both = jnp.concatenate([ref[base + k], beside], axis=1)
                if kp > lp:
                    both = jnp.concatenate([both, jnp.zeros((kp - lp, 2 * LANES), F32)], axis=0)
                high = both.astype(BF16)
                low = (both - high.astype(F32)).astype(BF16)
                s_ref[g, 8 * m + k, :kp] = high
                s_ref[g, 8 * m + k, kp : 2 * kp] = low
                s_ref[g, 8 * m + k, 2 * kp :] = high

    def mix(x, _):
        total = None
        for g in range(groups):
            part = jnp.dot(ins[7 * g + 6][...], s_ref[g, x], preferred_element_type=F32)
            total = part if total is None else total + part
        for j in range(TERMS):
            t_ref[j, x] = total[j * lp : (j + 1) * lp]
        return _

    lax.fori_loop(0, span, mix, 0)

    first_row = place_ref[0] * rows - HALO
    open_left = (place_ref[1] > 0) & (lane >= LANES - HALO)
    open_right = (place_ref[1] < limits[1] - 1) & (lane < HALO)
    side_mask = jnp.where(open_left | open_right, 1.0, 0.0)
    now = t_ref.at[SWEEPS]
    for step in range(SWEEPS):
        j = SWEEPS - 1 - step
        nxt = (ga_ref, gb_ref)[step % 2]

        def sweep(x, _, now=now, nxt=nxt, j=j):
            row = first_row + x
            inside = jnp.where((row >= 0) & (row < limits[0] * rows), 1.0, 0.0)
            main, side = now[x, :, :LANES], now[x, :, LANES:]
            left = pltpu.roll(jnp.where(lane == LANES - 1, side, main), 1, 1)
            right = pltpu.roll(jnp.where(lane == 0, side, main), LANES - 1, 1)
            beside = now[x - 1, :, :LANES] + now[x + 1, :, :LANES]
            nxt[x, :, :LANES] = ((beside + (left + right)) + t_ref[j, x, :, :LANES]) * inside
            left = pltpu.roll(jnp.where(lane == LANES - 1, main, side), 1, 1)
            right = pltpu.roll(jnp.where(lane == 0, main, side), LANES - 1, 1)
            beside = now[x - 1, :, LANES:] + now[x + 1, :, LANES:]
            nxt[x, :, LANES:] = ((beside + (left + right)) + t_ref[j, x, :, LANES:]) * (inside * side_mask)
            return _

        reach = j + 2
        lax.fori_loop(HALO - reach, HALO + rows + reach, sweep, 0, unroll=2)
        now = nxt

    def output(x, _):
        main, side = now[x + HALO, :levels, :LANES], now[x + HALO, :levels, LANES:]
        dy = north_step(main, side)

        def at(i):
            return now[x + HALO + i, :levels, :LANES]

        dx = 8.0 * (at(1) - at(-1)) - (at(2) - at(-2))
        set_row(east_ref, x, row_of(u_ref, x) - dx * (1.0 / 12.0))
        set_row(north_ref, x, row_of(v_ref, x) - dy * (1.0 / 12.0))
        set_row(height_ref, x, main)
        return _

    lax.fori_loop(0, rows, output, 0, unroll=2)


def shape(*dims, dtype=F32):
    return jax.ShapeDtypeStruct(dims, dtype)


def neighbours(axis):
    peers = lax.axis_size(axis)
    up = [(i, i + 1) for i in range(peers - 1)]
    return up, [(j, i) for i, j in up]


def on_device(east_wind, north_wind, height, to_modes, to_levels, mode_coef):
    levels, rows, cols = east_wind.shape
    groups = lax.axis_size("lev")
    limits = (lax.axis_size("gx"), lax.axis_size("gy"))
    lp, kp = up_to(levels, 8), up_to(levels, 16)
    span = rows + 2 * HALO
    x_up, x_down = neighbours("gx")
    y_up, y_down = neighbours("gy")

    lo, hi, packed = call(
        wind_edges,
        (shape(2, lp, LANES), shape(2, lp, LANES), shape(lp, LANES)),
        east_wind,
        north_wind,
        name="wind_edges",
    )
    u_below = lax.ppermute(hi, "gx", x_up)
    u_above = lax.ppermute(lo, "gx", x_down)
    v_left = lax.ppermute(packed, "gy", y_up)
    v_right = lax.ppermute(packed, "gy", y_down)

    mids = (rows - 2 * HALO) // 8
    edge, mid, low, high = call(
        source_rows,
        (
            shape(2 * HALO + mids, lp, LANES),
            shape(rows - 2 * HALO, lp, LANES),
            shape(HALO, lp, LANES),
            shape(HALO, lp, LANES),
        ),
        east_wind,
        north_wind,
        height,
        u_below,
        u_above,
        v_left,
        v_right,
        name="source_rows",
    )

    me = lax.axis_index("lev")
    my_levels = lax.dynamic_slice_in_dim(to_levels, me * levels, levels, 0)
    my_levels = jnp.pad(my_levels, ((0, lp - levels), (0, 0)))
    operands = []
    for d in range(groups):
        other = (me + d) % groups
        modes = lax.dynamic_slice_in_dim(to_modes, other * levels, levels, 1)
        modes = jnp.pad(modes, ((0, 0), (0, kp - levels)))
        w = call(
            weights,
            shape(TERMS * lp, 3 * kp, dtype=BF16),
            my_levels,
            modes,
            mode_coef.reshape(1, -1),
            name="weights",
        )
        if d == 0:
            e, c, l, h = edge, mid, low, high
        else:
            pairs = [((i + d) % groups, i) for i in range(groups)]
            e = lax.ppermute(edge, "lev", pairs)
            c = lax.ppermute(mid, "lev", pairs)
            l, h = e[:HALO], e[HALO : 2 * HALO]
        below = lax.ppermute(h, "gx", x_up)
        above = lax.ppermute(l, "gx", x_down)
        right, left = call(
            column_messages,
            (shape(span // 16, lp, LANES), shape(span // 16, lp, LANES)),
            e,
            below,
            above,
            name="column_messages",
        )
        from_left = lax.ppermute(right, "gy", y_up)
        from_right = lax.ppermute(left, "gy", y_down)
        operands += [e, c, below, above, from_left, from_right, w]

    place = jnp.stack([lax.axis_index("gx"), lax.axis_index("gy")]).astype(jnp.int32)
    out = shape(levels, rows, cols)
    return call(
        functools.partial(finish, groups=groups, limits=limits),
        (out, out, out),
        place,
        *operands,
        east_wind,
        north_wind,
        specs=[SMEM] + [VMEM] * (len(operands) + 2),
        scratch=(
            pltpu.VMEM((groups, span, 3 * kp, 2 * LANES), BF16),
            pltpu.VMEM((TERMS, span, lp, 2 * LANES), F32),
            pltpu.VMEM((span, lp, 2 * LANES), F32),
            pltpu.VMEM((span, lp, 2 * LANES), F32),
        ),
        vmem=60 << 20,
        name="finish",
    )


def solution(mesh):
    return jax.shard_map(
        on_device,
        mesh=mesh,
        in_specs=(P("lev", "gx", "gy"), P("lev", "gx", "gy"), P("lev", "gx", "gy"), P(), P(), P()),
        out_specs=(P("lev", "gx", "gy"), P("lev", "gx", "gy"), P("lev", "gx", "gy")),
        check_vma=False,
    )
```

time: 284 us -> 115 us (0.40)
  starting transfers between devices: 100 us -> 38.3 us
  Pallas kernels: 0 us -> 55 us
  waiting for transfers between devices: 59 us -> 13.1 us
  other arithmetic: 38.6 us -> 0.62 us
  blocking collectives: 30.1 us -> 0 us
  local copies, waits for them, and re-layouts: 33.3 us -> 5.99 us
  between operations: 15.3 us -> 1.07 us
  matrix products: 6.14 us -> 0 us
    ppermute x32 -> x14, starting transfers between devices: 98.1 us -> 38.3 us  [the longest x2 10.7 us: on_device(): below = lax.ppermute(h, 'gx', x_up)]
    pallas_call x0 -> x7, Pallas kernels: none -> 55 us  [call(): pl.pallas_call(body, out_shape=outs, in_specs=specs or [VMEM] * len(args)...]
    all_gather x1 -> x0, waiting for transfers between devices: 40 us -> none  [on_device(): piece = lax.all_gather(solved, 'lev', axis=0, tiled=True)]
    unnamed x1 -> x0, blocking collectives: 30.1 us -> none
    div x7 -> x0, other arithmetic: 23.4 us -> none  [the longest x6 23.1 us: on_device(): solved = (modal + stiff * beside_all) / denom]
    slice x13 -> x1, local copies, waits for them, and re-layouts: 12.3 us -> 0.95 us  [on_device(): l, h = (e[:HALO], e[HALO:2 * HALO])]
    sub x3 -> x0, other arithmetic: 8.47 us -> none  [the longest x1 4.27 us: on_device(): north_wind - north_diff(edged_height)]
    ppermute x4 -> x0, local copies, waits for them, and re-layouts: 7.06 us -> none  [the longest x2 4.08 us: with_halo(): before = lax.ppermute(last, axis, up)]
  transfers between devices with their start and end apart: 34 -> 14, of which waited for: 17 -> 3; matrix products, arithmetic and copies ran while one was open for 4% -> 2% of each run, Pallas kernels for 0% -> 2%
where the time goes in v1:
time: 115 us; the launch traced here: 114 us
  Pallas kernels  55 us (48%)
  starting transfers between devices  38.3 us (33%)
  waiting for transfers between devices  13.1 us (11%)
  local copies, waits for them, and re-layouts  5.99 us (5%)
    pallas_call x7, Pallas kernels, call(): pl.pallas_call(body, out_shape=outs, in_specs=specs or [VMEM] * len(args)...  55 us
    ppermute x2, starting transfers between devices, on_device(): below = lax.ppermute(h, 'gx', x_up)  10.7 us
    ppermute x1, waiting for transfers between devices, on_device(): e = lax.ppermute(edge, 'lev', pairs)  8.49 us
    ppermute x2, starting transfers between devices, on_device(): from_left = lax.ppermute(right, 'gy', y_up)  7.94 us
    ppermute x1, starting transfers between devices, on_device(): u_below = lax.ppermute(hi, 'gx', x_up)  4.54 us
    ppermute x1, starting transfers between devices, on_device(): v_left = lax.ppermute(packed, 'gy', y_up)  3.99 us
    unnamed x36, local copies, waits for them, and re-layouts  3.92 us
    ppermute x2, starting transfers between devices, on_device(): above = lax.ppermute(l, 'gx', x_down)  3.83 us
  transfers between devices with their start and end apart: 14, of which 3 were waited for; matrix products, arithmetic and copies ran while one was open for 2% of the time, Pallas kernels for 2%

profile of v1, /device:TPU:1, one launch (start us, length us, event | category | flops | bytes accessed | tf_op | source)
XLA Modules:
  0.0 114.0 jit_solution(14849126465507648931)
XLA Ops:
  0.7 1.3 %copy-done.1 = f32[68,32,128]{2,1,0:T(8,128)S(1)} copy-done((f32[68,32,128]{2,1,0:T(8,128)S(1)}, f32[68,32,128]{2,1,0:T(8,128)}, u32[]{:S(2)}) %copy-start.1) | copy-done | bytes 1114136
  1.9 1.2 %copy-done.2 = f32[68,32,128]{2,1,0:T(8,128)S(1)} copy-done((f32[68,32,128]{2,1,0:T(8,128)S(1)}, f32[68,32,128]{2,1,0:T(8,128)}, u32[]{:S(2)}) %copy-start.2) | copy-done | bytes 1114136
  3.2 1.4 %wind_edges.1 = (f32[2,72,128]{2,1,0:T(8,128)S(1)}, f32[2,72,128]{2,1,0:T(8,128)S(1)}, f32[72,128]{1,0:T(8,128)S(1)}) custom-call(f32[68,32,128]{2,1,0:T(8,128)S(1)} %copy-done.1, f32[68,32,128]{2,1,0:T(8,128)S(1)} %copy-done.2), custom_call_target="tpu_custom_call" | custom-call | tf_op jit(solution)/shard_map/wind_edges/pallas_call | solution.py:29
  4.6 4.5 %collective-permute-start = (f32[2,72,128]{2,1,0:T(8,128)S(1)}, f32[2,72,128]{2,1,0:T(8,128)S(1)}, u32[]{:S(2)}, u32[]{:S(2)}) collective-permute-start(f32[2,72,128]{2,1,0:T(8,128)S(1)} %get-tuple-element.14), channel_id=1, source_target_pairs={{0,8},{8,16},{16,24},{1,9},{9,17},{17,25},{2,10},{10,18},{18,26},{... | collective-permute-start | bytes 221192 | tf_op jit(solution)/shard_map/ppermute | solution.py:277
  9.2 1.9 %collective-permute-start.1 = (f32[2,72,128]{2,1,0:T(8,128)S(1)}, f32[2,72,128]{2,1,0:T(8,128)S(1)}, u32[]{:S(2)}, u32[]{:S(2)}) collective-permute-start(f32[2,72,128]{2,1,0:T(8,128)S(1)} %get-tuple-element.15), channel_id=1, source_target_pairs={{8,0},{16,8},{24,16},{9,1},{17,9},{25,17},{10,2},{18,10},{26,18},{... | collective-permute-start | bytes 221192 | tf_op jit(solution)/shard_map/ppermute | solution.py:278
  11.1 1.3 %collective-permute-start.3 = (f32[72,128]{1,0:T(8,128)S(1)}, f32[72,128]{1,0:T(8,128)S(1)}, u32[]{:S(2)}, u32[]{:S(2)}) collective-permute-start(f32[72,128]{1,0:T(8,128)S(1)} %get-tuple-element.16), channel_id=1, source_target_pairs={{2,0},{4,2},{6,4},{3,1},{5,3},{7,5},{10,8},{12,10},{14,12},{11,9},... | collective-permute-start | bytes 110600 | tf_op jit(solution)/shard_map/ppermute | solution.py:280
  12.4 4.0 %collective-permute-start.2 = (f32[72,128]{1,0:T(8,128)S(1)}, f32[72,128]{1,0:T(8,128)S(1)}, u32[]{:S(2)}, u32[]{:S(2)}) collective-permute-start(f32[72,128]{1,0:T(8,128)S(1)} %get-tuple-element.16), channel_id=1, source_target_pairs={{0,2},{2,4},{4,6},{1,3},{3,5},{5,7},{8,10},{10,12},{12,14},{9,11},... | collective-permute-start | bytes 110600 | tf_op jit(solution)/shard_map/ppermute | solution.py:279
  16.4 1.0 collective-permute-done.2.vl_ref
  17.4 6.1 %source_rows.1 = (f32[18,72,128]{2,1,0:T(8,128)S(1)}, f32[16,72,128]{2,1,0:T(8,128)S(1)}, f32[8,72,128]{2,1,0:T(8,128)S(1)}, f32[8,72,128]{2,1,0:T(8,128)}) custom-call(f32[68,32,128]{2,1,0:T(8,128)S(1)} %copy-done.1, f32[68,32,128]{2,1,0:T(8,128)S(1)} %copy-done.2, f32[68,32,128]{2,1,0:T(8,128)S(1)} %copy-done.9, ...), custom_call_target="tpu_custom_call" | custom-call | tf_op jit(solution)/shard_map/source_rows/pallas_call | solution.py:29
  23.6 1.2 %collective-permute-start.8 = (f32[18,72,128]{2,1,0:T(8,128)S(1)}, f32[18,72,128]{2,1,0:T(8,128)S(1)}, u32[]{:S(2)}, u32[]{:S(2)}) collective-permute-start(f32[18,72,128]{2,1,0:T(8,128)S(1)} %get-tuple-element.17.edge_ref.refs_0_), channel_id=1, source_target_pairs={{1,0},{0,1},{3,2},{2,3},{5,4},{4,5},{7,6},{6,7},{9,8},{8,9},{11,10... | collective-permute-start | bytes 1990664 | tf_op jit(solution)/shard_map/ppermute | solution.py:321
  24.8 5.0 %collective-permute-start.4 = (f32[8,72,128]{2,1,0:T(8,128)}, f32[8,72,128]{2,1,0:T(8,128)S(1)}, u32[]{:S(2)}, u32[]{:S(2)}) collective-permute-start(f32[8,72,128]{2,1,0:T(8,128)} %get-tuple-element.19), channel_id=1, source_target_pairs={{0,8},{8,16},{16,24},{1,9},{9,17},{17,25},{2,10},{10,18},{18,26},{... | collective-permute-start | bytes 884744 | tf_op jit(solution)/shard_map/ppermute | solution.py:324
  29.8 1.9 %collective-permute-start.5 = (f32[8,72,128]{2,1,0:T(8,128)S(1)}, f32[8,72,128]{2,1,0:T(8,128)S(1)}, u32[]{:S(2)}, u32[]{:S(2)}) collective-permute-start(f32[8,72,128]{2,1,0:T(8,128)S(1)} %get-tuple-element.20), channel_id=1, source_target_pairs={{8,0},{16,8},{24,16},{9,1},{17,9},{25,17},{10,2},{18,10},{26,18},{... | collective-permute-start | bytes 884744 | tf_op jit(solution)/shard_map/ppermute | solution.py:325
  32.1 8.5 %collective-permute-done.8.edge_ref.refs_7_ = f32[18,72,128]{2,1,0:T(8,128)S(1)} collective-permute-done((f32[18,72,128]{2,1,0:T(8,128)S(1)}, f32[18,72,128]{2,1,0:T(8,128)S(1)}, u32[]{:S(2)}, u32[]{:S(2)}) %collective-permute-start.8) | collective-permute-done | bytes 663584 | tf_op jit(solution)/shard_map/ppermute | solution.py:321
  40.6 0.9 fusion
  41.5 1.9 %collective-permute-start.11 = (f32[8,72,128]{2,1,0:T(8,128)}, f32[8,72,128]{2,1,0:T(8,128)S(1)}, u32[]{:S(2)}, u32[]{:S(2)}) collective-permute-start(f32[8,72,128]{2,1,0:T(8,128)} %get-tuple-element.25), channel_id=1, source_target_pairs={{8,0},{16,8},{24,16},{9,1},{17,9},{25,17},{10,2},{18,10},{26,18},{... | collective-permute-start | bytes 884744 | tf_op jit(solution)/shard_map/ppermute | solution.py:325
  43.4 5.6 %collective-permute-start.10 = (f32[8,72,128]{2,1,0:T(8,128)}, f32[8,72,128]{2,1,0:T(8,128)S(1)}, u32[]{:S(2)}, u32[]{:S(2)}) collective-permute-start(f32[8,72,128]{2,1,0:T(8,128)} %get-tuple-element.26), channel_id=1, source_target_pairs={{0,8},{8,16},{16,24},{1,9},{9,17},{17,25},{2,10},{10,18},{18,26},{... | collective-permute-start | bytes 884744 | tf_op jit(solution)/shard_map/ppermute | solution.py:324
  49.1 1.1 constant_dynamic-slice_fusion
  51.0 0.7 copy-done.10
  52.8 3.9 %collective-permute-start.6 = (f32[3,72,128]{2,1,0:T(8,128)S(1)}, f32[3,72,128]{2,1,0:T(8,128)S(1)}, u32[]{:S(2)}, u32[]{:S(2)}) collective-permute-start(f32[3,72,128]{2,1,0:T(8,128)S(1)} %get-tuple-element.21), channel_id=1, source_target_pairs={{0,2},{2,4},{4,6},{1,3},{3,5},{5,7},{8,10},{10,12},{12,14},{9,11},... | collective-permute-start | bytes 331784 | tf_op jit(solution)/shard_map/ppermute | solution.py:334
  56.8 1.3 %collective-permute-start.7 = (f32[3,72,128]{2,1,0:T(8,128)S(1)}, f32[3,72,128]{2,1,0:T(8,128)S(1)}, u32[]{:S(2)}, u32[]{:S(2)}) collective-permute-start(f32[3,72,128]{2,1,0:T(8,128)S(1)} %get-tuple-element.22), channel_id=1, source_target_pairs={{2,0},{4,2},{6,4},{3,1},{5,3},{7,5},{10,8},{12,10},{14,12},{11,9},... | collective-permute-start | bytes 331784 | tf_op jit(solution)/shard_map/ppermute | solution.py:335
  58.6 4.0 %collective-permute-start.12 = (f32[3,72,128]{2,1,0:T(8,128)S(1)}, f32[3,72,128]{2,1,0:T(8,128)S(1)}, u32[]{:S(2)}, u32[]{:S(2)}) collective-permute-start(f32[3,72,128]{2,1,0:T(8,128)S(1)} %get-tuple-element.23), channel_id=1, source_target_pairs={{0,2},{2,4},{4,6},{1,3},{3,5},{5,7},{8,10},{10,12},{12,14},{9,11},... | collective-permute-start | bytes 331784 | tf_op jit(solution)/shard_map/ppermute | solution.py:334
  62.6 1.3 %collective-permute-start.13 = (f32[3,72,128]{2,1,0:T(8,128)S(1)}, f32[3,72,128]{2,1,0:T(8,128)S(1)}, u32[]{:S(2)}, u32[]{:S(2)}) collective-permute-start(f32[3,72,128]{2,1,0:T(8,128)S(1)} %get-tuple-element.24), channel_id=1, source_target_pairs={{2,0},{4,2},{6,4},{3,1},{5,3},{7,5},{10,8},{12,10},{14,12},{11,9},... | collective-permute-start | bytes 331784 | tf_op jit(solution)/shard_map/ppermute | solution.py:335
  64.6 3.5 %collective-permute-done.13.refs_12_ = f32[3,72,128]{2,1,0:T(8,128)S(1)} collective-permute-done((f32[3,72,128]{2,1,0:T(8,128)S(1)}, f32[3,72,128]{2,1,0:T(8,128)S(1)}, u32[]{:S(2)}, u32[]{:S(2)}) %collective-permute-start.13) | collective-permute-done | bytes 110624 | tf_op jit(solution)/shard_map/ppermute | solution.py:335
  68.8 45.2 %finish.1 = (f32[68,32,128]{2,1,0:T(8,128)}, f32[68,32,128]{2,1,0:T(8,128)}, f32[68,32,128]{2,1,0:T(8,128)}) custom-call(s32[2]{0:T(128)} %pad_add_fusion.place_ref, f32[18,72,128]{2,1,0:T(8,128)} %copy-done.4, f32[16,72,128]{2,1,0:T(8,128)} %copy-done.12, f32[8,72,128]{2,1,0:T(8,128)} %copy-done.5, f32[8,72,128]{2,1,0:T(8,128)} %copy-done.6, ...), custom_call_target="tpu_custom_call" | custom-call | tf_op jit(solution)/shard_map/finish/pallas_call | solution.py:29
  (54 shorter events, 3.9 us)
Async XLA Ops:
  0.6 48.4 %copy-start = (f32[136,136]{1,0:T(8,128)S(1)}, f32[136,136]{1,0:T(8,128)}, u32[]{:S(2)}) copy-start(f32[136,136]{1,0:T(8,128)} %param.10) | copy-start | bytes 221956
  3.2 14.3 %copy-start.9 = (f32[68,32,128]{2,1,0:T(8,128)S(1)}, f32[68,32,128]{2,1,0:T(8,128)}, u32[]{:S(2)}) copy-start(f32[68,32,128]{2,1,0:T(8,128)} %h_ref.1) | copy-start | bytes 3342340
  4.6 12.8 %collective-permute-start = (f32[2,72,128]{2,1,0:T(8,128)S(1)}, f32[2,72,128]{2,1,0:T(8,128)S(1)}, u32[]{:S(2)}, u32[]{:S(2)}) collective-permute-start(f32[2,72,128]{2,1,0:T(8,128)S(1)} %get-tuple-element.14), channel_id=1, source_target_pairs={{0,8},{8,16},{16,24},{1,9},{9,17},{17,25},{2,10},{10,18},{18,26},{... | collective-permute-start | bytes 221192 | tf_op jit(solution)/shard_map/ppermute | solution.py:277
  9.2 8.3 %collective-permute-start.1 = (f32[2,72,128]{2,1,0:T(8,128)S(1)}, f32[2,72,128]{2,1,0:T(8,128)S(1)}, u32[]{:S(2)}, u32[]{:S(2)}) collective-permute-start(f32[2,72,128]{2,1,0:T(8,128)S(1)} %get-tuple-element.15), channel_id=1, source_target_pairs={{8,0},{16,8},{24,16},{9,1},{17,9},{25,17},{10,2},{18,10},{26,18},{... | collective-permute-start | bytes 221192 | tf_op jit(solution)/shard_map/ppermute | solution.py:278
  11.1 5.3 %collective-permute-start.3 = (f32[72,128]{1,0:T(8,128)S(1)}, f32[72,128]{1,0:T(8,128)S(1)}, u32[]{:S(2)}, u32[]{:S(2)}) collective-permute-start(f32[72,128]{1,0:T(8,128)S(1)} %get-tuple-element.16), channel_id=1, source_target_pairs={{2,0},{4,2},{6,4},{3,1},{5,3},{7,5},{10,8},{12,10},{14,12},{11,9},... | collective-permute-start | bytes 110600 | tf_op jit(solution)/shard_map/ppermute | solution.py:280
  12.4 5.0 %collective-permute-start.2 = (f32[72,128]{1,0:T(8,128)S(1)}, f32[72,128]{1,0:T(8,128)S(1)}, u32[]{:S(2)}, u32[]{:S(2)}) collective-permute-start(f32[72,128]{1,0:T(8,128)S(1)} %get-tuple-element.16), channel_id=1, source_target_pairs={{0,2},{2,4},{4,6},{1,3},{3,5},{5,7},{8,10},{10,12},{12,14},{9,11},... | collective-permute-start | bytes 110600 | tf_op jit(solution)/shard_map/ppermute | solution.py:279
  23.5 27.4 %copy-start.12 = (f32[16,72,128]{2,1,0:T(8,128)}, f32[16,72,128]{2,1,0:T(8,128)S(1)}, u32[]{:S(2)}) copy-start(f32[16,72,128]{2,1,0:T(8,128)S(1)} %get-tuple-element.18.refs_1_) | copy-start | bytes 1769476
  23.5 28.8 %copy-start.4 = (f32[18,72,128]{2,1,0:T(8,128)}, f32[18,72,128]{2,1,0:T(8,128)S(1)}, u32[]{:S(2)}) copy-start(f32[18,72,128]{2,1,0:T(8,128)S(1)} %get-tuple-element.17.edge_ref.refs_0_) | copy-start | bytes 1990660
  23.6 26.7 %copy-start.13 = (f32[136]{0:T(256)S(1)}, f32[136]{0:T(256)}, u32[]{:S(2)}) copy-start(f32[136]{0:T(256)} %param.11) | copy-start | bytes 1636
  23.6 17.0 %collective-permute-start.8 = (f32[18,72,128]{2,1,0:T(8,128)S(1)}, f32[18,72,128]{2,1,0:T(8,128)S(1)}, u32[]{:S(2)}, u32[]{:S(2)}) collective-permute-start(f32[18,72,128]{2,1,0:T(8,128)S(1)} %get-tuple-element.17.edge_ref.refs_0_), channel_id=1, source_target_pairs={{1,0},{0,1},{3,2},{2,3},{5,4},{4,5},{7,6},{6,7},{9,8},{8,9},{11,10... | collective-permute-start | bytes 1990664 | tf_op jit(solution)/shard_map/ppermute | solution.py:321
  24.8 27.6 %collective-permute-start.4 = (f32[8,72,128]{2,1,0:T(8,128)}, f32[8,72,128]{2,1,0:T(8,128)S(1)}, u32[]{:S(2)}, u32[]{:S(2)}) collective-permute-start(f32[8,72,128]{2,1,0:T(8,128)} %get-tuple-element.19), channel_id=1, source_target_pairs={{0,8},{8,16},{16,24},{1,9},{9,17},{17,25},{2,10},{10,18},{18,26},{... | collective-permute-start | bytes 884744 | tf_op jit(solution)/shard_map/ppermute | solution.py:324
  29.8 22.5 %collective-permute-start.5 = (f32[8,72,128]{2,1,0:T(8,128)S(1)}, f32[8,72,128]{2,1,0:T(8,128)S(1)}, u32[]{:S(2)}, u32[]{:S(2)}) collective-permute-start(f32[8,72,128]{2,1,0:T(8,128)S(1)} %get-tuple-element.20), channel_id=1, source_target_pairs={{8,0},{16,8},{24,16},{9,1},{17,9},{25,17},{10,2},{18,10},{26,18},{... | collective-permute-start | bytes 884744 | tf_op jit(solution)/shard_map/ppermute | solution.py:325
  31.7 32.8 %collective-permute-start.9 = (f32[16,72,128]{2,1,0:T(8,128)S(1)}, f32[16,72,128]{2,1,0:T(8,128)}, u32[]{:S(2)}, u32[]{:S(2)}) collective-permute-start(f32[16,72,128]{2,1,0:T(8,128)S(1)} %get-tuple-element.18.refs_1_), channel_id=1, source_target_pairs={{1,0},{0,1},{3,2},{2,3},{5,4},{4,5},{7,6},{6,7},{9,8},{8,9},{11,10... | collective-permute-start | bytes 1769480 | tf_op jit(solution)/shard_map/ppermute | solution.py:322
  40.6 17.6 %copy-start.3 = (f32[18,72,128]{2,1,0:T(8,128)}, f32[18,72,128]{2,1,0:T(8,128)S(1)}, u32[]{:S(2)}) copy-start(f32[18,72,128]{2,1,0:T(8,128)S(1)} %collective-permute-done.8.edge_ref.refs_7_) | copy-start | bytes 1990660
  41.5 16.6 %collective-permute-start.11 = (f32[8,72,128]{2,1,0:T(8,128)}, f32[8,72,128]{2,1,0:T(8,128)S(1)}, u32[]{:S(2)}, u32[]{:S(2)}) collective-permute-start(f32[8,72,128]{2,1,0:T(8,128)} %get-tuple-element.25), channel_id=1, source_target_pairs={{8,0},{16,8},{24,16},{9,1},{17,9},{25,17},{10,2},{18,10},{26,18},{... | collective-permute-start | bytes 884744 | tf_op jit(solution)/shard_map/ppermute | solution.py:325
  43.4 14.7 %collective-permute-start.10 = (f32[8,72,128]{2,1,0:T(8,128)}, f32[8,72,128]{2,1,0:T(8,128)S(1)}, u32[]{:S(2)}, u32[]{:S(2)}) collective-permute-start(f32[8,72,128]{2,1,0:T(8,128)} %get-tuple-element.26), channel_id=1, source_target_pairs={{0,8},{8,16},{16,24},{1,9},{9,17},{17,25},{2,10},{10,18},{18,26},{... | collective-permute-start | bytes 884744 | tf_op jit(solution)/shard_map/ppermute | solution.py:324
  52.3 6.3 %copy-start.11 = (bf16[504,240]{1,0:T(8,128)(2,1)}, bf16[504,240]{1,0:T(8,128)(2,1)S(1)}, u32[]{:S(2)}) copy-start(bf16[504,240]{1,0:T(8,128)(2,1)S(1)} %weights.3.refs_13_) | copy-start | bytes 725764
  52.3 6.3 %copy-start.5 = (f32[8,72,128]{2,1,0:T(8,128)}, f32[8,72,128]{2,1,0:T(8,128)S(1)}, u32[]{:S(2)}) copy-start(f32[8,72,128]{2,1,0:T(8,128)S(1)} %collective-permute-done.4.below_ref.refs_2_) | copy-start | bytes 884740
  52.8 11.7 %collective-permute-start.6 = (f32[3,72,128]{2,1,0:T(8,128)S(1)}, f32[3,72,128]{2,1,0:T(8,128)S(1)}, u32[]{:S(2)}, u32[]{:S(2)}) collective-permute-start(f32[3,72,128]{2,1,0:T(8,128)S(1)} %get-tuple-element.21), channel_id=1, source_target_pairs={{0,2},{2,4},{4,6},{1,3},{3,5},{5,7},{8,10},{10,12},{12,14},{9,11},... | collective-permute-start | bytes 331784 | tf_op jit(solution)/shard_map/ppermute | solution.py:334
  56.8 7.8 %collective-permute-start.7 = (f32[3,72,128]{2,1,0:T(8,128)S(1)}, f32[3,72,128]{2,1,0:T(8,128)S(1)}, u32[]{:S(2)}, u32[]{:S(2)}) collective-permute-start(f32[3,72,128]{2,1,0:T(8,128)S(1)} %get-tuple-element.22), channel_id=1, source_target_pairs={{2,0},{4,2},{6,4},{3,1},{5,3},{7,5},{10,8},{12,10},{14,12},{11,9},... | collective-permute-start | bytes 331784 | tf_op jit(solution)/shard_map/ppermute | solution.py:335
  58.1 10.0 %copy-start.7 = (f32[8,72,128]{2,1,0:T(8,128)}, f32[8,72,128]{2,1,0:T(8,128)S(1)}, u32[]{:S(2)}) copy-start(f32[8,72,128]{2,1,0:T(8,128)S(1)} %collective-permute-done.11.above_ref.refs_10_) | copy-start | bytes 884740
  58.1 10.0 %copy-start.8 = (f32[8,72,128]{2,1,0:T(8,128)}, f32[8,72,128]{2,1,0:T(8,128)S(1)}, u32[]{:S(2)}) copy-start(f32[8,72,128]{2,1,0:T(8,128)S(1)} %collective-permute-done.10.below_ref.refs_9_) | copy-start | bytes 884740
  58.6 6.0 %collective-permute-start.12 = (f32[3,72,128]{2,1,0:T(8,128)S(1)}, f32[3,72,128]{2,1,0:T(8,128)S(1)}, u32[]{:S(2)}, u32[]{:S(2)}) collective-permute-start(f32[3,72,128]{2,1,0:T(8,128)S(1)} %get-tuple-element.23), channel_id=1, source_target_pairs={{0,2},{2,4},{4,6},{1,3},{3,5},{5,7},{8,10},{10,12},{12,14},{9,11},... | collective-permute-start | bytes 331784 | tf_op jit(solution)/shard_map/ppermute | solution.py:334
  62.6 5.5 %collective-permute-start.13 = (f32[3,72,128]{2,1,0:T(8,128)S(1)}, f32[3,72,128]{2,1,0:T(8,128)S(1)}, u32[]{:S(2)}, u32[]{:S(2)}) collective-permute-start(f32[3,72,128]{2,1,0:T(8,128)S(1)} %get-tuple-element.24), channel_id=1, source_target_pairs={{2,0},{4,2},{6,4},{3,1},{5,3},{7,5},{10,8},{12,10},{14,12},{11,9},... | collective-permute-start | bytes 331784 | tf_op jit(solution)/shard_map/ppermute | solution.py:335
  (8 other events, 20.8 us)

commit v2 on v1

v2 whole, which is shorter than its diff:
```python
import functools

import jax
import jax.numpy as jnp
from jax import lax
from jax.experimental import pallas as pl
from jax.experimental.pallas import tpu as pltpu
from jax.sharding import PartitionSpec as P

SWEEPS = 6
HALO = SWEEPS + 2
TERMS = SWEEPS + 1
LANES = 128
VMEM = pl.BlockSpec(memory_space=pltpu.VMEM)
SMEM = pl.BlockSpec(memory_space=pltpu.SMEM)
ANY = pl.BlockSpec(memory_space=pl.ANY)
F32 = jnp.float32
BF16 = jnp.bfloat16


def up_to(n, k):
    return (n + k - 1) // k * k


def lanes_of():
    return lax.broadcasted_iota(jnp.int32, (1, LANES), 1)


def call(body, outs, *args, specs=None, out_specs=None, scratch=(), vmem=48 << 20, name):
    return pl.pallas_call(
        body,
        out_shape=outs,
        in_specs=specs or [VMEM] * len(args),
        out_specs=out_specs or jax.tree.map(lambda _: VMEM, outs),
        scratch_shapes=list(scratch),
        compiler_params=pltpu.CompilerParams(vmem_limit_bytes=vmem),
        name=name,
    )(*args)


def start_rows(src_ref, dst_ref, sems):
    copies = [pltpu.make_async_copy(src_ref.at[:, x, :], dst_ref.at[x], sems.at[x]) for x in range(dst_ref.shape[0])]
    for copy in copies:
        copy.start()
    return copies


def north_step(main, side):
    lane = lanes_of()
    one = pltpu.roll(jnp.where(lane < 1, side, main), LANES - 1, 1) - pltpu.roll(
        jnp.where(lane >= LANES - 1, side, main), 1, 1
    )
    two = pltpu.roll(jnp.where(lane < 2, side, main), LANES - 2, 1) - pltpu.roll(
        jnp.where(lane >= LANES - 2, side, main), 2, 1
    )
    return 8.0 * one - two


def wind_edges(u_ref, v_ref, lo_ref, hi_ref, cols_ref, v_rows, v_sems, u_sems):
    rows = u_ref.shape[1]
    lane = lanes_of()
    loads = start_rows(v_ref, v_rows, v_sems)
    edges = []
    for i in range(2):
        edges.append(pltpu.make_async_copy(u_ref.at[:, i, :], lo_ref.at[i], u_sems.at[i]))
        edges.append(pltpu.make_async_copy(u_ref.at[:, rows - 2 + i, :], hi_ref.at[i], u_sems.at[2 + i]))
    for copy in edges:
        copy.start()
    packed = None
    for x in range(rows):
        loads[x].wait()
        rolled = pltpu.roll(v_rows[x], (4 * x + 2) % LANES, 1)
        packed = rolled if packed is None else jnp.where(lane // 4 == x, rolled, packed)
    cols_ref[...] = packed
    for copy in edges:
        copy.wait()


def source_rows(
    u_ref, v_ref, h_ref, ulo_ref, uhi_ref, vl_ref, vr_ref, edge_ref, mid_ref, lo_ref, hi_ref, u_rows, v_rows, h_rows, sems
):
    rows, levels, _ = u_rows.shape
    lane = lanes_of()
    u_loads = start_rows(u_ref, u_rows, sems.at[0])
    v_loads = start_rows(v_ref, v_rows, sems.at[1])
    h_loads = start_rows(h_ref, h_rows, sems.at[2])
    vside = jnp.where(lane % 4 < 2, vl_ref[...], vr_ref[...])
    pad = edge_ref.shape[1] - levels

    def at(x):
        if x < 0:
            return ulo_ref[2 + x]
        if x >= rows:
            return uhi_ref[x - rows]
        return u_rows[x]

    def put(ref, i, value):
        ref[i, :levels] = value
        if pad:
            ref[i, levels:] = jnp.zeros((pad, LANES), F32)

    packed = None
    for x in range(rows):
        for i in range(0 if x == 0 else x + 2, min(x + 3, rows)):
            u_loads[i].wait()
        v_loads[x].wait()
        h_loads[x].wait()
        side = pltpu.roll(vside, (LANES - 4 * x - 2) % LANES, 1)
        dx = 8.0 * (at(x + 1) - at(x - 1)) - (at(x + 2) - at(x - 2))
        s = h_rows[x] - (dx + north_step(v_rows[x], side)) * (1.0 / 12.0)
        m, k = divmod(x, 8)
        if x < HALO:
            put(edge_ref, x, s)
            put(lo_ref, x, s)
        elif x >= rows - HALO:
            put(edge_ref, x - rows + 2 * HALO, s)
            put(hi_ref, x - rows + HALO, s)
        else:
            put(mid_ref, x - HALO, s)
            rolled = pltpu.roll(s, (16 * k + 8) % LANES, 1)
            packed = rolled if k == 0 else jnp.where(lane // 16 == k, rolled, packed)
            if k == 7:
                put(edge_ref, 2 * HALO + m - 1, packed)


def column_messages(edge_ref, below_ref, above_ref, right_ref, left_ref):
    lane = lanes_of()
    slot = lane % 16

    def pack(ref, base):
        packed = pltpu.roll(ref[base], 8, 1)
        for k in range(1, 8):
            packed = jnp.where(lane // 16 == k, pltpu.roll(ref[base + k], (16 * k + 8) % LANES, 1), packed)
        return packed

    mids = edge_ref.shape[0] - 2 * HALO
    packs = [pack(below_ref, 0), pack(edge_ref, 0)]
    packs += [edge_ref[2 * HALO + i] for i in range(mids)]
    packs += [pack(edge_ref, HALO), pack(above_ref, 0)]
    for i in range(len(packs) // 2):
        even, odd = packs[2 * i], packs[2 * i + 1]
        right_ref[i] = jnp.where(slot < 8, even, pltpu.roll(odd, 8, 1))
        left_ref[i] = jnp.where(slot < 8, pltpu.roll(even, LANES - 8, 1), odd)


def weights(levels_ref, modes_ref, coef_ref, out_ref):
    kp = out_ref.shape[0] // 3
    coef = coef_ref[...]
    denom = 1.0 + 4.0 * coef
    scaled = levels_ref[...] / denom
    ratio = coef / denom
    for j in range(TERMS):
        m = jnp.dot(scaled, modes_ref[...], precision=lax.Precision.HIGHEST, preferred_element_type=F32).T
        high = m.astype(BF16)
        low = (m - high.astype(F32)).astype(BF16)
        at = pl.ds(j * LANES, LANES)
        out_ref[:kp, at] = high
        out_ref[kp : 2 * kp, at] = high
        out_ref[2 * kp :, at] = low
        scaled = scaled * ratio


def level_part(place_ref, *refs, first, last, limits):
    (edge, mid, below, above, from_left, from_right, w), refs = refs[:7], refs[7:]
    if not first:
        before, refs = refs[0], refs[1:]
    if last:
        u_ref, v_ref, east_ref, north_ref, height_ref, t_ref, ga_ref, gb_ref, side_ref = refs[:9]
        u_rows, v_rows, h_rows, sems = refs[9:]
        loads = start_rows(u_ref, u_rows, sems.at[0]) + start_rows(v_ref, v_rows, sems.at[1])
    else:
        out_ref, t_ref, ga_ref, gb_ref, side_ref = refs
    span, wide, _ = ga_ref.shape
    rows = span - 2 * HALO
    lp = edge.shape[1]
    kp = w.shape[0] // 3
    slot = lanes_of() % 16

    for g_ref in (ga_ref, gb_ref):
        g_ref[:, :8] = jnp.zeros((span, 8, LANES), F32)
        g_ref[:, wide - 8 :] = jnp.zeros((span, 8, LANES), F32)

    def mixed(value):
        if kp > lp:
            value = jnp.concatenate([value, jnp.zeros((kp - lp, LANES), F32)], axis=0)
        high = value.astype(BF16)
        low = (value - high.astype(F32)).astype(BF16)
        both = jnp.concatenate([high, low, high], axis=0)
        return lax.dot_general(both, w[...], (((0,), (0,)), ((), ())), preferred_element_type=F32)

    def put(x, col, part):
        n = part.shape[0]
        for j in range(SWEEPS):
            t_ref[j, x, pl.ds(col, n)] = part[:, j * LANES : (j + 1) * LANES]
        ga_ref[x, pl.ds(col + 8, n)] = part[:, SWEEPS * LANES :]

    def rows_from(ref, at, count, x0):
        def body(i, _):
            put(x0 + i, HALO, mixed(ref[at + i]))
            return _

        lax.fori_loop(0, count, body, 0, unroll=2)

    rows_from(edge, 0, HALO, HALO)
    rows_from(mid, 0, rows - 2 * HALO, 2 * HALO)
    rows_from(edge, HALO, HALO, rows)
    rows_from(below, 0, HALO, 0)
    rows_from(above, 0, HALO, rows + HALO)
    for m in range(span // 8):
        zl, zr = from_left[m // 2], from_right[m // 2]
        if m % 2 == 0:
            side_ref[m] = jnp.where(slot < 8, zl, pltpu.roll(zr, 8, 1))
        else:
            side_ref[m] = jnp.where(slot < 8, pltpu.roll(zl, LANES - 8, 1), zr)

    def beside(m, _):
        part = mixed(side_ref[m])
        for k in range(8):
            put(8 * m + k, 0, part[16 * k : 16 * k + 8])
            put(8 * m + k, HALO + LANES, part[16 * k + 8 : 16 * k + 16])
        return _

    lax.fori_loop(0, span // 8, beside, 0)

    first_row = place_ref[0] * rows - HALO
    left = jnp.where(place_ref[1] > 0, 1.0, 0.0)
    right = jnp.where(place_ref[1] < limits[1] - 1, 1.0, 0.0)
    for step in range(SWEEPS):
        j = SWEEPS - 1 - step
        now, nxt = ((ga_ref, gb_ref), (gb_ref, ga_ref))[step % 2]
        reach = j + 2
        final = j == 0

        def sweep(x, _, now=now, nxt=nxt, j=j, final=final):
            row = first_row + x
            inside = jnp.where((row >= 0) & (row < limits[0] * rows), 1.0, 0.0)
            for y in range(8, wide - 8, 8):
                here = pl.ds(y, 8)
                total = (now[x - 1, here] + now[x + 1, here]) + (now[x, pl.ds(y - 1, 8)] + now[x, pl.ds(y + 1, 8)])
                mask = inside
                if y == 8:
                    mask = inside * left
                elif y == wide - 16:
                    mask = inside * right
                total = (total + t_ref[j, x, pl.ds(y - 8, 8)]) * mask
                if final and not first:
                    total = total + before[x - HALO + 2, pl.ds(y - 8, 8)]
                if final and not last:
                    out_ref[x - HALO + 2, pl.ds(y - 8, 8)] = total
                else:
                    nxt[x, here] = total
            return _

        lax.fori_loop(HALO - reach, HALO + rows + reach, sweep, 0, unroll=2)

    if not last:
        return
    done = (gb_ref, ga_ref)[(SWEEPS - 1) % 2]
    levels = u_rows.shape[1]

    def turn(x, _):
        h_rows[x] = done[x + HALO - 2, pl.ds(16, LANES)].T[:levels]
        return _

    lax.fori_loop(0, rows + 4, turn, 0, unroll=2)
    for copy in loads:
        copy.wait()

    def stores(x):
        return [
            pltpu.make_async_copy(src, dst.at[:, x, :], sems.at[i, x])
            for i, (src, dst) in enumerate(
                ((u_rows.at[x], east_ref), (v_rows.at[x], north_ref), (h_rows.at[x + 2], height_ref))
            )
        ]

    def output(x, _):
        def north(i):
            return done[x + HALO, pl.ds(16 + i, LANES)]

        dy = (8.0 * (north(1) - north(-1)) - (north(2) - north(-2))).T[:levels]
        dx = 8.0 * (h_rows[x + 3] - h_rows[x + 1]) - (h_rows[x + 4] - h_rows[x])
        u_rows[x] = u_rows[x] - dx * (1.0 / 12.0)
        v_rows[x] = v_rows[x] - dy * (1.0 / 12.0)
        for copy in stores(x):
            copy.start()
        return _

    lax.fori_loop(0, rows, output, 0, unroll=2)
    for x in range(rows):
        for copy in stores(x):
            copy.wait()


def shape(*dims, dtype=F32):
    return jax.ShapeDtypeStruct(dims, dtype)


def neighbours(axis):
    peers = lax.axis_size(axis)
    up = [(i, i + 1) for i in range(peers - 1)]
    return up, [(j, i) for i, j in up]


def on_device(east_wind, north_wind, height, to_modes, to_levels, mode_coef):
    levels, rows, cols = east_wind.shape
    groups = lax.axis_size("lev")
    limits = (lax.axis_size("gx"), lax.axis_size("gy"))
    lp, kp = up_to(levels, 8), up_to(levels, 16)
    span = rows + 2 * HALO
    x_up, x_down = neighbours("gx")
    y_up, y_down = neighbours("gy")

    dma = pltpu.SemaphoreType.DMA
    row_block = pltpu.VMEM((rows, levels, cols), F32)
    lo, hi, packed = call(
        wind_edges,
        (shape(2, levels, LANES), shape(2, levels, LANES), shape(levels, LANES)),
        east_wind,
        north_wind,
        specs=[ANY] * 2,
        scratch=(row_block, dma((rows,)), dma((4,))),
        name="wind_edges",
    )
    u_below = lax.ppermute(hi, "gx", x_up)
    u_above = lax.ppermute(lo, "gx", x_down)
    v_left = lax.ppermute(packed, "gy", y_up)
    v_right = lax.ppermute(packed, "gy", y_down)

    mids = (rows - 2 * HALO) // 8
    edge, mid, low, high = call(
        source_rows,
        (
            shape(2 * HALO + mids, lp, LANES),
            shape(rows - 2 * HALO, lp, LANES),
            shape(HALO, lp, LANES),
            shape(HALO, lp, LANES),
        ),
        east_wind,
        north_wind,
        height,
        u_below,
        u_above,
        v_left,
        v_right,
        specs=[ANY] * 3 + [VMEM] * 4,
        scratch=(row_block, row_block, row_block, dma((3, rows))),
        name="source_rows",
    )

    me = lax.axis_index("lev")
    my_levels = lax.dynamic_slice_in_dim(to_levels, me * levels, levels, 0)
    my_levels = jnp.pad(my_levels, ((0, LANES - levels), (0, 0)))
    place = jnp.stack([lax.axis_index("gx"), lax.axis_index("gy")]).astype(jnp.int32)
    out = shape(levels, rows, cols)
    part = None
    for d in range(groups):
        other = (me + d) % groups
        modes = lax.dynamic_slice_in_dim(to_modes, other * levels, levels, 1)
        modes = jnp.pad(modes, ((0, 0), (0, kp - levels)))
        w = call(
            weights,
            shape(3 * kp, TERMS * LANES, dtype=BF16),
            my_levels,
            modes,
            mode_coef.reshape(1, -1),
            name="weights",
        )
        if d == 0:
            e, c, l, h = edge, mid, low, high
        else:
            pairs = [((i + d) % groups, i) for i in range(groups)]
            e = lax.ppermute(edge, "lev", pairs)
            c = lax.ppermute(mid, "lev", pairs)
            l, h = e[:HALO], e[HALO : 2 * HALO]
        below = lax.ppermute(h, "gx", x_up)
        above = lax.ppermute(l, "gx", x_down)
        right, left = call(
            column_messages,
            (shape(span // 16, lp, LANES), shape(span // 16, lp, LANES)),
            e,
            below,
            above,
            name="column_messages",
        )
        from_left = lax.ppermute(right, "gy", y_up)
        from_right = lax.ppermute(left, "gy", y_down)
        last = d == groups - 1
        args = [e, c, below, above, from_left, from_right, w] + ([] if part is None else [part])
        specs = [SMEM] + [VMEM] * len(args)
        scratch = [
            pltpu.VMEM((SWEEPS, span, cols + 16, LANES), F32),
            pltpu.VMEM((span, cols + 32, LANES), F32),
            pltpu.VMEM((span, cols + 32, LANES), F32),
            pltpu.VMEM((span // 8, lp, LANES), F32),
        ]
        if last:
            args += [east_wind, north_wind]
            specs += [ANY] * 2
            scratch += [row_block, row_block, pltpu.VMEM((rows + 4, levels, cols), F32), dma((3, rows))]
        part = call(
            functools.partial(level_part, first=d == 0, last=last, limits=limits),
            (out, out, out) if last else shape(rows + 4, cols + 16, LANES),
            place,
            *args,
            specs=specs,
            out_specs=(ANY, ANY, ANY) if last else VMEM,
            scratch=scratch,
            name="level_part",
        )
    return part


def solution(mesh):
    return jax.shard_map(
        on_device,
        mesh=mesh,
        in_specs=(P("lev", "gx", "gy"), P("lev", "gx", "gy"), P("lev", "gx", "gy"), P(), P(), P()),
        out_specs=(P("lev", "gx", "gy"), P("lev", "gx", "gy"), P("lev", "gx", "gy")),
        check_vma=False,
    )
```

time: 115 us -> 115 us (level)
  Pallas kernels: 55 us -> 59.3 us
  waiting for transfers between devices: 13.1 us -> 9.55 us
    pallas_call x7 -> x8, Pallas kernels: 55 us -> 59.3 us  [call(): pl.pallas_call(body, out_shape=outs, in_specs=specs or [VMEM] * len(args)...]
    ppermute x2, waiting for transfers between devices: 3.53 us -> 0.01 us  [on_device(): from_right = lax.ppermute(left, 'gy', y_down)]
    unnamed x36 -> x16, local copies, waits for them, and re-layouts: 3.92 us -> 4.07 us
  transfers between devices with their start and end apart: 14 -> 14, of which waited for: 3 -> 2; matrix products, arithmetic and copies ran while one was open for 2% -> 2% of each run, Pallas kernels for 2% -> 16%
where the time goes in v2:
time: 115 us
  Pallas kernels  59.3 us (52%)
  starting transfers between devices  38.5 us (33%)
  waiting for transfers between devices  9.55 us (8%)
  local copies, waits for them, and re-layouts  6.06 us (5%)
    pallas_call x8, Pallas kernels, call(): pl.pallas_call(body, out_shape=outs, in_specs=specs or [VMEM] * len(args)...  59.3 us
    ppermute x2, starting transfers between devices, on_device(): below = lax.ppermute(h, 'gx', x_up)  10.7 us
    ppermute x1, waiting for transfers between devices, on_device(): e = lax.ppermute(edge, 'lev', pairs)  8.49 us
    ppermute x2, starting transfers between devices, on_device(): from_left = lax.ppermute(right, 'gy', y_up)  7.95 us
    ppermute x1, starting transfers between devices, on_device(): u_below = lax.ppermute(hi, 'gx', x_up)  4.54 us
    unnamed x16, local copies, waits for them, and re-layouts  4.07 us
    ppermute x1, starting transfers between devices, on_device(): v_left = lax.ppermute(packed, 'gy', y_up)  3.99 us
    ppermute x2, starting transfers between devices, on_device(): above = lax.ppermute(l, 'gx', x_down)  3.83 us
  transfers between devices with their start and end apart: 14, of which 2 were waited for; matrix products, arithmetic and copies ran while one was open for 2% of the time, Pallas kernels for 16%

profile of v2, /device:TPU:1, one launch (start us, length us, event | category | flops | bytes accessed | tf_op | source)
XLA Modules:
  0.0 114.7 jit_solution(2938166311870167863)
XLA Ops:
  0.7 1.3 %copy-done.2 = f32[68,32,128]{2,1,0:T(8,128)S(1)} copy-done((f32[68,32,128]{2,1,0:T(8,128)S(1)}, f32[68,32,128]{2,1,0:T(8,128)}, u32[]{:S(2)}) %copy-start.2) | copy-done | bytes 1114136
  1.9 1.2 %copy-done.4 = f32[68,32,128]{2,1,0:T(8,128)S(1)} copy-done((f32[68,32,128]{2,1,0:T(8,128)S(1)}, f32[68,32,128]{2,1,0:T(8,128)}, u32[]{:S(2)}) %copy-start.4) | copy-done | bytes 1114136
  3.2 4.1 %wind_edges.1 = (f32[2,68,128]{2,1,0:T(8,128)S(1)}, f32[2,68,128]{2,1,0:T(8,128)S(1)}, f32[68,128]{1,0:T(8,128)S(1)}) custom-call(f32[68,32,128]{2,1,0:T(8,128)S(1)} %copy-done.2, f32[68,32,128]{2,1,0:T(8,128)S(1)} %copy-done.4), custom_call_target="tpu_custom_call" | custom-call | tf_op jit(solution)/shard_map/wind_edges/pallas_call | solution.py:30
  7.3 4.5 %collective-permute-start = (f32[2,68,128]{2,1,0:T(8,128)S(1)}, f32[2,68,128]{2,1,0:T(8,128)S(1)}, u32[]{:S(2)}, u32[]{:S(2)}) collective-permute-start(f32[2,68,128]{2,1,0:T(8,128)S(1)} %get-tuple-element.14), channel_id=1, source_target_pairs={{0,8},{8,16},{16,24},{1,9},{9,17},{17,25},{2,10},{10,18},{18,26},{... | collective-permute-start | bytes 208904 | tf_op jit(solution)/shard_map/ppermute | solution.py:325
  11.9 1.9 %collective-permute-start.1 = (f32[2,68,128]{2,1,0:T(8,128)S(1)}, f32[2,68,128]{2,1,0:T(8,128)S(1)}, u32[]{:S(2)}, u32[]{:S(2)}) collective-permute-start(f32[2,68,128]{2,1,0:T(8,128)S(1)} %get-tuple-element.15), channel_id=1, source_target_pairs={{8,0},{16,8},{24,16},{9,1},{17,9},{25,17},{10,2},{18,10},{26,18},{... | collective-permute-start | bytes 208904 | tf_op jit(solution)/shard_map/ppermute | solution.py:326
  13.8 1.3 %collective-permute-start.3 = (f32[68,128]{1,0:T(8,128)S(1)}, f32[68,128]{1,0:T(8,128)S(1)}, u32[]{:S(2)}, u32[]{:S(2)}) collective-permute-start(f32[68,128]{1,0:T(8,128)S(1)} %get-tuple-element.16), channel_id=1, source_target_pairs={{2,0},{4,2},{6,4},{3,1},{5,3},{7,5},{10,8},{12,10},{14,12},{11,9},... | collective-permute-start | bytes 104456 | tf_op jit(solution)/shard_map/ppermute | solution.py:328
  15.1 4.0 %collective-permute-start.2 = (f32[68,128]{1,0:T(8,128)S(1)}, f32[68,128]{1,0:T(8,128)S(1)}, u32[]{:S(2)}, u32[]{:S(2)}) collective-permute-start(f32[68,128]{1,0:T(8,128)S(1)} %get-tuple-element.16), channel_id=1, source_target_pairs={{0,2},{2,4},{4,6},{1,3},{3,5},{5,7},{8,10},{10,12},{12,14},{9,11},... | collective-permute-start | bytes 104456 | tf_op jit(solution)/shard_map/ppermute | solution.py:327
  19.1 1.0 collective-permute-done.2.vl_ref
  20.1 12.0 %source_rows.1 = (f32[18,72,128]{2,1,0:T(8,128)S(1)}, f32[16,72,128]{2,1,0:T(8,128)S(1)}, f32[8,72,128]{2,1,0:T(8,128)S(1)}, f32[8,72,128]{2,1,0:T(8,128)}) custom-call(f32[68,32,128]{2,1,0:T(8,128)S(1)} %copy-done.2, f32[68,32,128]{2,1,0:T(8,128)S(1)} %copy-done.4, f32[68,32,128]{2,1,0:T(8,128)S(1)} %copy-done.6, ...), custom_call_target="tpu_custom_call" | custom-call | tf_op jit(solution)/shard_map/source_rows/pallas_call | solution.py:30
  32.2 1.3 %collective-permute-start.4 = (f32[18,72,128]{2,1,0:T(8,128)S(1)}, f32[18,72,128]{2,1,0:T(8,128)S(1)}, u32[]{:S(2)}, u32[]{:S(2)}) collective-permute-start(f32[18,72,128]{2,1,0:T(8,128)S(1)} %get-tuple-element.17.edge_ref.refs_0_), channel_id=1, source_target_pairs={{1,0},{0,1},{3,2},{2,3},{5,4},{4,5},{7,6},{6,7},{9,8},{8,9},{11,10... | collective-permute-start | bytes 1990664 | tf_op jit(solution)/shard_map/ppermute | solution.py:373
  33.5 5.0 %collective-permute-start.10 = (f32[8,72,128]{2,1,0:T(8,128)}, f32[8,72,128]{2,1,0:T(8,128)S(1)}, u32[]{:S(2)}, u32[]{:S(2)}) collective-permute-start(f32[8,72,128]{2,1,0:T(8,128)} %get-tuple-element.21), channel_id=1, source_target_pairs={{0,8},{8,16},{16,24},{1,9},{9,17},{17,25},{2,10},{10,18},{18,26},{... | collective-permute-start | bytes 884744 | tf_op jit(solution)/shard_map/ppermute | solution.py:376
  38.5 1.9 %collective-permute-start.11 = (f32[8,72,128]{2,1,0:T(8,128)S(1)}, f32[8,72,128]{2,1,0:T(8,128)S(1)}, u32[]{:S(2)}, u32[]{:S(2)}) collective-permute-start(f32[8,72,128]{2,1,0:T(8,128)S(1)} %get-tuple-element.22), channel_id=1, source_target_pairs={{8,0},{16,8},{24,16},{9,1},{17,9},{25,17},{10,2},{18,10},{26,18},{... | collective-permute-start | bytes 884744 | tf_op jit(solution)/shard_map/ppermute | solution.py:377
  40.8 8.5 %collective-permute-done.4.edge_ref.refs_0_ = f32[18,72,128]{2,1,0:T(8,128)S(1)} collective-permute-done((f32[18,72,128]{2,1,0:T(8,128)S(1)}, f32[18,72,128]{2,1,0:T(8,128)S(1)}, u32[]{:S(2)}, u32[]{:S(2)}) %collective-permute-start.4) | collective-permute-done | bytes 663584 | tf_op jit(solution)/shard_map/ppermute | solution.py:373
  50.1 1.9 %collective-permute-start.7 = (f32[8,72,128]{2,1,0:T(8,128)}, f32[8,72,128]{2,1,0:T(8,128)S(1)}, u32[]{:S(2)}, u32[]{:S(2)}) collective-permute-start(f32[8,72,128]{2,1,0:T(8,128)} %get-tuple-element.25), channel_id=1, source_target_pairs={{8,0},{16,8},{24,16},{9,1},{17,9},{25,17},{10,2},{18,10},{26,18},{... | collective-permute-start | bytes 884744 | tf_op jit(solution)/shard_map/ppermute | solution.py:377
  52.0 5.6 %collective-permute-start.6 = (f32[8,72,128]{2,1,0:T(8,128)}, f32[8,72,128]{2,1,0:T(8,128)S(1)}, u32[]{:S(2)}, u32[]{:S(2)}) collective-permute-start(f32[8,72,128]{2,1,0:T(8,128)} %get-tuple-element.26), channel_id=1, source_target_pairs={{0,8},{8,16},{16,24},{1,9},{9,17},{17,25},{2,10},{10,18},{18,26},{... | collective-permute-start | bytes 884744 | tf_op jit(solution)/shard_map/ppermute | solution.py:376
  57.7 1.1 constant_dynamic-slice_fusion
  58.9 0.9 weights.2.refs_6_
  61.3 4.0 %collective-permute-start.12 = (f32[3,72,128]{2,1,0:T(8,128)S(1)}, f32[3,72,128]{2,1,0:T(8,128)S(1)}, u32[]{:S(2)}, u32[]{:S(2)}) collective-permute-start(f32[3,72,128]{2,1,0:T(8,128)S(1)} %get-tuple-element.23), channel_id=1, source_target_pairs={{0,2},{2,4},{4,6},{1,3},{3,5},{5,7},{8,10},{10,12},{12,14},{9,11},... | collective-permute-start | bytes 331784 | tf_op jit(solution)/shard_map/ppermute | solution.py:386
  65.2 1.3 %collective-permute-start.13 = (f32[3,72,128]{2,1,0:T(8,128)S(1)}, f32[3,72,128]{2,1,0:T(8,128)S(1)}, u32[]{:S(2)}, u32[]{:S(2)}) collective-permute-start(f32[3,72,128]{2,1,0:T(8,128)S(1)} %get-tuple-element.24), channel_id=1, source_target_pairs={{2,0},{4,2},{6,4},{3,1},{5,3},{7,5},{10,8},{12,10},{14,12},{11,9},... | collective-permute-start | bytes 331784 | tf_op jit(solution)/shard_map/ppermute | solution.py:387
  67.0 4.0 %collective-permute-start.8 = (f32[3,72,128]{2,1,0:T(8,128)S(1)}, f32[3,72,128]{2,1,0:T(8,128)S(1)}, u32[]{:S(2)}, u32[]{:S(2)}) collective-permute-start(f32[3,72,128]{2,1,0:T(8,128)S(1)} %get-tuple-element.19), channel_id=1, source_target_pairs={{0,2},{2,4},{4,6},{1,3},{3,5},{5,7},{8,10},{10,12},{12,14},{9,11},... | collective-permute-start | bytes 331784 | tf_op jit(solution)/shard_map/ppermute | solution.py:386
  71.0 1.5 %collective-permute-start.9 = (f32[3,72,128]{2,1,0:T(8,128)S(1)}, f32[3,72,128]{2,1,0:T(8,128)S(1)}, u32[]{:S(2)}, u32[]{:S(2)}) collective-permute-start(f32[3,72,128]{2,1,0:T(8,128)S(1)} %get-tuple-element.20), channel_id=1, source_target_pairs={{2,0},{4,2},{6,4},{3,1},{5,3},{7,5},{10,8},{12,10},{14,12},{11,9},... | collective-permute-start | bytes 331784 | tf_op jit(solution)/shard_map/ppermute | solution.py:387
  72.6 15.8 %level_part.2.refs_7_ = f32[36,144,128]{2,1,0:T(8,128)S(1)} custom-call(s32[2]{0:T(128)S(1)} %pad_add_fusion.place_ref, f32[18,72,128]{2,1,0:T(8,128)S(1)} %get-tuple-element.17.edge_ref.refs_0_, f32[16,72,128]{2,1,0:T(8,128)S(1)} %get-tuple-element.18.refs_1_, f32[8,72,128]{2,1,0:T(8,128)S(1)} %collective-permute-done.10.below_ref.refs_2_, ...), custom_call_target="tpu_custom_call" | custom-call | tf_op jit(solution)/shard_map/level_part/pallas_call | solution.py:30
  88.4 1.5 %copy-done.1 = f32[36,144,128]{2,1,0:T(8,128)} copy-done((f32[36,144,128]{2,1,0:T(8,128)}, f32[36,144,128]{2,1,0:T(8,128)S(1)}, u32[]{:S(2)}) %copy-start.1) | copy-done | bytes 2654232
  89.9 24.6 %level_part.3 = (f32[68,32,128]{2,1,0:T(8,128)}, f32[68,32,128]{2,1,0:T(8,128)}, f32[68,32,128]{2,1,0:T(8,128)}) custom-call(s32[2]{0:T(128)S(1)} %pad_add_fusion.place_ref, f32[18,72,128]{2,1,0:T(8,128)S(1)} %collective-permute-done.4.edge_ref.refs_0_, f32[16,72,128]{2,1,0:T(8,128)} %collective-permute-done.5.refs_1_, ...), custom_call_target="tpu_custom_call" | custom-call | tf_op jit(solution)/shard_map/level_part/pallas_call | solution.py:30
  (35 shorter events, 3.2 us)
Async XLA Ops:
  0.6 57.1 %copy-start = (f32[136,136]{1,0:T(8,128)S(1)}, f32[136,136]{1,0:T(8,128)}, u32[]{:S(2)}) copy-start(f32[136,136]{1,0:T(8,128)} %param.10) | copy-start | bytes 221956
  0.6 1.3 %copy-start.2 = (f32[68,32,128]{2,1,0:T(8,128)S(1)}, f32[68,32,128]{2,1,0:T(8,128)}, u32[]{:S(2)}) copy-start(f32[68,32,128]{2,1,0:T(8,128)} %refs_8_.1) | copy-start | bytes 3342340
  1.9 1.2 %copy-start.4 = (f32[68,32,128]{2,1,0:T(8,128)S(1)}, f32[68,32,128]{2,1,0:T(8,128)}, u32[]{:S(2)}) copy-start(f32[68,32,128]{2,1,0:T(8,128)} %refs_9_.1) | copy-start | bytes 3342340
  3.2 17.0 %copy-start.6 = (f32[68,32,128]{2,1,0:T(8,128)S(1)}, f32[68,32,128]{2,1,0:T(8,128)}, u32[]{:S(2)}) copy-start(f32[68,32,128]{2,1,0:T(8,128)} %h_ref.1) | copy-start | bytes 3342340
  7.3 12.8 %collective-permute-start = (f32[2,68,128]{2,1,0:T(8,128)S(1)}, f32[2,68,128]{2,1,0:T(8,128)S(1)}, u32[]{:S(2)}, u32[]{:S(2)}) collective-permute-start(f32[2,68,128]{2,1,0:T(8,128)S(1)} %get-tuple-element.14), channel_id=1, source_target_pairs={{0,8},{8,16},{16,24},{1,9},{9,17},{17,25},{2,10},{10,18},{18,26},{... | collective-permute-start | bytes 208904 | tf_op jit(solution)/shard_map/ppermute | solution.py:325
  11.9 8.3 %collective-permute-start.1 = (f32[2,68,128]{2,1,0:T(8,128)S(1)}, f32[2,68,128]{2,1,0:T(8,128)S(1)}, u32[]{:S(2)}, u32[]{:S(2)}) collective-permute-start(f32[2,68,128]{2,1,0:T(8,128)S(1)} %get-tuple-element.15), channel_id=1, source_target_pairs={{8,0},{16,8},{24,16},{9,1},{17,9},{25,17},{10,2},{18,10},{26,18},{... | collective-permute-start | bytes 208904 | tf_op jit(solution)/shard_map/ppermute | solution.py:326
  13.8 5.3 %collective-permute-start.3 = (f32[68,128]{1,0:T(8,128)S(1)}, f32[68,128]{1,0:T(8,128)S(1)}, u32[]{:S(2)}, u32[]{:S(2)}) collective-permute-start(f32[68,128]{1,0:T(8,128)S(1)} %get-tuple-element.16), channel_id=1, source_target_pairs={{2,0},{4,2},{6,4},{3,1},{5,3},{7,5},{10,8},{12,10},{14,12},{11,9},... | collective-permute-start | bytes 104456 | tf_op jit(solution)/shard_map/ppermute | solution.py:328
  15.1 5.0 %collective-permute-start.2 = (f32[68,128]{1,0:T(8,128)S(1)}, f32[68,128]{1,0:T(8,128)S(1)}, u32[]{:S(2)}, u32[]{:S(2)}) collective-permute-start(f32[68,128]{1,0:T(8,128)S(1)} %get-tuple-element.16), channel_id=1, source_target_pairs={{0,2},{2,4},{4,6},{1,3},{3,5},{5,7},{8,10},{10,12},{12,14},{9,11},... | collective-permute-start | bytes 104456 | tf_op jit(solution)/shard_map/ppermute | solution.py:327
  32.2 26.7 %copy-start.7 = (f32[136]{0:T(256)S(1)}, f32[136]{0:T(256)}, u32[]{:S(2)}) copy-start(f32[136]{0:T(256)} %param.11) | copy-start | bytes 1636
  32.2 17.1 %collective-permute-start.4 = (f32[18,72,128]{2,1,0:T(8,128)S(1)}, f32[18,72,128]{2,1,0:T(8,128)S(1)}, u32[]{:S(2)}, u32[]{:S(2)}) collective-permute-start(f32[18,72,128]{2,1,0:T(8,128)S(1)} %get-tuple-element.17.edge_ref.refs_0_), channel_id=1, source_target_pairs={{1,0},{0,1},{3,2},{2,3},{5,4},{4,5},{7,6},{6,7},{9,8},{8,9},{11,10... | collective-permute-start | bytes 1990664 | tf_op jit(solution)/shard_map/ppermute | solution.py:373
  33.5 27.3 %collective-permute-start.10 = (f32[8,72,128]{2,1,0:T(8,128)}, f32[8,72,128]{2,1,0:T(8,128)S(1)}, u32[]{:S(2)}, u32[]{:S(2)}) collective-permute-start(f32[8,72,128]{2,1,0:T(8,128)} %get-tuple-element.21), channel_id=1, source_target_pairs={{0,8},{8,16},{16,24},{1,9},{9,17},{17,25},{2,10},{10,18},{18,26},{... | collective-permute-start | bytes 884744 | tf_op jit(solution)/shard_map/ppermute | solution.py:376
  38.5 22.3 %collective-permute-start.11 = (f32[8,72,128]{2,1,0:T(8,128)S(1)}, f32[8,72,128]{2,1,0:T(8,128)S(1)}, u32[]{:S(2)}, u32[]{:S(2)}) collective-permute-start(f32[8,72,128]{2,1,0:T(8,128)S(1)} %get-tuple-element.22), channel_id=1, source_target_pairs={{8,0},{16,8},{24,16},{9,1},{17,9},{25,17},{10,2},{18,10},{26,18},{... | collective-permute-start | bytes 884744 | tf_op jit(solution)/shard_map/ppermute | solution.py:377
  40.5 49.4 %collective-permute-start.5 = (f32[16,72,128]{2,1,0:T(8,128)S(1)}, f32[16,72,128]{2,1,0:T(8,128)}, u32[]{:S(2)}, u32[]{:S(2)}) collective-permute-start(f32[16,72,128]{2,1,0:T(8,128)S(1)} %get-tuple-element.18.refs_1_), channel_id=1, source_target_pairs={{1,0},{0,1},{3,2},{2,3},{5,4},{4,5},{7,6},{6,7},{9,8},{8,9},{11,10... | collective-permute-start | bytes 1769480 | tf_op jit(solution)/shard_map/ppermute | solution.py:374
  50.1 16.4 %collective-permute-start.7 = (f32[8,72,128]{2,1,0:T(8,128)}, f32[8,72,128]{2,1,0:T(8,128)S(1)}, u32[]{:S(2)}, u32[]{:S(2)}) collective-permute-start(f32[8,72,128]{2,1,0:T(8,128)} %get-tuple-element.25), channel_id=1, source_target_pairs={{8,0},{16,8},{24,16},{9,1},{17,9},{25,17},{10,2},{18,10},{26,18},{... | collective-permute-start | bytes 884744 | tf_op jit(solution)/shard_map/ppermute | solution.py:377
  52.0 14.5 %collective-permute-start.6 = (f32[8,72,128]{2,1,0:T(8,128)}, f32[8,72,128]{2,1,0:T(8,128)S(1)}, u32[]{:S(2)}, u32[]{:S(2)}) collective-permute-start(f32[8,72,128]{2,1,0:T(8,128)} %get-tuple-element.26), channel_id=1, source_target_pairs={{0,8},{8,16},{16,24},{1,9},{9,17},{17,25},{2,10},{10,18},{18,26},{... | collective-permute-start | bytes 884744 | tf_op jit(solution)/shard_map/ppermute | solution.py:376
  61.3 11.3 %collective-permute-start.12 = (f32[3,72,128]{2,1,0:T(8,128)S(1)}, f32[3,72,128]{2,1,0:T(8,128)S(1)}, u32[]{:S(2)}, u32[]{:S(2)}) collective-permute-start(f32[3,72,128]{2,1,0:T(8,128)S(1)} %get-tuple-element.23), channel_id=1, source_target_pairs={{0,2},{2,4},{4,6},{1,3},{3,5},{5,7},{8,10},{10,12},{12,14},{9,11},... | collective-permute-start | bytes 331784 | tf_op jit(solution)/shard_map/ppermute | solution.py:386
  65.2 7.3 %collective-permute-start.13 = (f32[3,72,128]{2,1,0:T(8,128)S(1)}, f32[3,72,128]{2,1,0:T(8,128)S(1)}, u32[]{:S(2)}, u32[]{:S(2)}) collective-permute-start(f32[3,72,128]{2,1,0:T(8,128)S(1)} %get-tuple-element.24), channel_id=1, source_target_pairs={{2,0},{4,2},{6,4},{3,1},{5,3},{7,5},{10,8},{12,10},{14,12},{11,9},... | collective-permute-start | bytes 331784 | tf_op jit(solution)/shard_map/ppermute | solution.py:387
  67.0 22.9 %collective-permute-start.8 = (f32[3,72,128]{2,1,0:T(8,128)S(1)}, f32[3,72,128]{2,1,0:T(8,128)S(1)}, u32[]{:S(2)}, u32[]{:S(2)}) collective-permute-start(f32[3,72,128]{2,1,0:T(8,128)S(1)} %get-tuple-element.19), channel_id=1, source_target_pairs={{0,2},{2,4},{4,6},{1,3},{3,5},{5,7},{8,10},{10,12},{12,14},{9,11},... | collective-permute-start | bytes 331784 | tf_op jit(solution)/shard_map/ppermute | solution.py:386
  71.0 18.9 %collective-permute-start.9 = (f32[3,72,128]{2,1,0:T(8,128)S(1)}, f32[3,72,128]{2,1,0:T(8,128)S(1)}, u32[]{:S(2)}, u32[]{:S(2)}) collective-permute-start(f32[3,72,128]{2,1,0:T(8,128)S(1)} %get-tuple-element.20), channel_id=1, source_target_pairs={{2,0},{4,2},{6,4},{3,1},{5,3},{7,5},{10,8},{12,10},{14,12},{11,9},... | collective-permute-start | bytes 331784 | tf_op jit(solution)/shard_map/ppermute | solution.py:387
  72.6 17.4 %copy-start.3 = (f32[68,32,128]{2,1,0:T(8,128)S(1)}, f32[68,32,128]{2,1,0:T(8,128)}, u32[]{:S(2)}) copy-start(f32[68,32,128]{2,1,0:T(8,128)} %refs_8_.1) | copy-start | bytes 3342340
  72.6 17.4 %copy-start.5 = (f32[68,32,128]{2,1,0:T(8,128)S(1)}, f32[68,32,128]{2,1,0:T(8,128)}, u32[]{:S(2)}) copy-start(f32[68,32,128]{2,1,0:T(8,128)} %refs_9_.1) | copy-start | bytes 3342340
  88.4 1.5 %copy-start.1 = (f32[36,144,128]{2,1,0:T(8,128)}, f32[36,144,128]{2,1,0:T(8,128)S(1)}, u32[]{:S(2)}) copy-start(f32[36,144,128]{2,1,0:T(8,128)S(1)} %level_part.2.refs_7_) | copy-start | bytes 7962628

commit v3 on v2

v3 whole, which is shorter than its diff:
```python
import functools

import jax
import jax.numpy as jnp
from jax import lax
from jax.experimental import pallas as pl
from jax.experimental.pallas import tpu as pltpu
from jax.sharding import PartitionSpec as P

SWEEPS = 6
HALO = SWEEPS + 2
TERMS = SWEEPS + 1
LANES = 128
VMEM = pl.BlockSpec(memory_space=pltpu.VMEM)
SMEM = pl.BlockSpec(memory_space=pltpu.SMEM)
HBM = pl.BlockSpec(memory_space=pltpu.HBM)
F32 = jnp.float32
BF16 = jnp.bfloat16


def up_to(n, k):
    return (n + k - 1) // k * k


def lanes_of():
    return lax.broadcasted_iota(jnp.int32, (1, LANES), 1)


def call(body, outs, *args, specs=None, out_specs=None, scratch=(), vmem=48 << 20, name):
    return pl.pallas_call(
        body,
        out_shape=outs,
        in_specs=specs or [VMEM] * len(args),
        out_specs=out_specs or jax.tree.map(lambda _: VMEM, outs),
        scratch_shapes=list(scratch),
        compiler_params=pltpu.CompilerParams(vmem_limit_bytes=vmem),
        name=name,
    )(*args)


def start_rows(src_ref, dst_ref, sems, rows):
    copies = {x: pltpu.make_async_copy(src_ref.at[:, x, :], dst_ref.at[x], sems.at[x]) for x in rows}
    for copy in copies.values():
        copy.start()
    return copies


def north_step(main, side):
    lane = lanes_of()
    one = pltpu.roll(jnp.where(lane < 1, side, main), LANES - 1, 1) - pltpu.roll(
        jnp.where(lane >= LANES - 1, side, main), 1, 1
    )
    two = pltpu.roll(jnp.where(lane < 2, side, main), LANES - 2, 1) - pltpu.roll(
        jnp.where(lane >= LANES - 2, side, main), 2, 1
    )
    return 8.0 * one - two


def source_row(x, at, v, h, side):
    dx = 8.0 * (at(x + 1) - at(x - 1)) - (at(x + 2) - at(x - 2))
    return h - (dx + north_step(v, side)) * (1.0 / 12.0)


def put_padded(ref, i, value):
    levels, pad = value.shape[0], ref.shape[1] - value.shape[0]
    ref[i, :levels] = value
    if pad:
        ref[i, levels:] = jnp.zeros((pad, LANES), F32)


def inner_rows(u_ref, v_ref, h_ref, lo_ref, hi_ref, cols_ref, mid_ref, u_rows, v_rows, h_rows, sems, edge_sems):
    rows = u_ref.shape[1]
    lane = lanes_of()
    edges = []
    for i in range(2):
        edges.append(pltpu.make_async_copy(u_ref.at[:, i, :], lo_ref.at[i], edge_sems.at[i]))
        edges.append(pltpu.make_async_copy(u_ref.at[:, rows - 2 + i, :], hi_ref.at[i], edge_sems.at[2 + i]))
    for copy in edges:
        copy.start()
    v_loads = start_rows(v_ref, v_rows, sems.at[0], range(rows))
    u_loads = start_rows(u_ref, u_rows, sems.at[1], range(HALO - 2, rows - HALO + 2))
    h_loads = start_rows(h_ref, h_rows, sems.at[2], range(HALO, rows - HALO))
    for copy in v_loads.values():
        copy.wait()
    packed = None
    for x in range(rows):
        rolled = pltpu.roll(v_rows[x], (4 * x + 2) % LANES, 1)
        packed = rolled if packed is None else jnp.where(lane // 4 == x, rolled, packed)
    cols_ref[...] = packed
    for copy in (*u_loads.values(), *h_loads.values()):
        copy.wait()
    for x in range(HALO, rows - HALO):
        put_padded(mid_ref, x - HALO, source_row(x, lambda i: u_rows[i], v_rows[x], h_rows[x], v_rows[x]))
    for copy in edges:
        copy.wait()


def outer_rows(
    u_ref, v_ref, h_ref, ulo_ref, uhi_ref, vl_ref, vr_ref, low_ref, high_ref, pack_ref, u_rows, v_rows, h_rows, sems
):
    rows = u_ref.shape[1]
    lane = lanes_of()
    loads = [start_rows(ref, to, sems.at[i], range(rows)) for i, (ref, to) in enumerate(((u_ref, u_rows), (v_ref, v_rows), (h_ref, h_rows)))]
    vside = jnp.where(lane % 4 < 2, vl_ref[...], vr_ref[...])

    def at(x):
        if x < 0:
            return ulo_ref[2 + x]
        if x >= rows:
            return uhi_ref[x - rows]
        return u_rows[x]

    for some in loads:
        for copy in some.values():
            copy.wait()
    packed = None
    for x in range(rows):
        side = pltpu.roll(vside, (LANES - 4 * x - 2) % LANES, 1)
        s = source_row(x, at, v_rows[x], h_rows[x], side)
        m, k = divmod(x, 8)
        if x < HALO:
            put_padded(low_ref, x, s)
        elif x >= rows - HALO:
            put_padded(high_ref, x - rows + HALO, s)
        else:
            rolled = pltpu.roll(s, (16 * k + 8) % LANES, 1)
            packed = rolled if k == 0 else jnp.where(lane // 16 == k, rolled, packed)
            if k == 7:
                put_padded(pack_ref, m - 1, packed)


def column_messages(low_ref, high_ref, pack_ref, below_ref, above_ref, right_ref, left_ref):
    lane = lanes_of()
    slot = lane % 16

    def pack(ref):
        packed = pltpu.roll(ref[0], 8, 1)
        for k in range(1, 8):
            packed = jnp.where(lane // 16 == k, pltpu.roll(ref[k], (16 * k + 8) % LANES, 1), packed)
        return packed

    packs = [pack(below_ref), pack(low_ref)]
    packs += [pack_ref[i] for i in range(pack_ref.shape[0])]
    packs += [pack(high_ref), pack(above_ref)]
    for i in range(len(packs) // 2):
        even, odd = packs[2 * i], packs[2 * i + 1]
        right_ref[i] = jnp.where(slot < 8, even, pltpu.roll(odd, 8, 1))
        left_ref[i] = jnp.where(slot < 8, pltpu.roll(even, LANES - 8, 1), odd)


def weights(levels_ref, modes_ref, coef_ref, out_ref):
    groups, _, kp = modes_ref.shape
    coef = coef_ref[...]
    denom = 1.0 + 4.0 * coef
    scaled = levels_ref[...] / denom
    ratio = coef / denom
    for j in range(TERMS):
        at = pl.ds(j * LANES, LANES)
        for g in range(groups):
            m = jnp.dot(scaled, modes_ref[g], precision=lax.Precision.HIGHEST, preferred_element_type=F32).T
            high = m.astype(BF16)
            low = (m - high.astype(F32)).astype(BF16)
            for i, part in enumerate((high, high, low)):
                out_ref[pl.ds((3 * g + i) * kp, kp), at] = part
        scaled = scaled * ratio


PARTS = 8


def finish(place_ref, w_ref, *refs, groups, limits):
    ins, refs = refs[: PARTS * groups], refs[PARTS * groups :]
    u_ref, v_ref, east_ref, north_ref, height_ref, s_ref, z_ref, t_ref, ga_ref, gb_ref, u_rows, v_rows, h_rows, sems = refs
    span, wide, _ = ga_ref.shape
    rows = span - 2 * HALO
    blocks = span // 8
    loads = [*start_rows(u_ref, u_rows, sems.at[0], range(rows)).values()]
    loads += start_rows(v_ref, v_rows, sems.at[1], range(rows)).values()
    lane = lanes_of()
    slot = lane % 16
    outer = (lane < HALO) | (lane >= LANES - HALO)
    kp = w_ref.shape[0] // (3 * groups)

    for g_ref in (ga_ref, gb_ref):
        g_ref[:, :8] = jnp.zeros((span, 8, LANES), F32)
        g_ref[:, wide - 8 :] = jnp.zeros((span, 8, LANES), F32)

    def parts(value):
        lp = value.shape[0]
        if kp > lp:
            value = jnp.concatenate([value, jnp.zeros((kp - lp, LANES), F32)], axis=0)
        high = value.astype(BF16)
        low = (value - high.astype(F32)).astype(BF16)
        return high, low, high

    for g in range(groups):
        low, high, pack, mid, below, above, left_ref, right_ref = ins[PARTS * g : PARTS * (g + 1)]
        sources = [below, low] + [mid.at[pl.ds(8 * i, 8)] for i in range(blocks - 4)] + [high, above]
        for m in range(blocks):
            fix = pack[m - 2] if 2 <= m < blocks - 2 else None

            def stage(k, _, ref=sources[m], fix=fix, m=m, g=g):
                value = ref[k]
                if fix is not None:
                    value = jnp.where(outer, pltpu.roll(fix, LANES - 16 * k - 8, 1), value)
                at = pl.ds(pl.multiple_of(k * LANES, LANES), LANES)
                for i, part in enumerate(parts(value)):
                    s_ref[m, pl.ds((3 * g + i) * kp, kp), at] = part
                return _

            lax.fori_loop(0, 8, stage, 0, unroll=4)
            zl, zr = left_ref[m // 2], right_ref[m // 2]
            if m % 2 == 0:
                side = jnp.where(slot < 8, zl, pltpu.roll(zr, 8, 1))
            else:
                side = jnp.where(slot < 8, pltpu.roll(zl, LANES - 8, 1), zr)
            for i, part in enumerate(parts(side)):
                z_ref[pl.ds((3 * g + i) * kp, kp), m * LANES : (m + 1) * LANES] = part

    def put(x, col, part):
        n = part.shape[0]
        for j in range(SWEEPS):
            t_ref[j, x, pl.ds(col, n)] = part[:, j * LANES : (j + 1) * LANES]
        ga_ref[x, pl.ds(col + 8, n)] = part[:, SWEEPS * LANES :]

    def mix(operand):
        return lax.dot_general(operand, w_ref[...], (((0,), (0,)), ((), ())), preferred_element_type=F32)

    def block(m, _):
        part = mix(s_ref[m])
        for k in range(8):
            put(8 * m + k, HALO, part[k * LANES : (k + 1) * LANES])
        return _

    lax.fori_loop(0, blocks, block, 0)
    part = mix(z_ref[...])
    for x in range(span):
        put(x, 0, part[16 * x : 16 * x + 8])
        put(x, HALO + LANES, part[16 * x + 8 : 16 * x + 16])

    first_row = place_ref[0] * rows - HALO
    left = jnp.where(place_ref[1] > 0, 1.0, 0.0)
    right = jnp.where(place_ref[1] < limits[1] - 1, 1.0, 0.0)
    for step in range(SWEEPS):
        j = SWEEPS - 1 - step
        now, nxt = ((ga_ref, gb_ref), (gb_ref, ga_ref))[step % 2]
        reach = j + 2

        def sweep(x, _, now=now, nxt=nxt, j=j):
            row = first_row + x
            inside = jnp.where((row >= 0) & (row < limits[0] * rows), 1.0, 0.0)
            for y in range(8, wide - 8, 8):
                here = pl.ds(y, 8)
                total = (now[x - 1, here] + now[x + 1, here]) + (now[x, pl.ds(y - 1, 8)] + now[x, pl.ds(y + 1, 8)])
                mask = inside
                if y == 8:
                    mask = inside * left
                elif y == wide - 16:
                    mask = inside * right
                nxt[x, here] = (total + t_ref[j, x, pl.ds(y - 8, 8)]) * mask
            return _

        lax.fori_loop(HALO - reach, HALO + rows + reach, sweep, 0, unroll=4)

    done = (gb_ref, ga_ref)[(SWEEPS - 1) % 2]
    levels = u_rows.shape[1]

    def turn(x, _):
        h_rows[x] = done[x + HALO - 2, pl.ds(16, LANES)].T[:levels]
        return _

    lax.fori_loop(0, rows + 4, turn, 0, unroll=2)
    for copy in loads:
        copy.wait()

    def stores(x):
        return [
            pltpu.make_async_copy(src, dst.at[:, x, :], sems.at[i, x])
            for i, (src, dst) in enumerate(
                ((u_rows.at[x], east_ref), (v_rows.at[x], north_ref), (h_rows.at[x + 2], height_ref))
            )
        ]

    def output(x, _):
        def north(i):
            return done[x + HALO, pl.ds(16 + i, LANES)]

        dy = (8.0 * (north(1) - north(-1)) - (north(2) - north(-2))).T[:levels]
        dx = 8.0 * (h_rows[x + 3] - h_rows[x + 1]) - (h_rows[x + 4] - h_rows[x])
        u_rows[x] = u_rows[x] - dx * (1.0 / 12.0)
        v_rows[x] = v_rows[x] - dy * (1.0 / 12.0)
        for copy in stores(x):
            copy.start()
        return _

    lax.fori_loop(0, rows, output, 0, unroll=2)
    for x in range(rows):
        for copy in stores(x):
            copy.wait()


def shape(*dims, dtype=F32):
    return jax.ShapeDtypeStruct(dims, dtype)


def neighbours(axis):
    peers = lax.axis_size(axis)
    up = [(i, i + 1) for i in range(peers - 1)]
    return up, [(j, i) for i, j in up]


def on_device(east_wind, north_wind, height, to_modes, to_levels, mode_coef):
    levels, rows, cols = east_wind.shape
    groups = lax.axis_size("lev")
    limits = (lax.axis_size("gx"), lax.axis_size("gy"))
    lp, kp = up_to(levels, 8), up_to(levels, 16)
    span = rows + 2 * HALO
    x_up, x_down = neighbours("gx")
    y_up, y_down = neighbours("gy")
    dma = pltpu.SemaphoreType.DMA
    row_block = pltpu.VMEM((rows, levels, cols), F32)

    east_wind, north_wind, height = (
        pltpu.with_memory_space_constraint(value, pltpu.HBM) for value in (east_wind, north_wind, height)
    )

    def to_others(value):
        return [value] + [
            lax.ppermute(value, "lev", [((i + d) % groups, i) for i in range(groups)]) for d in range(1, groups)
        ]

    lo, hi, packed, mid = call(
        inner_rows,
        (
            shape(2, levels, LANES),
            shape(2, levels, LANES),
            shape(levels, LANES),
            shape(rows - 2 * HALO, lp, LANES),
        ),
        east_wind,
        north_wind,
        height,
        specs=[HBM] * 3,
        scratch=(row_block, row_block, row_block, dma((3, rows)), dma((4,))),
        name="inner_rows",
    )
    mids = to_others(mid)
    halo = (
        lax.ppermute(hi, "gx", x_up),
        lax.ppermute(lo, "gx", x_down),
        lax.ppermute(packed, "gy", y_up),
        lax.ppermute(packed, "gy", y_down),
    )

    me = lax.axis_index("lev")
    my_levels = lax.dynamic_slice_in_dim(to_levels, me * levels, levels, 0)
    my_levels = jnp.pad(my_levels, ((0, LANES - levels), (0, 0)))
    modes = []
    for d in range(groups):
        part = lax.dynamic_slice_in_dim(to_modes, (me + d) % groups * levels, levels, 1)
        modes.append(jnp.pad(part, ((0, 0), (0, kp - levels))))
    w = call(
        weights,
        shape(groups * 3 * kp, TERMS * LANES, dtype=BF16),
        my_levels,
        jnp.stack(modes),
        mode_coef.reshape(1, -1),
        name="weights",
    )
    place = jnp.stack([lax.axis_index("gx"), lax.axis_index("gy")]).astype(jnp.int32)
    halo, w, place, mids = lax.optimization_barrier((halo, w, place, mids))

    low, high, pack = call(
        outer_rows,
        (shape(HALO, lp, LANES), shape(HALO, lp, LANES), shape(rows // 8 - 2, lp, LANES)),
        east_wind,
        north_wind,
        height,
        *halo,
        specs=[HBM] * 3 + [VMEM] * 4,
        scratch=(row_block, row_block, row_block, dma((3, rows))),
        name="outer_rows",
    )
    highs, lows, packs = to_others(high), to_others(low), to_others(pack)
    below = lax.ppermute(high, "gx", x_up)
    above = lax.ppermute(low, "gx", x_down)
    right, left = call(
        column_messages,
        (shape(span // 16, lp, LANES), shape(span // 16, lp, LANES)),
        low,
        high,
        pack,
        below,
        above,
        name="column_messages",
    )
    from_left = lax.ppermute(right, "gy", y_up)
    from_right = lax.ppermute(left, "gy", y_down)
    highs, lows, packs, from_left, from_right = lax.optimization_barrier((highs, lows, packs, from_left, from_right))
    belows = [below] + [lax.ppermute(h, "gx", x_up) for h in highs[1:]]
    aboves = [above] + [lax.ppermute(l, "gx", x_down) for l in lows[1:]]
    from_left, from_right = to_others(from_left), to_others(from_right)
    operands = []
    for d in range(groups):
        operands += [lows[d], highs[d], packs[d], mids[d], belows[d], aboves[d], from_left[d], from_right[d]]
    out = shape(levels, rows, cols)
    k = groups * 3 * kp
    return call(
        functools.partial(finish, groups=groups, limits=limits),
        (out, out, out),
        place,
        w,
        *operands,
        east_wind,
        north_wind,
        specs=[SMEM] + [VMEM] * (1 + len(operands)) + [HBM] * 2,
        out_specs=(HBM, HBM, HBM),
        scratch=(
            pltpu.VMEM((span // 8, k, 8 * LANES), BF16),
            pltpu.VMEM((k, span // 8 * LANES), BF16),
            pltpu.VMEM((SWEEPS, span, cols + 16, LANES), F32),
            pltpu.VMEM((span, cols + 32, LANES), F32),
            pltpu.VMEM((span, cols + 32, LANES), F32),
            row_block,
            row_block,
            pltpu.VMEM((rows + 4, levels, cols), F32),
            dma((3, rows)),
        ),
        vmem=56 << 20,
        name="finish",
    )


def solution(mesh):
    return jax.shard_map(
        on_device,
        mesh=mesh,
        in_specs=(P("lev", "gx", "gy"), P("lev", "gx", "gy"), P("lev", "gx", "gy"), P(), P(), P()),
        out_specs=(P("lev", "gx", "gy"), P("lev", "gx", "gy"), P("lev", "gx", "gy")),
        check_vma=False,
    )
```

time: 115 us -> 88.9 us (0.77)
  Pallas kernels: 59.3 us -> 37.5 us
  starting transfers between devices: 38.5 us -> 32.6 us
  waiting for transfers between devices: 9.55 us -> 14 us
  local copies, waits for them, and re-layouts: 6.06 us -> 2.5 us
    pallas_call x8 -> x5, Pallas kernels: 59.3 us -> 37.5 us  [call(): pl.pallas_call(body, out_shape=outs, in_specs=specs or [VMEM] * len(args)...]
    ppermute x2 -> x1, starting transfers between devices: 7.95 us -> 3.21 us  [on_device(): from_left = lax.ppermute(right, 'gy', y_up)]
    ppermute x10 -> x14, waiting for transfers between devices: 9.54 us -> 14 us  [the longest x6 8.77 us: to_others(): lax.ppermute(value, 'lev', [((i + d) % groups, i) for i in range(groups)])]
    unnamed x16 -> x40, local copies, waits for them, and re-layouts: 4.07 us -> 2.36 us
    ppermute x2 -> x1, starting transfers between devices: 2.76 us -> 1.29 us  [on_device(): from_right = lax.ppermute(left, 'gy', y_down)]
    ppermute x10 -> x14, starting transfers between devices: 27.8 us -> 28.1 us  [the longest x6 5.49 us: to_others(): lax.ppermute(value, 'lev', [((i + d) % groups, i) for i in range(groups)])]
  transfers between devices with their start and end apart: 14 -> 16, of which waited for: 2 -> 6; matrix products, arithmetic and copies ran while one was open for 2% -> 1% of each run, Pallas kernels for 16% -> 2%
where the time goes in v3:
time: 88.9 us; the launch traced here: 88.3 us
  Pallas kernels  37.5 us (42%)
  starting transfers between devices  32.6 us (37%)
  waiting for transfers between devices  14 us (16%)
  local copies, waits for them, and re-layouts  2.5 us (3%)
  between operations  1.06 us (1%)
    pallas_call x5, Pallas kernels, call(): pl.pallas_call(body, out_shape=outs, in_specs=specs or [VMEM] * len(args)...  37.5 us
    ppermute x6, waiting for transfers between devices, to_others(): lax.ppermute(value, 'lev', [((i + d) % groups, i) for i in range(groups)])  8.77 us
    ppermute x6, starting transfers between devices, to_others(): lax.ppermute(value, 'lev', [((i + d) % groups, i) for i in range(groups)])  5.49 us
    ppermute x1, waiting for transfers between devices, on_device(): above = lax.ppermute(low, 'gx', x_down)  4.69 us
    ppermute x1, starting transfers between devices, on_device(): lax.ppermute(hi, 'gx', x_up)  4.55 us
    ppermute x1, starting transfers between devices, on_device(): lax.ppermute(packed, 'gy', y_up)  3.99 us
    ppermute x1, starting transfers between devices, on_device(): belows = [below] + [lax.ppermute(h, 'gx', x_up) for h in highs[1:]]  3.71 us
    ppermute x1, starting transfers between devices, on_device(): below = lax.ppermute(high, 'gx', x_up)  3.37 us
  transfers between devices with their start and end apart: 16, of which 6 were waited for; matrix products, arithmetic and copies ran while one was open for 1% of the time, Pallas kernels for 2%

profile of v3, /device:TPU:1, one launch (start us, length us, event | category | flops | bytes accessed | tf_op | source)
XLA Modules:
  0.0 88.3 jit_solution(13711017070085057231)
XLA Ops:
  0.7 3.6 %inner_rows.1 = (f32[2,68,128]{2,1,0:T(8,128)S(1)}, f32[2,68,128]{2,1,0:T(8,128)S(1)}, f32[68,128]{1,0:T(8,128)S(1)}, f32[16,72,128]{2,1,0:T(8,128)S(1)}) custom-call(f32[68,32,128]{2,1,0:T(8,128)} %refs_16_.1, f32[68,32,128]{2,1,0:T(8,128)} %refs_17_.1, f32[68,32,128]{2,1,0:T(8,128)} %h_ref.3), custom_call_target="tpu_custom_call" | custom-call | tf_op jit(solution)/shard_map/inner_rows/pallas_call | solution.py:30
  4.3 2.1 %collective-permute-start.4 = (f32[16,72,128]{2,1,0:T(8,128)S(1)}, f32[16,72,128]{2,1,0:T(8,128)S(1)}, u32[]{:S(2)}, u32[]{:S(2)}) collective-permute-start(f32[16,72,128]{2,1,0:T(8,128)S(1)} %get-tuple-element.46.refs_3_), channel_id=1, source_target_pairs={{1,0},{0,1},{3,2},{2,3},{5,4},{4,5},{7,6},{6,7},{9,8},{8,9},{11,10... | collective-permute-start | bytes 1769480 | tf_op jit(solution)/shard_map/ppermute | solution.py:329
  6.4 1.3 %collective-permute-start.3 = (f32[68,128]{1,0:T(8,128)S(1)}, f32[68,128]{1,0:T(8,128)S(1)}, u32[]{:S(2)}, u32[]{:S(2)}) collective-permute-start(f32[68,128]{1,0:T(8,128)S(1)} %get-tuple-element.30), channel_id=1, source_target_pairs={{2,0},{4,2},{6,4},{3,1},{5,3},{7,5},{10,8},{12,10},{14,12},{11,9},... | collective-permute-start | bytes 104456 | tf_op jit(solution)/shard_map/ppermute | solution.py:352
  7.7 4.0 %collective-permute-start.2 = (f32[68,128]{1,0:T(8,128)S(1)}, f32[68,128]{1,0:T(8,128)S(1)}, u32[]{:S(2)}, u32[]{:S(2)}) collective-permute-start(f32[68,128]{1,0:T(8,128)S(1)} %get-tuple-element.30), channel_id=1, source_target_pairs={{0,2},{2,4},{4,6},{1,3},{3,5},{5,7},{8,10},{10,12},{12,14},{9,11},... | collective-permute-start | bytes 104456 | tf_op jit(solution)/shard_map/ppermute | solution.py:351
  11.7 4.5 %collective-permute-start = (f32[2,68,128]{2,1,0:T(8,128)S(1)}, f32[2,68,128]{2,1,0:T(8,128)S(1)}, u32[]{:S(2)}, u32[]{:S(2)}) collective-permute-start(f32[2,68,128]{2,1,0:T(8,128)S(1)} %get-tuple-element.28), channel_id=1, source_target_pairs={{0,8},{8,16},{16,24},{1,9},{9,17},{17,25},{2,10},{10,18},{18,26},{... | collective-permute-start | bytes 208904 | tf_op jit(solution)/shard_map/ppermute | solution.py:349
  16.2 1.9 %collective-permute-start.1 = (f32[2,68,128]{2,1,0:T(8,128)S(1)}, f32[2,68,128]{2,1,0:T(8,128)S(1)}, u32[]{:S(2)}, u32[]{:S(2)}) collective-permute-start(f32[2,68,128]{2,1,0:T(8,128)S(1)} %get-tuple-element.29), channel_id=1, source_target_pairs={{8,0},{16,8},{24,16},{9,1},{17,9},{25,17},{10,2},{18,10},{26,18},{... | collective-permute-start | bytes 208904 | tf_op jit(solution)/shard_map/ppermute | solution.py:350
  18.4 0.6 pad_add_fusion.place_ref
  19.0 1.6 %weights.1.w_ref = bf16[480,896]{1,0:T(8,128)(2,1)S(1)} custom-call(f32[128,136]{1,0:T(8,128)S(1)} %pad.11.levels_ref, f32[2,136,80]{2,1,0:T(8,128)S(1)} %pad_maximum_fusion.modes_ref, f32[1,136]{1,0:T(1,128)S(1)} %bitcast.7), custom_call_target="tpu_custom_call" | custom-call | tf_op jit(solution)/shard_map/weights/pallas_call | solution.py:30
  20.7 0.9 %copy-done.1 = bf16[480,896]{1,0:T(8,128)(2,1)} copy-done((bf16[480,896]{1,0:T(8,128)(2,1)}, bf16[480,896]{1,0:T(8,128)(2,1)S(1)}, u32[]{:S(2)}) %copy-start.1) | copy-done | bytes 860184
  21.9 7.9 %outer_rows.1 = (f32[8,72,128]{2,1,0:T(8,128)S(1)}, f32[8,72,128]{2,1,0:T(8,128)S(1)}, f32[2,72,128]{2,1,0:T(8,128)S(1)}) custom-call(f32[68,32,128]{2,1,0:T(8,128)} %refs_16_.1, f32[68,32,128]{2,1,0:T(8,128)} %refs_17_.1, f32[68,32,128]{2,1,0:T(8,128)} %h_ref.3, f32[2,68,128]{2,1,0:T(8,128)S(1)} %collective-permute-done.ulo_ref, ...), custom_call_target="tpu_custom_call" | custom-call | tf_op jit(solution)/shard_map/outer_rows/pallas_call | solution.py:30
  29.8 3.4 %collective-permute-start.8 = (f32[8,72,128]{2,1,0:T(8,128)S(1)}, f32[8,72,128]{2,1,0:T(8,128)S(1)}, u32[]{:S(2)}, u32[]{:S(2)}) collective-permute-start(f32[8,72,128]{2,1,0:T(8,128)S(1)} %get-tuple-element.44.high_ref.refs_1_), channel_id=1, source_target_pairs={{0,8},{8,16},{16,24},{1,9},{9,17},{17,25},{2,10},{10,18},{18,26},{... | collective-permute-start | bytes 884744 | tf_op jit(solution)/shard_map/ppermute | solution.py:385
  33.2 1.9 %collective-permute-start.9 = (f32[8,72,128]{2,1,0:T(8,128)S(1)}, f32[8,72,128]{2,1,0:T(8,128)S(1)}, u32[]{:S(2)}, u32[]{:S(2)}) collective-permute-start(f32[8,72,128]{2,1,0:T(8,128)S(1)} %get-tuple-element.43.low_ref.refs_0_), channel_id=1, source_target_pairs={{8,0},{16,8},{24,16},{9,1},{17,9},{25,17},{10,2},{18,10},{26,18},{... | collective-permute-start | bytes 884744 | tf_op jit(solution)/shard_map/ppermute | solution.py:386
  35.5 1.2 %collective-permute-start.6 = (f32[8,72,128]{2,1,0:T(8,128)S(1)}, f32[8,72,128]{2,1,0:T(8,128)S(1)}, u32[]{:S(2)}, u32[]{:S(2)}) collective-permute-start(f32[8,72,128]{2,1,0:T(8,128)S(1)} %get-tuple-element.43.low_ref.refs_0_), channel_id=1, source_target_pairs={{1,0},{0,1},{3,2},{2,3},{5,4},{4,5},{7,6},{6,7},{9,8},{8,9},{11,10... | collective-permute-start | bytes 884744 | tf_op jit(solution)/shard_map/ppermute | solution.py:329
  36.9 4.7 %collective-permute-done.9.above_ref.refs_5_ = f32[8,72,128]{2,1,0:T(8,128)S(1)} collective-permute-done((f32[8,72,128]{2,1,0:T(8,128)S(1)}, f32[8,72,128]{2,1,0:T(8,128)S(1)}, u32[]{:S(2)}, u32[]{:S(2)}) %collective-permute-start.9) | collective-permute-done | bytes 294944 | tf_op jit(solution)/shard_map/ppermute | solution.py:386
  42.0 3.2 %collective-permute-start.10 = (f32[3,72,128]{2,1,0:T(8,128)S(1)}, f32[3,72,128]{2,1,0:T(8,128)S(1)}, u32[]{:S(2)}, u32[]{:S(2)}) collective-permute-start(f32[3,72,128]{2,1,0:T(8,128)S(1)} %get-tuple-element.41), channel_id=1, source_target_pairs={{0,2},{2,4},{4,6},{1,3},{3,5},{5,7},{8,10},{10,12},{12,14},{9,11},... | collective-permute-start | bytes 331784 | tf_op jit(solution)/shard_map/ppermute | solution.py:397
  45.2 1.3 %collective-permute-start.11 = (f32[3,72,128]{2,1,0:T(8,128)S(1)}, f32[3,72,128]{2,1,0:T(8,128)S(1)}, u32[]{:S(2)}, u32[]{:S(2)}) collective-permute-start(f32[3,72,128]{2,1,0:T(8,128)S(1)} %get-tuple-element.42), channel_id=1, source_target_pairs={{2,0},{4,2},{6,4},{3,1},{5,3},{7,5},{10,8},{12,10},{14,12},{11,9},... | collective-permute-start | bytes 331784 | tf_op jit(solution)/shard_map/ppermute | solution.py:398
  46.8 3.9 %collective-permute-done.7.refs_10_ = f32[2,72,128]{2,1,0:T(8,128)S(1)} collective-permute-done((f32[2,72,128]{2,1,0:T(8,128)S(1)}, f32[2,72,128]{2,1,0:T(8,128)S(1)}, u32[]{:S(2)}, u32[]{:S(2)}) %collective-permute-start.7) | collective-permute-done | bytes 73760 | tf_op jit(solution)/shard_map/ppermute | solution.py:329
  50.8 1.9 %collective-permute-start.13 = (f32[8,72,128]{2,1,0:T(8,128)S(1)}, f32[8,72,128]{2,1,0:T(8,128)S(1)}, u32[]{:S(2)}, u32[]{:S(2)}) collective-permute-start(f32[8,72,128]{2,1,0:T(8,128)S(1)} %collective-permute-done.6.refs_8_), channel_id=1, source_target_pairs={{8,0},{16,8},{24,16},{9,1},{17,9},{25,17},{10,2},{18,10},{26,18},{... | collective-permute-start | bytes 884744 | tf_op jit(solution)/shard_map/ppermute | solution.py:401
  52.7 3.7 %collective-permute-start.12 = (f32[8,72,128]{2,1,0:T(8,128)S(1)}, f32[8,72,128]{2,1,0:T(8,128)S(1)}, u32[]{:S(2)}, u32[]{:S(2)}) collective-permute-start(f32[8,72,128]{2,1,0:T(8,128)S(1)} %collective-permute-done.5.refs_9_), channel_id=1, source_target_pairs={{0,8},{8,16},{16,24},{1,9},{9,17},{17,25},{2,10},{10,18},{18,26},{... | collective-permute-start | bytes 884744 | tf_op jit(solution)/shard_map/ppermute | solution.py:400
  56.8 1.2 %collective-permute-start.15 = (f32[3,72,128]{2,1,0:T(8,128)S(1)}, f32[3,72,128]{2,1,0:T(8,128)S(1)}, u32[]{:S(2)}, u32[]{:S(2)}) collective-permute-start(f32[3,72,128]{2,1,0:T(8,128)S(1)} %collective-permute-done.11.refs_7_), channel_id=1, source_target_pairs={{1,0},{0,1},{3,2},{2,3},{5,4},{4,5},{7,6},{6,7},{9,8},{8,9},{11,10... | collective-permute-start | bytes 331784 | tf_op jit(solution)/shard_map/ppermute | solution.py:329
  58.0 3.6 %collective-permute-done.14.refs_14_ = f32[3,72,128]{2,1,0:T(8,128)S(1)} collective-permute-done((f32[3,72,128]{2,1,0:T(8,128)S(1)}, f32[3,72,128]{2,1,0:T(8,128)S(1)}, u32[]{:S(2)}, u32[]{:S(2)}) %collective-permute-start.14) | collective-permute-done | bytes 110624 | tf_op jit(solution)/shard_map/ppermute | solution.py:329
  61.6 1.3 %collective-permute-done.15.refs_15_ = f32[3,72,128]{2,1,0:T(8,128)S(1)} collective-permute-done((f32[3,72,128]{2,1,0:T(8,128)S(1)}, f32[3,72,128]{2,1,0:T(8,128)S(1)}, u32[]{:S(2)}, u32[]{:S(2)}) %collective-permute-start.15) | collective-permute-done | bytes 110624 | tf_op jit(solution)/shard_map/ppermute | solution.py:329
  63.6 0.7 copy-done.13
  64.3 23.9 %finish.1 = (f32[68,32,128]{2,1,0:T(8,128)}, f32[68,32,128]{2,1,0:T(8,128)}, f32[68,32,128]{2,1,0:T(8,128)}) custom-call(s32[2]{0:T(128)} %pad_add_fusion.place_ref, bf16[480,896]{1,0:T(8,128)(2,1)} %copy-done.1, f32[8,72,128]{2,1,0:T(8,128)} %copy-done.2, f32[8,72,128]{2,1,0:T(8,128)} %copy-done.3, f32[2,72,128]{2,1,0:T(8,128)} %copy-done.7, ...), custom_call_target="tpu_custom_call" | custom-call | tf_op jit(solution)/shard_map/finish/pallas_call | solution.py:30
  (59 shorter events, 2.8 us)
Async XLA Ops:
  0.6 17.6 %copy-start = (f32[136,136]{1,0:T(8,128)S(1)}, f32[136,136]{1,0:T(8,128)}, u32[]{:S(2)}) copy-start(f32[136,136]{1,0:T(8,128)} %param.10) | copy-start | bytes 221956
  0.6 17.6 %copy-start.14 = (f32[136,136]{1,0:T(8,128)S(1)}, f32[136,136]{1,0:T(8,128)}, u32[]{:S(2)}) copy-start(f32[136,136]{1,0:T(8,128)} %param.9) | copy-start | bytes 221956
  4.3 16.4 %copy-start.6 = (f32[16,72,128]{2,1,0:T(8,128)}, f32[16,72,128]{2,1,0:T(8,128)S(1)}, u32[]{:S(2)}) copy-start(f32[16,72,128]{2,1,0:T(8,128)S(1)} %get-tuple-element.46.refs_3_) | copy-start | bytes 1769476
  4.3 17.6 %collective-permute-start.4 = (f32[16,72,128]{2,1,0:T(8,128)S(1)}, f32[16,72,128]{2,1,0:T(8,128)S(1)}, u32[]{:S(2)}, u32[]{:S(2)}) collective-permute-start(f32[16,72,128]{2,1,0:T(8,128)S(1)} %get-tuple-element.46.refs_3_), channel_id=1, source_target_pairs={{1,0},{0,1},{3,2},{2,3},{5,4},{4,5},{7,6},{6,7},{9,8},{8,9},{11,10... | collective-permute-start | bytes 1769480 | tf_op jit(solution)/shard_map/ppermute | solution.py:329
  6.4 15.2 %collective-permute-start.3 = (f32[68,128]{1,0:T(8,128)S(1)}, f32[68,128]{1,0:T(8,128)S(1)}, u32[]{:S(2)}, u32[]{:S(2)}) collective-permute-start(f32[68,128]{1,0:T(8,128)S(1)} %get-tuple-element.30), channel_id=1, source_target_pairs={{2,0},{4,2},{6,4},{3,1},{5,3},{7,5},{10,8},{12,10},{14,12},{11,9},... | collective-permute-start | bytes 104456 | tf_op jit(solution)/shard_map/ppermute | solution.py:352
  7.7 13.9 %collective-permute-start.2 = (f32[68,128]{1,0:T(8,128)S(1)}, f32[68,128]{1,0:T(8,128)S(1)}, u32[]{:S(2)}, u32[]{:S(2)}) collective-permute-start(f32[68,128]{1,0:T(8,128)S(1)} %get-tuple-element.30), channel_id=1, source_target_pairs={{0,2},{2,4},{4,6},{1,3},{3,5},{5,7},{8,10},{10,12},{12,14},{9,11},... | collective-permute-start | bytes 104456 | tf_op jit(solution)/shard_map/ppermute | solution.py:351
  11.7 9.9 %collective-permute-start = (f32[2,68,128]{2,1,0:T(8,128)S(1)}, f32[2,68,128]{2,1,0:T(8,128)S(1)}, u32[]{:S(2)}, u32[]{:S(2)}) collective-permute-start(f32[2,68,128]{2,1,0:T(8,128)S(1)} %get-tuple-element.28), channel_id=1, source_target_pairs={{0,8},{8,16},{16,24},{1,9},{9,17},{17,25},{2,10},{10,18},{18,26},{... | collective-permute-start | bytes 208904 | tf_op jit(solution)/shard_map/ppermute | solution.py:349
  16.2 5.7 %collective-permute-start.1 = (f32[2,68,128]{2,1,0:T(8,128)S(1)}, f32[2,68,128]{2,1,0:T(8,128)S(1)}, u32[]{:S(2)}, u32[]{:S(2)}) collective-permute-start(f32[2,68,128]{2,1,0:T(8,128)S(1)} %get-tuple-element.29), channel_id=1, source_target_pairs={{8,0},{16,8},{24,16},{9,1},{17,9},{25,17},{10,2},{18,10},{26,18},{... | collective-permute-start | bytes 208904 | tf_op jit(solution)/shard_map/ppermute | solution.py:350
  29.8 33.1 %copy-start.2 = (f32[8,72,128]{2,1,0:T(8,128)}, f32[8,72,128]{2,1,0:T(8,128)S(1)}, u32[]{:S(2)}) copy-start(f32[8,72,128]{2,1,0:T(8,128)S(1)} %get-tuple-element.43.low_ref.refs_0_) | copy-start | bytes 884740
  29.8 33.1 %copy-start.3 = (f32[8,72,128]{2,1,0:T(8,128)}, f32[8,72,128]{2,1,0:T(8,128)S(1)}, u32[]{:S(2)}) copy-start(f32[8,72,128]{2,1,0:T(8,128)S(1)} %get-tuple-element.44.high_ref.refs_1_) | copy-start | bytes 884740
  29.8 33.1 %copy-start.7 = (f32[2,72,128]{2,1,0:T(8,128)}, f32[2,72,128]{2,1,0:T(8,128)S(1)}, u32[]{:S(2)}) copy-start(f32[2,72,128]{2,1,0:T(8,128)S(1)} %get-tuple-element.45.pack_ref.refs_2_) | copy-start | bytes 221188
  29.8 7.0 %collective-permute-start.8 = (f32[8,72,128]{2,1,0:T(8,128)S(1)}, f32[8,72,128]{2,1,0:T(8,128)S(1)}, u32[]{:S(2)}, u32[]{:S(2)}) collective-permute-start(f32[8,72,128]{2,1,0:T(8,128)S(1)} %get-tuple-element.44.high_ref.refs_1_), channel_id=1, source_target_pairs={{0,8},{8,16},{16,24},{1,9},{9,17},{17,25},{2,10},{10,18},{18,26},{... | collective-permute-start | bytes 884744 | tf_op jit(solution)/shard_map/ppermute | solution.py:385
  33.2 8.3 %collective-permute-start.9 = (f32[8,72,128]{2,1,0:T(8,128)S(1)}, f32[8,72,128]{2,1,0:T(8,128)S(1)}, u32[]{:S(2)}, u32[]{:S(2)}) collective-permute-start(f32[8,72,128]{2,1,0:T(8,128)S(1)} %get-tuple-element.43.low_ref.refs_0_), channel_id=1, source_target_pairs={{8,0},{16,8},{24,16},{9,1},{17,9},{25,17},{10,2},{18,10},{26,18},{... | collective-permute-start | bytes 884744 | tf_op jit(solution)/shard_map/ppermute | solution.py:386
  35.1 15.6 %collective-permute-start.5 = (f32[8,72,128]{2,1,0:T(8,128)S(1)}, f32[8,72,128]{2,1,0:T(8,128)S(1)}, u32[]{:S(2)}, u32[]{:S(2)}) collective-permute-start(f32[8,72,128]{2,1,0:T(8,128)S(1)} %get-tuple-element.44.high_ref.refs_1_), channel_id=1, source_target_pairs={{1,0},{0,1},{3,2},{2,3},{5,4},{4,5},{7,6},{6,7},{9,8},{8,9},{11,10... | collective-permute-start | bytes 884744 | tf_op jit(solution)/shard_map/ppermute | solution.py:329
  35.5 15.3 %collective-permute-start.6 = (f32[8,72,128]{2,1,0:T(8,128)S(1)}, f32[8,72,128]{2,1,0:T(8,128)S(1)}, u32[]{:S(2)}, u32[]{:S(2)}) collective-permute-start(f32[8,72,128]{2,1,0:T(8,128)S(1)} %get-tuple-element.43.low_ref.refs_0_), channel_id=1, source_target_pairs={{1,0},{0,1},{3,2},{2,3},{5,4},{4,5},{7,6},{6,7},{9,8},{8,9},{11,10... | collective-permute-start | bytes 884744 | tf_op jit(solution)/shard_map/ppermute | solution.py:329
  36.9 26.0 %copy-start.4 = (f32[8,72,128]{2,1,0:T(8,128)}, f32[8,72,128]{2,1,0:T(8,128)S(1)}, u32[]{:S(2)}) copy-start(f32[8,72,128]{2,1,0:T(8,128)S(1)} %collective-permute-done.8.below_ref.refs_4_) | copy-start | bytes 884740
  41.6 21.4 %copy-start.5 = (f32[8,72,128]{2,1,0:T(8,128)}, f32[8,72,128]{2,1,0:T(8,128)S(1)}, u32[]{:S(2)}) copy-start(f32[8,72,128]{2,1,0:T(8,128)S(1)} %collective-permute-done.9.above_ref.refs_5_) | copy-start | bytes 884740
  42.0 8.8 %collective-permute-start.10 = (f32[3,72,128]{2,1,0:T(8,128)S(1)}, f32[3,72,128]{2,1,0:T(8,128)S(1)}, u32[]{:S(2)}, u32[]{:S(2)}) collective-permute-start(f32[3,72,128]{2,1,0:T(8,128)S(1)} %get-tuple-element.41), channel_id=1, source_target_pairs={{0,2},{2,4},{4,6},{1,3},{3,5},{5,7},{8,10},{10,12},{12,14},{9,11},... | collective-permute-start | bytes 331784 | tf_op jit(solution)/shard_map/ppermute | solution.py:397
  45.2 5.6 %collective-permute-start.11 = (f32[3,72,128]{2,1,0:T(8,128)S(1)}, f32[3,72,128]{2,1,0:T(8,128)S(1)}, u32[]{:S(2)}, u32[]{:S(2)}) collective-permute-start(f32[3,72,128]{2,1,0:T(8,128)S(1)} %get-tuple-element.42), channel_id=1, source_target_pairs={{2,0},{4,2},{6,4},{3,1},{5,3},{7,5},{10,8},{12,10},{14,12},{11,9},... | collective-permute-start | bytes 331784 | tf_op jit(solution)/shard_map/ppermute | solution.py:398
  46.5 4.2 %collective-permute-start.7 = (f32[2,72,128]{2,1,0:T(8,128)S(1)}, f32[2,72,128]{2,1,0:T(8,128)S(1)}, u32[]{:S(2)}, u32[]{:S(2)}) collective-permute-start(f32[2,72,128]{2,1,0:T(8,128)S(1)} %get-tuple-element.45.pack_ref.refs_2_), channel_id=1, source_target_pairs={{1,0},{0,1},{3,2},{2,3},{5,4},{4,5},{7,6},{6,7},{9,8},{8,9},{11,10... | collective-permute-start | bytes 221192 | tf_op jit(solution)/shard_map/ppermute | solution.py:329
  50.8 12.1 %collective-permute-start.13 = (f32[8,72,128]{2,1,0:T(8,128)S(1)}, f32[8,72,128]{2,1,0:T(8,128)S(1)}, u32[]{:S(2)}, u32[]{:S(2)}) collective-permute-start(f32[8,72,128]{2,1,0:T(8,128)S(1)} %collective-permute-done.6.refs_8_), channel_id=1, source_target_pairs={{8,0},{16,8},{24,16},{9,1},{17,9},{25,17},{10,2},{18,10},{26,18},{... | collective-permute-start | bytes 884744 | tf_op jit(solution)/shard_map/ppermute | solution.py:401
  52.7 10.1 %collective-permute-start.12 = (f32[8,72,128]{2,1,0:T(8,128)S(1)}, f32[8,72,128]{2,1,0:T(8,128)S(1)}, u32[]{:S(2)}, u32[]{:S(2)}) collective-permute-start(f32[8,72,128]{2,1,0:T(8,128)S(1)} %collective-permute-done.5.refs_9_), channel_id=1, source_target_pairs={{0,8},{8,16},{16,24},{1,9},{9,17},{17,25},{2,10},{10,18},{18,26},{... | collective-permute-start | bytes 884744 | tf_op jit(solution)/shard_map/ppermute | solution.py:400
  56.5 5.1 %collective-permute-start.14 = (f32[3,72,128]{2,1,0:T(8,128)S(1)}, f32[3,72,128]{2,1,0:T(8,128)S(1)}, u32[]{:S(2)}, u32[]{:S(2)}) collective-permute-start(f32[3,72,128]{2,1,0:T(8,128)S(1)} %collective-permute-done.10.refs_6_), channel_id=1, source_target_pairs={{1,0},{0,1},{3,2},{2,3},{5,4},{4,5},{7,6},{6,7},{9,8},{8,9},{11,10... | collective-permute-start | bytes 331784 | tf_op jit(solution)/shard_map/ppermute | solution.py:329
  56.8 6.1 %collective-permute-start.15 = (f32[3,72,128]{2,1,0:T(8,128)S(1)}, f32[3,72,128]{2,1,0:T(8,128)S(1)}, u32[]{:S(2)}, u32[]{:S(2)}) collective-permute-start(f32[3,72,128]{2,1,0:T(8,128)S(1)} %collective-permute-done.11.refs_7_), channel_id=1, source_target_pairs={{1,0},{0,1},{3,2},{2,3},{5,4},{4,5},{7,6},{6,7},{9,8},{8,9},{11,10... | collective-permute-start | bytes 331784 | tf_op jit(solution)/shard_map/ppermute | solution.py:329
  (12 other events, 88.0 us)

commit v4 on v3

--- a/solution.py
+++ b/solution.py
@@ -17,26 +17,24 @@
 F32 = jnp.float32
 BF16 = jnp.bfloat16
 
-
 def up_to(n, k):
     return (n + k - 1) // k * k
 
-
 def lanes_of():
     return lax.broadcasted_iota(jnp.int32, (1, LANES), 1)
 
-
-def call(body, outs, *args, specs=None, out_specs=None, scratch=(), vmem=48 << 20, name):
+def call(body, outs, *args, specs=None, out_specs=None, scratch=(), alias=None, vmem=12 << 20, name):
     return pl.pallas_call(
         body,
         out_shape=outs,
         in_specs=specs or [VMEM] * len(args),
         out_specs=out_specs or jax.tree.map(lambda _: VMEM, outs),
         scratch_shapes=list(scratch),
+        input_output_aliases=alias or {},
+        cost_estimate=pl.CostEstimate(flops=1, transcendentals=0, bytes_accessed=1),
         compiler_params=pltpu.CompilerParams(vmem_limit_bytes=vmem),
         name=name,
     )(*args)
-
 
 def start_rows(src_ref, dst_ref, sems, rows):
     copies = {x: pltpu.make_async_copy(src_ref.at[:, x, :], dst_ref.at[x], sems.at[x]) for x in rows}
@@ -44,7 +42,6 @@
         copy.start()
     return copies
 
-
 def north_step(main, side):
     lane = lanes_of()
     one = pltpu.roll(jnp.where(lane < 1, side, main), LANES - 1, 1) - pltpu.roll(
@@ -55,18 +52,15 @@
     )
     return 8.0 * one - two
 
-
 def source_row(x, at, v, h, side):
     dx = 8.0 * (at(x + 1) - at(x - 1)) - (at(x + 2) - at(x - 2))
     return h - (dx + north_step(v, side)) * (1.0 / 12.0)
-
 
 def put_padded(ref, i, value):
     levels, pad = value.shape[0], ref.shape[1] - value.shape[0]
     ref[i, :levels] = value
     if pad:
         ref[i, levels:] = jnp.zeros((pad, LANES), F32)
-
 
 def inner_rows(u_ref, v_ref, h_ref, lo_ref, hi_ref, cols_ref, mid_ref, u_rows, v_rows, h_rows, sems, edge_sems):
     rows = u_ref.shape[1]
@@ -94,39 +88,70 @@
     for copy in edges:
         copy.wait()
 
-
-def outer_rows(
-    u_ref, v_ref, h_ref, ulo_ref, uhi_ref, vl_ref, vr_ref, low_ref, high_ref, pack_ref, u_rows, v_rows, h_rows, sems
-):
-    rows = u_ref.shape[1]
+def outer_rows(u_ref, v_ref, h_ref, mid_ref, low_ref, high_ref, pack_ref, u_rows, v_rows, h_rows, sems):
+    rows, levels, _ = u_rows.shape
     lane = lanes_of()
-    loads = [start_rows(ref, to, sems.at[i], range(rows)) for i, (ref, to) in enumerate(((u_ref, u_rows), (v_ref, v_rows), (h_ref, h_rows)))]
-    vside = jnp.where(lane % 4 < 2, vl_ref[...], vr_ref[...])
+    ends = [*range(HALO), *range(rows - HALO, rows)]
+    wide = [*range(HALO + 2), *range(rows - HALO - 2, rows)]
+    loads = [
+        *start_rows(v_ref, v_rows, sems.at[1], ends).values(),
+        *start_rows(u_ref, u_rows, sems.at[0], wide).values(),
+        *start_rows(h_ref, h_rows, sems.at[2], ends).values(),
+    ]
+    for m in range(pack_ref.shape[0]):
+        packed = pltpu.roll(mid_ref[8 * m], 8, 1)
+        for k in range(1, 8):
+            packed = jnp.where(lane // 16 == k, pltpu.roll(mid_ref[8 * m + k], (16 * k + 8) % LANES, 1), packed)
+        pack_ref[m] = packed
+    for copy in loads:
+        copy.wait()
 
     def at(x):
-        if x < 0:
-            return ulo_ref[2 + x]
-        if x >= rows:
-            return uhi_ref[x - rows]
-        return u_rows[x]
-
-    for some in loads:
-        for copy in some.values():
-            copy.wait()
-    packed = None
-    for x in range(rows):
-        side = pltpu.roll(vside, (LANES - 4 * x - 2) % LANES, 1)
-        s = source_row(x, at, v_rows[x], h_rows[x], side)
-        m, k = divmod(x, 8)
+        return u_rows[x] if 0 <= x < rows else jnp.zeros((levels, LANES), F32)
+
+    for x in ends:
+        s = source_row(x, at, v_rows[x], h_rows[x], v_rows[x])
         if x < HALO:
             put_padded(low_ref, x, s)
-        elif x >= rows - HALO:
+        else:
             put_padded(high_ref, x - rows + HALO, s)
-        else:
-            rolled = pltpu.roll(s, (16 * k + 8) % LANES, 1)
-            packed = rolled if k == 0 else jnp.where(lane // 16 == k, rolled, packed)
-            if k == 7:
-                put_padded(pack_ref, m - 1, packed)
+
+def column_terms(own_ref, left_ref, right_ref):
+    slot = lanes_of() % 4
+    d = jnp.where(slot < 2, left_ref[...], right_ref[...]) - own_ref[...]
+    far = jnp.where(slot < 2, pltpu.roll(d, LANES - 2, 1), -pltpu.roll(d, 2, 1))
+    near = jnp.where(slot == 1, -pltpu.roll(d, LANES - 1, 1), jnp.where(slot == 2, pltpu.roll(d, 1, 1), 0.0))
+    return (far + 8.0 * near) * (1.0 / 12.0)
+
+def outer_fix(low_in, high_in, pack_in, own_ref, ulo_ref, uhi_ref, vl_ref, vr_ref, low_ref, high_ref, pack_ref, edge_ref):
+    levels = own_ref.shape[0]
+    lane = lanes_of()
+    rows = LANES // 4
+    terms = column_terms(own_ref, vl_ref, vr_ref)
+    edge = (lane < 2) | (lane >= LANES - 2)
+    below = {0: 8.0 * ulo_ref[1] - ulo_ref[0], 1: -ulo_ref[1]}
+    above = {HALO - 1: uhi_ref[1] - 8.0 * uhi_ref[0], HALO - 2: uhi_ref[0]}
+    for ref_in, ref, x0, at, more in (
+        (high_in, high_ref, rows - HALO, HALO, above),
+        (low_in, low_ref, 0, 0, below),
+    ):
+        for i in range(HALO):
+            add = jnp.where(edge, pltpu.roll(terms, (LANES - 4 * (x0 + i) - 2) % LANES, 1), 0.0)
+            if i in more:
+                add = add + more[i] * (1.0 / 12.0)
+            value = ref_in[i, :levels] + add
+            put_padded(ref, i, value)
+            put_padded(edge_ref, at + i, value)
+    slot = lane % 16
+    for m in range(pack_ref.shape[0]):
+        add = jnp.zeros((levels, LANES), F32)
+        for k in range(8):
+            x = HALO + 8 * m + k
+            here = (lane // 16 == k) & (slot >= 6) & (slot < 10)
+            add = jnp.where(here, pltpu.roll(terms, (16 * k + 6 - 4 * x) % LANES, 1), add)
+        value = pack_in[m, :levels] + add
+        put_padded(pack_ref, m, value)
+        put_padded(edge_ref, 2 * HALO + m, value)
 
 
 def column_messages(low_ref, high_ref, pack_ref, below_ref, above_ref, right_ref, left_ref):
@@ -146,7 +171,6 @@
         even, odd = packs[2 * i], packs[2 * i + 1]
         right_ref[i] = jnp.where(slot < 8, even, pltpu.roll(odd, 8, 1))
         left_ref[i] = jnp.where(slot < 8, pltpu.roll(even, LANES - 8, 1), odd)
-
 
 def weights(levels_ref, modes_ref, coef_ref, out_ref):
     groups, _, kp = modes_ref.shape
@@ -164,79 +188,109 @@
                 out_ref[pl.ds((3 * g + i) * kp, kp), at] = part
         scaled = scaled * ratio
 
-
-PARTS = 8
-
-
-def finish(place_ref, w_ref, *refs, groups, limits):
-    ins, refs = refs[: PARTS * groups], refs[PARTS * groups :]
-    u_ref, v_ref, east_ref, north_ref, height_ref, s_ref, z_ref, t_ref, ga_ref, gb_ref, u_rows, v_rows, h_rows, sems = refs
+def parts(value, kp):
+    if kp > value.shape[0]:
+        value = jnp.concatenate([value, jnp.zeros((kp - value.shape[0], LANES), F32)], axis=0)
+    high = value.astype(BF16)
+    low = (value - high.astype(F32)).astype(BF16)
+    return high, low, high
+
+def stage_block(s_ref, m, g, kp, ref, fix=None):
+    lane = lanes_of()
+    outer = (lane < HALO) | (lane >= LANES - HALO)
+
+    def stage(k, _):
+        value = ref[k]
+        if fix is not None:
+            value = jnp.where(outer, pltpu.roll(fix, LANES - 16 * k - 8, 1), value)
+        at = pl.ds(pl.multiple_of(k * LANES, LANES), LANES)
+        for i, part in enumerate(parts(value, kp)):
+            s_ref[m, pl.ds((3 * g + i) * kp, kp), at] = part
+        return _
+
+    lax.fori_loop(0, 8, stage, 0, unroll=4)
+
+def stage_sides(z_ref, g, kp, left_ref, right_ref):
+    slot = lanes_of() % 16
+    for m in range(z_ref.shape[1] // LANES):
+        zl, zr = left_ref[m // 2], right_ref[m // 2]
+        if m % 2 == 0:
+            side = jnp.where(slot < 8, zl, pltpu.roll(zr, 8, 1))
+        else:
+            side = jnp.where(slot < 8, pltpu.roll(zl, LANES - 8, 1), zr)
+        for i, part in enumerate(parts(side, kp)):
+            z_ref[pl.ds((3 * g + i) * kp, kp), m * LANES : (m + 1) * LANES] = part
+
+def mix(operand, w_ref):
+    return lax.dot_general(operand, w_ref[...], (((0,), (0,)), ((), ())), preferred_element_type=F32)
+
+def put(t_ref, g_ref, x, col, part, add):
+    at = pl.ds(col, part.shape[0])
+    for j in range(TERMS):
+        value = part[:, j * LANES : (j + 1) * LANES]
+        if j == SWEEPS:
+            at = pl.ds(col + 8, part.shape[0])
+            g_ref[x, at] = g_ref[x, at] + value if add else value
+        else:
+            t_ref[j, x, at] = t_ref[j, x, at] + value if add else value
+
+def put_blocks(t_ref, g_ref, s_ref, w_ref, row_of_block, add):
+    def block(m, _):
+        part = mix(s_ref[m], w_ref)
+        for k in range(8):
+            put(t_ref, g_ref, row_of_block(m) + k, HALO, part[k * LANES : (k + 1) * LANES], add)
+        return _
+
+    lax.fori_loop(0, s_ref.shape[0], block, 0)
+
+def put_sides(t_ref, g_ref, z_ref, w_ref, add):
+    part = mix(z_ref[...], w_ref)
+    for x in range(g_ref.shape[0]):
+        put(t_ref, g_ref, x, 0, part[16 * x : 16 * x + 8], add)
+        put(t_ref, g_ref, x, HALO + LANES, part[16 * x + 8 : 16 * x + 16], add)
+
+
+def mix_inner(w_ref, *refs, groups):
+    ins, (below, above, zl, zr, t_ref, g_ref, s_ref, r_ref, z_ref) = refs[: 2 * groups], refs[2 * groups :]
+    span, wide, _ = g_ref.shape
+    kp = r_ref.shape[1] // 3
+    w_own = w_ref.at[pl.ds(0, 3 * kp)]
+    g_ref[:, :8] = jnp.zeros((span, 8, LANES), F32)
+    g_ref[:, wide - 8 :] = jnp.zeros((span, 8, LANES), F32)
+    stage_block(r_ref, 0, 0, kp, below)
+    stage_block(r_ref, 1, 0, kp, above)
+    stage_sides(z_ref, 0, kp, zl, zr)
+    put_blocks(t_ref, g_ref, r_ref, w_own, lambda m: m * (span - HALO), False)
+    put_sides(t_ref, g_ref, z_ref, w_own, False)
+    for g in range(groups):
+        edge, mid = ins[2 * g : 2 * g + 2]
+        inner = mid.shape[0] // 8
+        stage_block(s_ref, 0, g, kp, edge.at[pl.ds(0, HALO)])
+        for i in range(inner):
+            stage_block(s_ref, 1 + i, g, kp, mid.at[pl.ds(8 * i, 8)], edge[2 * HALO + i])
+        stage_block(s_ref, 1 + inner, g, kp, edge.at[pl.ds(HALO, HALO)])
+    put_blocks(t_ref, g_ref, s_ref, w_ref, lambda m: HALO + 8 * m, False)
+
+
+def finish(place_ref, w_ref, *refs, others, limits):
+    ins, refs = refs[: 4 * others], refs[4 * others :]
+    _, _, u_ref, v_ref, t_ref, ga_ref, east_ref, north_ref, height_ref, s_ref, z_ref, gb_ref, u_rows, v_rows, h_rows, sems = refs
     span, wide, _ = ga_ref.shape
     rows = span - 2 * HALO
-    blocks = span // 8
     loads = [*start_rows(u_ref, u_rows, sems.at[0], range(rows)).values()]
     loads += start_rows(v_ref, v_rows, sems.at[1], range(rows)).values()
-    lane = lanes_of()
-    slot = lane % 16
-    outer = (lane < HALO) | (lane >= LANES - HALO)
-    kp = w_ref.shape[0] // (3 * groups)
-
-    for g_ref in (ga_ref, gb_ref):
-        g_ref[:, :8] = jnp.zeros((span, 8, LANES), F32)
-        g_ref[:, wide - 8 :] = jnp.zeros((span, 8, LANES), F32)
-
-    def parts(value):
-        lp = value.shape[0]
-        if kp > lp:
-            value = jnp.concatenate([value, jnp.zeros((kp - lp, LANES), F32)], axis=0)
-        high = value.astype(BF16)
-        low = (value - high.astype(F32)).astype(BF16)
-        return high, low, high
-
-    for g in range(groups):
-        low, high, pack, mid, below, above, left_ref, right_ref = ins[PARTS * g : PARTS * (g + 1)]
-        sources = [below, low] + [mid.at[pl.ds(8 * i, 8)] for i in range(blocks - 4)] + [high, above]
-        for m in range(blocks):
-            fix = pack[m - 2] if 2 <= m < blocks - 2 else None
-
-            def stage(k, _, ref=sources[m], fix=fix, m=m, g=g):
-                value = ref[k]
-                if fix is not None:
-                    value = jnp.where(outer, pltpu.roll(fix, LANES - 16 * k - 8, 1), value)
-                at = pl.ds(pl.multiple_of(k * LANES, LANES), LANES)
-                for i, part in enumerate(parts(value)):
-                    s_ref[m, pl.ds((3 * g + i) * kp, kp), at] = part
-                return _
-
-            lax.fori_loop(0, 8, stage, 0, unroll=4)
-            zl, zr = left_ref[m // 2], right_ref[m // 2]
-            if m % 2 == 0:
-                side = jnp.where(slot < 8, zl, pltpu.roll(zr, 8, 1))
-            else:
-                side = jnp.where(slot < 8, pltpu.roll(zl, LANES - 8, 1), zr)
-            for i, part in enumerate(parts(side)):
-                z_ref[pl.ds((3 * g + i) * kp, kp), m * LANES : (m + 1) * LANES] = part
-
-    def put(x, col, part):
-        n = part.shape[0]
-        for j in range(SWEEPS):
-            t_ref[j, x, pl.ds(col, n)] = part[:, j * LANES : (j + 1) * LANES]
-        ga_ref[x, pl.ds(col + 8, n)] = part[:, SWEEPS * LANES :]
-
-    def mix(operand):
-        return lax.dot_general(operand, w_ref[...], (((0,), (0,)), ((), ())), preferred_element_type=F32)
-
-    def block(m, _):
-        part = mix(s_ref[m])
-        for k in range(8):
-            put(8 * m + k, HALO, part[k * LANES : (k + 1) * LANES])
-        return _
-
-    lax.fori_loop(0, blocks, block, 0)
-    part = mix(z_ref[...])
-    for x in range(span):
-        put(x, 0, part[16 * x : 16 * x + 8])
-        put(x, HALO + LANES, part[16 * x + 8 : 16 * x + 16])
+    gb_ref[:, :8] = jnp.zeros((span, 8, LANES), F32)
+    gb_ref[:, wide - 8 :] = jnp.zeros((span, 8, LANES), F32)
+    k = s_ref.shape[1]
+    for d in range(others):
+        below, above, zl, zr = ins[4 * d : 4 * d + 4]
+        kp = k // (3 * others)
+        stage_block(s_ref, 0, d, kp, below)
+        stage_block(s_ref, 1, d, kp, above)
+        stage_sides(z_ref, d, kp, zl, zr)
+    w_others = w_ref.at[pl.ds(w_ref.shape[0] - k, k)]
+    put_blocks(t_ref, ga_ref, s_ref, w_others, lambda m: m * (span - HALO), True)
+    put_sides(t_ref, ga_ref, z_ref, w_others, True)
 
     first_row = place_ref[0] * rows - HALO
     left = jnp.where(place_ref[1] > 0, 1.0, 0.0)
@@ -298,16 +352,13 @@
         for copy in stores(x):
             copy.wait()
 
-
 def shape(*dims, dtype=F32):
     return jax.ShapeDtypeStruct(dims, dtype)
-
 
 def neighbours(axis):
     peers = lax.axis_size(axis)
     up = [(i, i + 1) for i in range(peers - 1)]
     return up, [(j, i) for i, j in up]
-
 
 def on_device(east_wind, north_wind, height, to_modes, to_levels, mode_coef):
     levels, rows, cols = east_wind.shape
@@ -368,20 +419,36 @@
         name="weights",
     )
     place = jnp.stack([lax.axis_index("gx"), lax.axis_index("gy")]).astype(jnp.int32)
-    halo, w, place, mids = lax.optimization_barrier((halo, w, place, mids))
-
     low, high, pack = call(
         outer_rows,
         (shape(HALO, lp, LANES), shape(HALO, lp, LANES), shape(rows // 8 - 2, lp, LANES)),
         east_wind,
         north_wind,
         height,
-        *halo,
-        specs=[HBM] * 3 + [VMEM] * 4,
+        mid,
+        specs=[HBM] * 3 + [VMEM],
         scratch=(row_block, row_block, row_block, dma((3, rows))),
         name="outer_rows",
     )
-    highs, lows, packs = to_others(high), to_others(low), to_others(pack)
+    halo, w, place, mids, low, high, pack = lax.optimization_barrier((halo, w, place, mids, low, high, pack))
+
+    mids_rows = rows // 8 - 2
+    low, high, pack, edge = call(
+        outer_fix,
+        (
+            shape(HALO, lp, LANES),
+            shape(HALO, lp, LANES),
+            shape(mids_rows, lp, LANES),
+            shape(2 * HALO + mids_rows, lp, LANES),
+        ),
+        low,
+        high,
+        pack,
+        packed,
+        *halo,
+        name="outer_fix",
+    )
+    edges = to_others(edge)
     below = lax.ppermute(high, "gx", x_up)
     above = lax.ppermute(low, "gx", x_down)
     right, left = call(
@@ -396,39 +463,59 @@
     )
     from_left = lax.ppermute(right, "gy", y_up)
     from_right = lax.ppermute(left, "gy", y_down)
-    highs, lows, packs, from_left, from_right = lax.optimization_barrier((highs, lows, packs, from_left, from_right))
-    belows = [below] + [lax.ppermute(h, "gx", x_up) for h in highs[1:]]
-    aboves = [above] + [lax.ppermute(l, "gx", x_down) for l in lows[1:]]
-    from_left, from_right = to_others(from_left), to_others(from_right)
+    edges, zl, zr = lax.optimization_barrier((edges, from_left, from_right))
+    belows = [lax.ppermute(e[HALO : 2 * HALO], "gx", x_up) for e in edges[1:]]
+    aboves = [lax.ppermute(e[:HALO], "gx", x_down) for e in edges[1:]]
+    lefts, rights = to_others(zl), to_others(zr)
+
+    k = 3 * kp
     operands = []
     for d in range(groups):
-        operands += [lows[d], highs[d], packs[d], mids[d], belows[d], aboves[d], from_left[d], from_right[d]]
+        operands += [edges[d], mids[d]]
+    t, g = call(
+        functools.partial(mix_inner, groups=groups),
+        (shape(SWEEPS, span, cols + 16, LANES), shape(span, cols + 32, LANES)),
+        w,
+        *operands,
+        below,
+        above,
+        zl,
+        zr,
+        scratch=(
+            pltpu.VMEM((rows // 8, groups * k, 8 * LANES), BF16),
+            pltpu.VMEM((2, k, 8 * LANES), BF16),
+            pltpu.VMEM((k, span // 8 * LANES), BF16),
+        ),
+        name="mix_inner",
+    )
+    operands = []
+    for d in range(groups - 1):
+        operands += [belows[d], aboves[d], lefts[d + 1], rights[d + 1]]
     out = shape(levels, rows, cols)
-    k = groups * 3 * kp
     return call(
-        functools.partial(finish, groups=groups, limits=limits),
-        (out, out, out),
+        functools.partial(finish, others=groups - 1, limits=limits),
+        (shape(SWEEPS, span, cols + 16, LANES), shape(span, cols + 32, LANES), out, out, out),
         place,
         w,
         *operands,
+        t,
+        g,
         east_wind,
         north_wind,
-        specs=[SMEM] + [VMEM] * (1 + len(operands)) + [HBM] * 2,
-        out_specs=(HBM, HBM, HBM),
+        specs=[SMEM] + [VMEM] * (len(operands) + 3) + [HBM] * 2,
+        out_specs=(VMEM, VMEM, HBM, HBM, HBM),
         scratch=(
-            pltpu.VMEM((span // 8, k, 8 * LANES), BF16),
-            pltpu.VMEM((k, span // 8 * LANES), BF16),
-            pltpu.VMEM((SWEEPS, span, cols + 16, LANES), F32),
-            pltpu.VMEM((span, cols + 32, LANES), F32),
+            pltpu.VMEM((2, (groups - 1) * k, 8 * LANES), BF16),
+            pltpu.VMEM(((groups - 1) * k, span // 8 * LANES), BF16),
             pltpu.VMEM((span, cols + 32, LANES), F32),
             row_block,
             row_block,
             pltpu.VMEM((rows + 4, levels, cols), F32),
             dma((3, rows)),
         ),
-        vmem=56 << 20,
+        alias={2 + len(operands): 0, 3 + len(operands): 1},
         name="finish",
-    )
+    )[2:]
 
 
 def solution(mesh):

time: 88.9 us -> 74.9 us (0.84)
  waiting for transfers between devices: 14 us -> 7.86 us
  Pallas kernels: 37.5 us -> 31.4 us
  local copies, waits for them, and re-layouts: 2.5 us -> 0.2 us
  starting transfers between devices: 32.6 us -> 33.8 us
    ppermute x6 -> x4, waiting for transfers between devices: 8.77 us -> 0.01 us  [to_others(): lax.ppermute(value, 'lev', [((i + d) % groups, i) for i in range(groups)])]
    pallas_call x5 -> x7, Pallas kernels: 37.5 us -> 31.4 us  [call(): pl.pallas_call(body, out_shape=outs, in_specs=specs or [VMEM] * len(args)...]
    ppermute x1, waiting for transfers between devices: 0.01 us -> 3.76 us  [on_device(): from_right = lax.ppermute(left, 'gy', y_down)]
    unnamed x40 -> x6, local copies, waits for them, and re-layouts: 2.36 us -> 0.02 us
    ppermute x2, starting transfers between devices: 5.63 us -> 7.74 us  [the longest x1 5.82 us: on_device(): belows = [lax.ppermute(e[HALO:2 * HALO], 'gx', x_up) for e in edges[1:]]]
    ppermute x1, waiting for transfers between devices: 4.69 us -> 2.76 us  [on_device(): above = lax.ppermute(low, 'gx', x_down)]
    ppermute x6 -> x4, starting transfers between devices: 5.49 us -> 3.96 us  [to_others(): lax.ppermute(value, 'lev', [((i + d) % groups, i) for i in range(groups)])]
  transfers between devices with their start and end apart: 16 -> 14, of which waited for: 6 -> 4; matrix products, arithmetic and copies ran while one was open for 1% -> 0% of each run, Pallas kernels for 2% -> 20%
where the time goes in v4:
time: 74.9 us; the launch traced here: 74.3 us
  starting transfers between devices  33.8 us (45%)
  Pallas kernels  31.4 us (42%)
  waiting for transfers between devices  7.86 us (10%)
  between operations  0.94 us (1%)
    pallas_call x7, Pallas kernels, call(): pl.pallas_call(body, out_shape=outs, in_specs=specs or [VMEM] * len(args)...  31.4 us
    ppermute x1, starting transfers between devices, on_device(): belows = [lax.ppermute(e[HALO:2 * HALO], 'gx', x_up) for e in edges[1:]]  5.82 us
    ppermute x1, starting transfers between devices, on_device(): lax.ppermute(hi, 'gx', x_up)  4.55 us
    ppermute x1, starting transfers between devices, on_device(): lax.ppermute(packed, 'gy', y_up)  3.99 us
    ppermute x4, starting transfers between devices, to_others(): lax.ppermute(value, 'lev', [((i + d) % groups, i) for i in range(groups)])  3.96 us
    ppermute x1, starting transfers between devices, on_device(): below = lax.ppermute(high, 'gx', x_up)  3.92 us
    ppermute x1, waiting for transfers between devices, on_device(): from_right = lax.ppermute(left, 'gy', y_down)  3.76 us
    ppermute x1, starting transfers between devices, on_device(): from_left = lax.ppermute(right, 'gy', y_up)  3.21 us
  transfers between devices with their start and end apart: 14, of which 4 were waited for; matrix products, arithmetic and copies ran while one was open for 0% of the time, Pallas kernels for 20%

profile of v4, /device:TPU:1, one launch (start us, length us, event | category | flops | bytes accessed | tf_op | source)
XLA Modules:
  0.0 74.3 jit_solution(1489113382865471549)
XLA Ops:
  0.7 3.6 %inner_rows.1 = (f32[2,68,128]{2,1,0:T(8,128)S(1)}, f32[2,68,128]{2,1,0:T(8,128)S(1)}, f32[68,128]{1,0:T(8,128)S(1)}, f32[16,72,128]{2,1,0:T(8,128)S(1)}) custom-call(f32[68,32,128]{2,1,0:T(8,128)} %refs_6_.1, f32[68,32,128]{2,1,0:T(8,128)} %refs_7_.1, f32[68,32,128]{2,1,0:T(8,128)} %h_ref.3), custom_call_target="tpu_custom_call" | custom-call | flops 1 | bytes 1 | tf_op jit(solution)/shard_map/inner_rows/pallas_call | solution.py:27
  4.3 2.1 %collective-permute-start.4 = (f32[16,72,128]{2,1,0:T(8,128)S(1)}, f32[16,72,128]{2,1,0:T(8,128)S(1)}, u32[]{:S(2)}, u32[]{:S(2)}) collective-permute-start(f32[16,72,128]{2,1,0:T(8,128)S(1)} %get-tuple-element.62.mid_ref.refs_1_), channel_id=1, source_target_pairs={{1,0},{0,1},{3,2},{2,3},{5,4},{4,5},{7,6},{6,7},{9,8},{8,9},{11,10... | collective-permute-start | bytes 1769480 | tf_op jit(solution)/shard_map/ppermute | solution.py:380
  6.4 1.3 %collective-permute-start.3 = (f32[68,128]{1,0:T(8,128)S(1)}, f32[68,128]{1,0:T(8,128)S(1)}, u32[]{:S(2)}, u32[]{:S(2)}) collective-permute-start(f32[68,128]{1,0:T(8,128)S(1)} %get-tuple-element.38.own_ref), channel_id=1, source_target_pairs={{2,0},{4,2},{6,4},{3,1},{5,3},{7,5},{10,8},{12,10},{14,12},{11,9},... | collective-permute-start | bytes 104456 | tf_op jit(solution)/shard_map/ppermute | solution.py:403
  7.7 4.0 %collective-permute-start.2 = (f32[68,128]{1,0:T(8,128)S(1)}, f32[68,128]{1,0:T(8,128)S(1)}, u32[]{:S(2)}, u32[]{:S(2)}) collective-permute-start(f32[68,128]{1,0:T(8,128)S(1)} %get-tuple-element.38.own_ref), channel_id=1, source_target_pairs={{0,2},{2,4},{4,6},{1,3},{3,5},{5,7},{8,10},{10,12},{12,14},{9,11},... | collective-permute-start | bytes 104456 | tf_op jit(solution)/shard_map/ppermute | solution.py:402
  11.7 4.5 %collective-permute-start = (f32[2,68,128]{2,1,0:T(8,128)S(1)}, f32[2,68,128]{2,1,0:T(8,128)S(1)}, u32[]{:S(2)}, u32[]{:S(2)}) collective-permute-start(f32[2,68,128]{2,1,0:T(8,128)S(1)} %get-tuple-element.36), channel_id=1, source_target_pairs={{0,8},{8,16},{16,24},{1,9},{9,17},{17,25},{2,10},{10,18},{18,26},{... | collective-permute-start | bytes 208904 | tf_op jit(solution)/shard_map/ppermute | solution.py:400
  16.2 1.9 %collective-permute-start.1 = (f32[2,68,128]{2,1,0:T(8,128)S(1)}, f32[2,68,128]{2,1,0:T(8,128)S(1)}, u32[]{:S(2)}, u32[]{:S(2)}) collective-permute-start(f32[2,68,128]{2,1,0:T(8,128)S(1)} %get-tuple-element.37), channel_id=1, source_target_pairs={{8,0},{16,8},{24,16},{9,1},{17,9},{25,17},{10,2},{18,10},{26,18},{... | collective-permute-start | bytes 208904 | tf_op jit(solution)/shard_map/ppermute | solution.py:401
  18.4 3.3 %outer_rows.1 = (f32[8,72,128]{2,1,0:T(8,128)S(1)}, f32[8,72,128]{2,1,0:T(8,128)S(1)}, f32[2,72,128]{2,1,0:T(8,128)S(1)}) custom-call(f32[68,32,128]{2,1,0:T(8,128)} %refs_6_.1, f32[68,32,128]{2,1,0:T(8,128)} %refs_7_.1, f32[68,32,128]{2,1,0:T(8,128)} %h_ref.3, f32[16,72,128]{2,1,0:T(8,128)S(1)} %get-tuple-element.62.mid_ref.refs_1_), custom_call_target="tpu_custom_call" | custom-call | flops 1 | bytes 1 | tf_op jit(solution)/shard_map/outer_rows/pallas_call | solution.py:27
  21.8 1.6 %weights.1.w_ref = bf16[480,896]{1,0:T(8,128)(2,1)S(1)} custom-call(f32[128,136]{1,0:T(8,128)S(1)} %pad.11.levels_ref, f32[2,136,80]{2,1,0:T(8,128)S(1)} %pad_maximum_fusion.modes_ref, f32[1,136]{1,0:T(1,128)S(1)} %bitcast.7), custom_call_target="tpu_custom_call" | custom-call | flops 1 | bytes 1 | tf_op jit(solution)/shard_map/weights/pallas_call | solution.py:27
  23.5 0.4 outer_fix.1
  23.9 0.3 collective-permute-start.5
  24.2 1.9 %collective-permute-start.7 = (f32[8,72,128]{2,1,0:T(8,128)S(1)}, f32[8,72,128]{2,1,0:T(8,128)S(1)}, u32[]{:S(2)}, u32[]{:S(2)}) collective-permute-start(f32[8,72,128]{2,1,0:T(8,128)S(1)} %get-tuple-element.53.low_ref), channel_id=1, source_target_pairs={{8,0},{16,8},{24,16},{9,1},{17,9},{25,17},{10,2},{18,10},{26,18},{... | collective-permute-start | bytes 884744 | tf_op jit(solution)/shard_map/ppermute | solution.py:453
  26.1 3.9 %collective-permute-start.6 = (f32[8,72,128]{2,1,0:T(8,128)S(1)}, f32[8,72,128]{2,1,0:T(8,128)S(1)}, u32[]{:S(2)}, u32[]{:S(2)}) collective-permute-start(f32[8,72,128]{2,1,0:T(8,128)S(1)} %get-tuple-element.54.high_ref), channel_id=1, source_target_pairs={{0,8},{8,16},{16,24},{1,9},{9,17},{17,25},{2,10},{10,18},{18,26},{... | collective-permute-start | bytes 884744 | tf_op jit(solution)/shard_map/ppermute | solution.py:452
  30.0 2.8 %collective-permute-done.7.above_ref.refs_5_ = f32[8,72,128]{2,1,0:T(8,128)S(1)} collective-permute-done((f32[8,72,128]{2,1,0:T(8,128)S(1)}, f32[8,72,128]{2,1,0:T(8,128)S(1)}, u32[]{:S(2)}, u32[]{:S(2)}) %collective-permute-start.7) | collective-permute-done | bytes 294944 | tf_op jit(solution)/shard_map/ppermute | solution.py:453
  32.8 0.9 %collective-permute-done.6.below_ref.refs_4_ = f32[8,72,128]{2,1,0:T(8,128)S(1)} collective-permute-done((f32[8,72,128]{2,1,0:T(8,128)S(1)}, f32[8,72,128]{2,1,0:T(8,128)S(1)}, u32[]{:S(2)}, u32[]{:S(2)}) %collective-permute-start.6) | collective-permute-done | bytes 294944 | tf_op jit(solution)/shard_map/ppermute | solution.py:452
  33.7 0.4 column_messages.1
  34.1 3.2 %collective-permute-start.8 = (f32[3,72,128]{2,1,0:T(8,128)S(1)}, f32[3,72,128]{2,1,0:T(8,128)S(1)}, u32[]{:S(2)}, u32[]{:S(2)}) collective-permute-start(f32[3,72,128]{2,1,0:T(8,128)S(1)} %get-tuple-element.56), channel_id=1, source_target_pairs={{0,2},{2,4},{4,6},{1,3},{3,5},{5,7},{8,10},{10,12},{12,14},{9,11},... | collective-permute-start | bytes 331784 | tf_op jit(solution)/shard_map/ppermute | solution.py:464
  37.3 1.3 %collective-permute-start.9 = (f32[3,72,128]{2,1,0:T(8,128)S(1)}, f32[3,72,128]{2,1,0:T(8,128)S(1)}, u32[]{:S(2)}, u32[]{:S(2)}) collective-permute-start(f32[3,72,128]{2,1,0:T(8,128)S(1)} %get-tuple-element.57), channel_id=1, source_target_pairs={{2,0},{4,2},{6,4},{3,1},{5,3},{7,5},{10,8},{12,10},{14,12},{11,9},... | collective-permute-start | bytes 331784 | tf_op jit(solution)/shard_map/ppermute | solution.py:465
  38.6 0.4 collective-permute-done.8.refs_6_
  39.1 3.8 %collective-permute-done.9.refs_7_ = f32[3,72,128]{2,1,0:T(8,128)S(1)} collective-permute-done((f32[3,72,128]{2,1,0:T(8,128)S(1)}, f32[3,72,128]{2,1,0:T(8,128)S(1)}, u32[]{:S(2)}, u32[]{:S(2)}) %collective-permute-start.9) | collective-permute-done | bytes 110624 | tf_op jit(solution)/shard_map/ppermute | solution.py:465
  42.9 1.9 %collective-permute-start.11 = (f32[8,72,128]{2,1,0:T(8,128)S(1)}, f32[8,72,128]{2,1,0:T(8,128)S(1)}, u32[]{:S(2)}, u32[]{:S(2)}) collective-permute-start(f32[8,72,128]{2,1,0:T(8,128)S(1)} %get-tuple-element.69), channel_id=1, source_target_pairs={{8,0},{16,8},{24,16},{9,1},{17,9},{25,17},{10,2},{18,10},{26,18},{... | collective-permute-start | bytes 884744 | tf_op jit(solution)/shard_map/ppermute | solution.py:468
  44.8 5.8 %collective-permute-start.10 = (f32[8,72,128]{2,1,0:T(8,128)S(1)}, f32[8,72,128]{2,1,0:T(8,128)S(1)}, u32[]{:S(2)}, u32[]{:S(2)}) collective-permute-start(f32[8,72,128]{2,1,0:T(8,128)S(1)} %get-tuple-element.70), channel_id=1, source_target_pairs={{0,8},{8,16},{16,24},{1,9},{9,17},{17,25},{2,10},{10,18},{18,26},{... | collective-permute-start | bytes 884744 | tf_op jit(solution)/shard_map/ppermute | solution.py:467
  50.6 1.3 %collective-permute-start.12 = (f32[3,72,128]{2,1,0:T(8,128)S(1)}, f32[3,72,128]{2,1,0:T(8,128)S(1)}, u32[]{:S(2)}, u32[]{:S(2)}) collective-permute-start(f32[3,72,128]{2,1,0:T(8,128)S(1)} %collective-permute-done.8.refs_6_), channel_id=1, source_target_pairs={{1,0},{0,1},{3,2},{2,3},{5,4},{4,5},{7,6},{6,7},{9,8},{8,9},{11,10... | collective-permute-start | bytes 331784 | tf_op jit(solution)/shard_map/ppermute | solution.py:380
  52.2 9.1 %mix_inner.1 = (f32[6,48,144,128]{3,2,1,0:T(8,128)S(1)}, f32[48,160,128]{2,1,0:T(8,128)S(1)}) custom-call(bf16[480,896]{1,0:T(8,128)(2,1)S(1)} %weights.1.w_ref, f32[18,72,128]{2,1,0:T(8,128)S(1)} %get-tuple-element.61.refs_0_, f32[16,72,128]{2,1,0:T(8,128)S(1)} %get-tuple-element.62.mid_ref.refs_1_, f32[18,72,128]{2,1,0:T(8,128)S(1)} %collective-permute-done.5.refs_2_, ...), custom_call_target="tpu_custom_call" | custom-call | flops 1 | bytes 1 | tf_op jit(solution)/shard_map/mix_inner/pallas_call | solution.py:27
  61.3 13.0 %finish.1 = (f32[6,48,144,128]{3,2,1,0:T(8,128)S(1)}, f32[48,160,128]{2,1,0:T(8,128)S(1)}, f32[68,32,128]{2,1,0:T(8,128)}, f32[68,32,128]{2,1,0:T(8,128)}, f32[68,32,128]{2,1,0:T(8,128)}) custom-call(s32[2]{0:T(128)S(1)} %pad_add_fusion.place_ref, bf16[480,896]{1,0:T(8,128)(2,1)S(1)} %weights.1.w_ref, ...), custom_call_target="tpu_custom_call", output_to_operand_aliasing={{0}: (6, {}), {1}: (7, {})} | custom-call | flops 1 | bytes 1 | tf_op jit(solution)/shard_map/finish/pallas_call | solution.py:27
  (24 shorter events, 0.6 us)
Async XLA Ops:
  0.6 17.5 %copy-start = (f32[136,136]{1,0:T(8,128)S(1)}, f32[136,136]{1,0:T(8,128)}, u32[]{:S(2)}) copy-start(f32[136,136]{1,0:T(8,128)} %param.10) | copy-start | bytes 221956
  0.6 17.6 %copy-start.2 = (f32[136,136]{1,0:T(8,128)S(1)}, f32[136,136]{1,0:T(8,128)}, u32[]{:S(2)}) copy-start(f32[136,136]{1,0:T(8,128)} %param.9) | copy-start | bytes 221956
  4.3 19.2 %collective-permute-start.4 = (f32[16,72,128]{2,1,0:T(8,128)S(1)}, f32[16,72,128]{2,1,0:T(8,128)S(1)}, u32[]{:S(2)}, u32[]{:S(2)}) collective-permute-start(f32[16,72,128]{2,1,0:T(8,128)S(1)} %get-tuple-element.62.mid_ref.refs_1_), channel_id=1, source_target_pairs={{1,0},{0,1},{3,2},{2,3},{5,4},{4,5},{7,6},{6,7},{9,8},{8,9},{11,10... | collective-permute-start | bytes 1769480 | tf_op jit(solution)/shard_map/ppermute | solution.py:380
  6.4 17.1 %collective-permute-start.3 = (f32[68,128]{1,0:T(8,128)S(1)}, f32[68,128]{1,0:T(8,128)S(1)}, u32[]{:S(2)}, u32[]{:S(2)}) collective-permute-start(f32[68,128]{1,0:T(8,128)S(1)} %get-tuple-element.38.own_ref), channel_id=1, source_target_pairs={{2,0},{4,2},{6,4},{3,1},{5,3},{7,5},{10,8},{12,10},{14,12},{11,9},... | collective-permute-start | bytes 104456 | tf_op jit(solution)/shard_map/ppermute | solution.py:403
  7.7 15.8 %collective-permute-start.2 = (f32[68,128]{1,0:T(8,128)S(1)}, f32[68,128]{1,0:T(8,128)S(1)}, u32[]{:S(2)}, u32[]{:S(2)}) collective-permute-start(f32[68,128]{1,0:T(8,128)S(1)} %get-tuple-element.38.own_ref), channel_id=1, source_target_pairs={{0,2},{2,4},{4,6},{1,3},{3,5},{5,7},{8,10},{10,12},{12,14},{9,11},... | collective-permute-start | bytes 104456 | tf_op jit(solution)/shard_map/ppermute | solution.py:402
  11.7 11.8 %collective-permute-start = (f32[2,68,128]{2,1,0:T(8,128)S(1)}, f32[2,68,128]{2,1,0:T(8,128)S(1)}, u32[]{:S(2)}, u32[]{:S(2)}) collective-permute-start(f32[2,68,128]{2,1,0:T(8,128)S(1)} %get-tuple-element.36), channel_id=1, source_target_pairs={{0,8},{8,16},{16,24},{1,9},{9,17},{17,25},{2,10},{10,18},{18,26},{... | collective-permute-start | bytes 208904 | tf_op jit(solution)/shard_map/ppermute | solution.py:400
  16.2 7.2 %collective-permute-start.1 = (f32[2,68,128]{2,1,0:T(8,128)S(1)}, f32[2,68,128]{2,1,0:T(8,128)S(1)}, u32[]{:S(2)}, u32[]{:S(2)}) collective-permute-start(f32[2,68,128]{2,1,0:T(8,128)S(1)} %get-tuple-element.37), channel_id=1, source_target_pairs={{8,0},{16,8},{24,16},{9,1},{17,9},{25,17},{10,2},{18,10},{26,18},{... | collective-permute-start | bytes 208904 | tf_op jit(solution)/shard_map/ppermute | solution.py:401
  18.4 3.3 %copy-start.1 = (f32[136]{0:T(256)S(1)}, f32[136]{0:T(256)}, u32[]{:S(2)}) copy-start(f32[136]{0:T(256)} %param.11) | copy-start | bytes 1636
  23.9 19.0 %collective-permute-start.5 = (f32[18,72,128]{2,1,0:T(8,128)S(1)}, f32[18,72,128]{2,1,0:T(8,128)S(1)}, u32[]{:S(2)}, u32[]{:S(2)}) collective-permute-start(f32[18,72,128]{2,1,0:T(8,128)S(1)} %get-tuple-element.61.refs_0_), channel_id=1, source_target_pairs={{1,0},{0,1},{3,2},{2,3},{5,4},{4,5},{7,6},{6,7},{9,8},{8,9},{11,10... | collective-permute-start | bytes 1990664 | tf_op jit(solution)/shard_map/ppermute | solution.py:380
  24.2 8.6 %collective-permute-start.7 = (f32[8,72,128]{2,1,0:T(8,128)S(1)}, f32[8,72,128]{2,1,0:T(8,128)S(1)}, u32[]{:S(2)}, u32[]{:S(2)}) collective-permute-start(f32[8,72,128]{2,1,0:T(8,128)S(1)} %get-tuple-element.53.low_ref), channel_id=1, source_target_pairs={{8,0},{16,8},{24,16},{9,1},{17,9},{25,17},{10,2},{18,10},{26,18},{... | collective-permute-start | bytes 884744 | tf_op jit(solution)/shard_map/ppermute | solution.py:453
  26.1 7.6 %collective-permute-start.6 = (f32[8,72,128]{2,1,0:T(8,128)S(1)}, f32[8,72,128]{2,1,0:T(8,128)S(1)}, u32[]{:S(2)}, u32[]{:S(2)}) collective-permute-start(f32[8,72,128]{2,1,0:T(8,128)S(1)} %get-tuple-element.54.high_ref), channel_id=1, source_target_pairs={{0,8},{8,16},{16,24},{1,9},{9,17},{17,25},{2,10},{10,18},{18,26},{... | collective-permute-start | bytes 884744 | tf_op jit(solution)/shard_map/ppermute | solution.py:452
  34.1 4.9 %collective-permute-start.8 = (f32[3,72,128]{2,1,0:T(8,128)S(1)}, f32[3,72,128]{2,1,0:T(8,128)S(1)}, u32[]{:S(2)}, u32[]{:S(2)}) collective-permute-start(f32[3,72,128]{2,1,0:T(8,128)S(1)} %get-tuple-element.56), channel_id=1, source_target_pairs={{0,2},{2,4},{4,6},{1,3},{3,5},{5,7},{8,10},{10,12},{12,14},{9,11},... | collective-permute-start | bytes 331784 | tf_op jit(solution)/shard_map/ppermute | solution.py:464
  37.3 5.5 %collective-permute-start.9 = (f32[3,72,128]{2,1,0:T(8,128)S(1)}, f32[3,72,128]{2,1,0:T(8,128)S(1)}, u32[]{:S(2)}, u32[]{:S(2)}) collective-permute-start(f32[3,72,128]{2,1,0:T(8,128)S(1)} %get-tuple-element.57), channel_id=1, source_target_pairs={{2,0},{4,2},{6,4},{3,1},{5,3},{7,5},{10,8},{12,10},{14,12},{11,9},... | collective-permute-start | bytes 331784 | tf_op jit(solution)/shard_map/ppermute | solution.py:465
  42.9 18.4 %collective-permute-start.11 = (f32[8,72,128]{2,1,0:T(8,128)S(1)}, f32[8,72,128]{2,1,0:T(8,128)S(1)}, u32[]{:S(2)}, u32[]{:S(2)}) collective-permute-start(f32[8,72,128]{2,1,0:T(8,128)S(1)} %get-tuple-element.69), channel_id=1, source_target_pairs={{8,0},{16,8},{24,16},{9,1},{17,9},{25,17},{10,2},{18,10},{26,18},{... | collective-permute-start | bytes 884744 | tf_op jit(solution)/shard_map/ppermute | solution.py:468
  44.8 16.5 %collective-permute-start.10 = (f32[8,72,128]{2,1,0:T(8,128)S(1)}, f32[8,72,128]{2,1,0:T(8,128)S(1)}, u32[]{:S(2)}, u32[]{:S(2)}) collective-permute-start(f32[8,72,128]{2,1,0:T(8,128)S(1)} %get-tuple-element.70), channel_id=1, source_target_pairs={{0,8},{8,16},{16,24},{1,9},{9,17},{17,25},{2,10},{10,18},{18,26},{... | collective-permute-start | bytes 884744 | tf_op jit(solution)/shard_map/ppermute | solution.py:467
  50.6 10.7 %collective-permute-start.12 = (f32[3,72,128]{2,1,0:T(8,128)S(1)}, f32[3,72,128]{2,1,0:T(8,128)S(1)}, u32[]{:S(2)}, u32[]{:S(2)}) collective-permute-start(f32[3,72,128]{2,1,0:T(8,128)S(1)} %collective-permute-done.8.refs_6_), channel_id=1, source_target_pairs={{1,0},{0,1},{3,2},{2,3},{5,4},{4,5},{7,6},{6,7},{9,8},{8,9},{11,10... | collective-permute-start | bytes 331784 | tf_op jit(solution)/shard_map/ppermute | solution.py:380
  51.9 9.4 %collective-permute-start.13 = (f32[3,72,128]{2,1,0:T(8,128)S(1)}, f32[3,72,128]{2,1,0:T(8,128)S(1)}, u32[]{:S(2)}, u32[]{:S(2)}) collective-permute-start(f32[3,72,128]{2,1,0:T(8,128)S(1)} %collective-permute-done.9.refs_7_), channel_id=1, source_target_pairs={{1,0},{0,1},{3,2},{2,3},{5,4},{4,5},{7,6},{6,7},{9,8},{8,9},{11,10... | collective-permute-start | bytes 331784 | tf_op jit(solution)/shard_map/ppermute | solution.py:380

commit v5 on v4

--- a/solution.py
+++ b/solution.py
@@ -250,26 +250,35 @@
         put(t_ref, g_ref, x, HALO + LANES, part[16 * x + 8 : 16 * x + 16], add)
 
 
-def mix_inner(w_ref, *refs, groups):
-    ins, (below, above, zl, zr, t_ref, g_ref, s_ref, r_ref, z_ref) = refs[: 2 * groups], refs[2 * groups :]
+def mix_outer(w_ref, low, high, below, above, t_ref, g_ref, s_ref):
     span, wide, _ = g_ref.shape
-    kp = r_ref.shape[1] // 3
-    w_own = w_ref.at[pl.ds(0, 3 * kp)]
+    kp = s_ref.shape[1] // 3
     g_ref[:, :8] = jnp.zeros((span, 8, LANES), F32)
     g_ref[:, wide - 8 :] = jnp.zeros((span, 8, LANES), F32)
-    stage_block(r_ref, 0, 0, kp, below)
-    stage_block(r_ref, 1, 0, kp, above)
+    for m, ref in enumerate((below, low, high, above)):
+        stage_block(s_ref, m, 0, kp, ref)
+    far = span - 4 * HALO
+    put_blocks(t_ref, g_ref, s_ref, w_ref.at[pl.ds(0, 3 * kp)], lambda m: HALO * m + jnp.where(m > 1, far, 0), False)
+
+
+def mix_inner(w_ref, *refs, groups):
+    ins, (zl, zr, _, _, t_ref, g_ref, s_ref, r_ref, z_ref) = refs[: 2 * groups], refs[2 * groups :]
+    span, wide, _ = g_ref.shape
+    k = z_ref.shape[0]
+    kp = k // 3
+    w_own = w_ref.at[pl.ds(0, k)]
+    w_others = w_ref.at[pl.ds(k, k * (groups - 1))]
     stage_sides(z_ref, 0, kp, zl, zr)
-    put_blocks(t_ref, g_ref, r_ref, w_own, lambda m: m * (span - HALO), False)
     put_sides(t_ref, g_ref, z_ref, w_own, False)
     for g in range(groups):
         edge, mid = ins[2 * g : 2 * g + 2]
-        inner = mid.shape[0] // 8
-        stage_block(s_ref, 0, g, kp, edge.at[pl.ds(0, HALO)])
-        for i in range(inner):
-            stage_block(s_ref, 1 + i, g, kp, mid.at[pl.ds(8 * i, 8)], edge[2 * HALO + i])
-        stage_block(s_ref, 1 + inner, g, kp, edge.at[pl.ds(HALO, HALO)])
-    put_blocks(t_ref, g_ref, s_ref, w_ref, lambda m: HALO + 8 * m, False)
+        for i in range(mid.shape[0] // 8):
+            stage_block(s_ref, i, g, kp, mid.at[pl.ds(8 * i, 8)], edge[2 * HALO + i])
+        if g > 0:
+            stage_block(r_ref, 0, g - 1, kp, edge.at[pl.ds(0, HALO)])
+            stage_block(r_ref, 1, g - 1, kp, edge.at[pl.ds(HALO, HALO)])
+    put_blocks(t_ref, g_ref, r_ref, w_others, lambda m: HALO + (span - 3 * HALO) * m, True)
+    put_blocks(t_ref, g_ref, s_ref, w_ref, lambda m: 2 * HALO + 8 * m, False)
 
 
 def finish(place_ref, w_ref, *refs, others, limits):
@@ -430,7 +439,7 @@
         scratch=(row_block, row_block, row_block, dma((3, rows))),
         name="outer_rows",
     )
-    halo, w, place, mids, low, high, pack = lax.optimization_barrier((halo, w, place, mids, low, high, pack))
+    halo, place, mids, low, high, pack = lax.optimization_barrier((halo, place, mids, low, high, pack))
 
     mids_rows = rows // 8 - 2
     low, high, pack, edge = call(
@@ -463,29 +472,43 @@
     )
     from_left = lax.ppermute(right, "gy", y_up)
     from_right = lax.ppermute(left, "gy", y_down)
-    edges, zl, zr = lax.optimization_barrier((edges, from_left, from_right))
+    k = 3 * kp
+    terms = (shape(SWEEPS, span, cols + 16, LANES), shape(span, cols + 32, LANES))
+    t, g = call(
+        mix_outer,
+        terms,
+        w,
+        low,
+        high,
+        below,
+        above,
+        scratch=(pltpu.VMEM((4, k, 8 * LANES), BF16),),
+        name="mix_outer",
+    )
+    edges, zl, zr, t, g = lax.optimization_barrier((edges, from_left, from_right, t, g))
     belows = [lax.ppermute(e[HALO : 2 * HALO], "gx", x_up) for e in edges[1:]]
     aboves = [lax.ppermute(e[:HALO], "gx", x_down) for e in edges[1:]]
     lefts, rights = to_others(zl), to_others(zr)
 
-    k = 3 * kp
     operands = []
     for d in range(groups):
         operands += [edges[d], mids[d]]
+    n = len(operands)
     t, g = call(
         functools.partial(mix_inner, groups=groups),
-        (shape(SWEEPS, span, cols + 16, LANES), shape(span, cols + 32, LANES)),
+        terms,
         w,
         *operands,
-        below,
-        above,
         zl,
         zr,
+        t,
+        g,
         scratch=(
-            pltpu.VMEM((rows // 8, groups * k, 8 * LANES), BF16),
-            pltpu.VMEM((2, k, 8 * LANES), BF16),
+            pltpu.VMEM((rows // 8 - 2, groups * k, 8 * LANES), BF16),
+            pltpu.VMEM((2, (groups - 1) * k, 8 * LANES), BF16),
             pltpu.VMEM((k, span // 8 * LANES), BF16),
         ),
+        alias={n + 3: 0, n + 4: 1},
         name="mix_inner",
     )
     operands = []

time: 74.9 us -> 70.8 us (0.945)
  waiting for transfers between devices: 7.86 us -> 3.81 us
  starting transfers between devices: 33.8 us -> 32.5 us
  Pallas kernels: 31.4 us -> 32.6 us
    ppermute x1, waiting for transfers between devices: 3.76 us -> 0.01 us  [on_device(): from_right = lax.ppermute(left, 'gy', y_down)]
    pallas_call x7 -> x8, Pallas kernels: 31.4 us -> 32.6 us  [call(): pl.pallas_call(body, out_shape=outs, in_specs=specs or [VMEM] * len(args)...]
    ppermute x1, starting transfers between devices: 5.82 us -> 4.79 us  [on_device(): belows = [lax.ppermute(e[HALO:2 * HALO], 'gx', x_up) for e in edges[1:]]]
  transfers between devices with their start and end apart: 14 -> 14, of which waited for: 4 -> 3; matrix products, arithmetic and copies ran while one was open for 0% -> 0% of each run, Pallas kernels for 20% -> 21%
where the time goes in v5:
time: 70.8 us; the launch traced here: 70.1 us
  Pallas kernels  32.6 us (46%)
  starting transfers between devices  32.5 us (46%)
  waiting for transfers between devices  3.81 us (5%)
  between operations  0.94 us (1%)
    pallas_call x8, Pallas kernels, call(): pl.pallas_call(body, out_shape=outs, in_specs=specs or [VMEM] * len(args)...  32.6 us
    ppermute x1, starting transfers between devices, on_device(): belows = [lax.ppermute(e[HALO:2 * HALO], 'gx', x_up) for e in edges[1:]]  4.79 us
    ppermute x1, starting transfers between devices, on_device(): lax.ppermute(hi, 'gx', x_up)  4.55 us
    ppermute x1, starting transfers between devices, on_device(): lax.ppermute(packed, 'gy', y_up)  3.99 us
    ppermute x4, starting transfers between devices, to_others(): lax.ppermute(value, 'lev', [((i + d) % groups, i) for i in range(groups)])  3.96 us
    ppermute x1, starting transfers between devices, on_device(): below = lax.ppermute(high, 'gx', x_up)  3.4 us
    ppermute x1, starting transfers between devices, on_device(): from_left = lax.ppermute(right, 'gy', y_up)  3.21 us
    ppermute x1, waiting for transfers between devices, on_device(): above = lax.ppermute(low, 'gx', x_down)  2.56 us
  transfers between devices with their start and end apart: 14, of which 3 were waited for; matrix products, arithmetic and copies ran while one was open for 0% of the time, Pallas kernels for 21%

profile of v5, /device:TPU:1, one launch (start us, length us, event | category | flops | bytes accessed | tf_op | source)
XLA Modules:
  0.0 70.1 jit_solution(5955927263465088899)
XLA Ops:
  0.7 3.6 %inner_rows.1 = (f32[2,68,128]{2,1,0:T(8,128)S(1)}, f32[2,68,128]{2,1,0:T(8,128)S(1)}, f32[68,128]{1,0:T(8,128)S(1)}, f32[16,72,128]{2,1,0:T(8,128)S(1)}) custom-call(f32[68,32,128]{2,1,0:T(8,128)} %refs_6_.1, f32[68,32,128]{2,1,0:T(8,128)} %refs_7_.1, f32[68,32,128]{2,1,0:T(8,128)} %h_ref.3), custom_call_target="tpu_custom_call" | custom-call | flops 1 | bytes 1 | tf_op jit(solution)/shard_map/inner_rows/pallas_call | solution.py:27
  4.3 2.1 %collective-permute-start.4 = (f32[16,72,128]{2,1,0:T(8,128)S(1)}, f32[16,72,128]{2,1,0:T(8,128)S(1)}, u32[]{:S(2)}, u32[]{:S(2)}) collective-permute-start(f32[16,72,128]{2,1,0:T(8,128)S(1)} %get-tuple-element.66.mid_ref.refs_1_), channel_id=1, source_target_pairs={{1,0},{0,1},{3,2},{2,3},{5,4},{4,5},{7,6},{6,7},{9,8},{8,9},{11,10... | collective-permute-start | bytes 1769480 | tf_op jit(solution)/shard_map/ppermute | solution.py:389
  6.4 1.3 %collective-permute-start.3 = (f32[68,128]{1,0:T(8,128)S(1)}, f32[68,128]{1,0:T(8,128)S(1)}, u32[]{:S(2)}, u32[]{:S(2)}) collective-permute-start(f32[68,128]{1,0:T(8,128)S(1)} %get-tuple-element.41.own_ref), channel_id=1, source_target_pairs={{2,0},{4,2},{6,4},{3,1},{5,3},{7,5},{10,8},{12,10},{14,12},{11,9},... | collective-permute-start | bytes 104456 | tf_op jit(solution)/shard_map/ppermute | solution.py:412
  7.7 4.0 %collective-permute-start.2 = (f32[68,128]{1,0:T(8,128)S(1)}, f32[68,128]{1,0:T(8,128)S(1)}, u32[]{:S(2)}, u32[]{:S(2)}) collective-permute-start(f32[68,128]{1,0:T(8,128)S(1)} %get-tuple-element.41.own_ref), channel_id=1, source_target_pairs={{0,2},{2,4},{4,6},{1,3},{3,5},{5,7},{8,10},{10,12},{12,14},{9,11},... | collective-permute-start | bytes 104456 | tf_op jit(solution)/shard_map/ppermute | solution.py:411
  11.7 4.5 %collective-permute-start = (f32[2,68,128]{2,1,0:T(8,128)S(1)}, f32[2,68,128]{2,1,0:T(8,128)S(1)}, u32[]{:S(2)}, u32[]{:S(2)}) collective-permute-start(f32[2,68,128]{2,1,0:T(8,128)S(1)} %get-tuple-element.39), channel_id=1, source_target_pairs={{0,8},{8,16},{16,24},{1,9},{9,17},{17,25},{2,10},{10,18},{18,26},{... | collective-permute-start | bytes 208904 | tf_op jit(solution)/shard_map/ppermute | solution.py:409
  16.2 1.9 %collective-permute-start.1 = (f32[2,68,128]{2,1,0:T(8,128)S(1)}, f32[2,68,128]{2,1,0:T(8,128)S(1)}, u32[]{:S(2)}, u32[]{:S(2)}) collective-permute-start(f32[2,68,128]{2,1,0:T(8,128)S(1)} %get-tuple-element.40), channel_id=1, source_target_pairs={{8,0},{16,8},{24,16},{9,1},{17,9},{25,17},{10,2},{18,10},{26,18},{... | collective-permute-start | bytes 208904 | tf_op jit(solution)/shard_map/ppermute | solution.py:410
  18.2 3.3 %outer_rows.1 = (f32[8,72,128]{2,1,0:T(8,128)S(1)}, f32[8,72,128]{2,1,0:T(8,128)S(1)}, f32[2,72,128]{2,1,0:T(8,128)S(1)}) custom-call(f32[68,32,128]{2,1,0:T(8,128)} %refs_6_.1, f32[68,32,128]{2,1,0:T(8,128)} %refs_7_.1, f32[68,32,128]{2,1,0:T(8,128)} %h_ref.3, f32[16,72,128]{2,1,0:T(8,128)S(1)} %get-tuple-element.66.mid_ref.refs_1_), custom_call_target="tpu_custom_call" | custom-call | flops 1 | bytes 1 | tf_op jit(solution)/shard_map/outer_rows/pallas_call | solution.py:27
  21.6 0.3 collective-permute-done.1.uhi_ref
  21.9 0.4 outer_fix.1
  22.3 0.3 collective-permute-start.5
  22.6 2.1 %collective-permute-start.7 = (f32[8,72,128]{2,1,0:T(8,128)S(1)}, f32[8,72,128]{2,1,0:T(8,128)S(1)}, u32[]{:S(2)}, u32[]{:S(2)}) collective-permute-start(f32[8,72,128]{2,1,0:T(8,128)S(1)} %get-tuple-element.55.low_ref.low), channel_id=1, source_target_pairs={{8,0},{16,8},{24,16},{9,1},{17,9},{25,17},{10,2},{18,10},{26,18},{... | collective-permute-start | bytes 884744 | tf_op jit(solution)/shard_map/ppermute | solution.py:462
  24.8 3.4 %collective-permute-start.6 = (f32[8,72,128]{2,1,0:T(8,128)S(1)}, f32[8,72,128]{2,1,0:T(8,128)S(1)}, u32[]{:S(2)}, u32[]{:S(2)}) collective-permute-start(f32[8,72,128]{2,1,0:T(8,128)S(1)} %get-tuple-element.56.high_ref.high), channel_id=1, source_target_pairs={{0,8},{8,16},{16,24},{1,9},{9,17},{17,25},{2,10},{10,18},{18,26},{... | collective-permute-start | bytes 884744 | tf_op jit(solution)/shard_map/ppermute | solution.py:461
  28.4 2.6 %collective-permute-done.7.above_ref.above = f32[8,72,128]{2,1,0:T(8,128)S(1)} collective-permute-done((f32[8,72,128]{2,1,0:T(8,128)S(1)}, f32[8,72,128]{2,1,0:T(8,128)S(1)}, u32[]{:S(2)}, u32[]{:S(2)}) %collective-permute-start.7) | collective-permute-done | bytes 294944 | tf_op jit(solution)/shard_map/ppermute | solution.py:462
  30.9 0.9 %collective-permute-done.6.below_ref.below = f32[8,72,128]{2,1,0:T(8,128)S(1)} collective-permute-done((f32[8,72,128]{2,1,0:T(8,128)S(1)}, f32[8,72,128]{2,1,0:T(8,128)S(1)}, u32[]{:S(2)}, u32[]{:S(2)}) %collective-permute-start.6) | collective-permute-done | bytes 294944 | tf_op jit(solution)/shard_map/ppermute | solution.py:461
  31.8 0.4 column_messages.1
  32.3 3.2 %collective-permute-start.8 = (f32[3,72,128]{2,1,0:T(8,128)S(1)}, f32[3,72,128]{2,1,0:T(8,128)S(1)}, u32[]{:S(2)}, u32[]{:S(2)}) collective-permute-start(f32[3,72,128]{2,1,0:T(8,128)S(1)} %get-tuple-element.58), channel_id=1, source_target_pairs={{0,2},{2,4},{4,6},{1,3},{3,5},{5,7},{8,10},{10,12},{12,14},{9,11},... | collective-permute-start | bytes 331784 | tf_op jit(solution)/shard_map/ppermute | solution.py:473
  35.5 1.3 %collective-permute-start.9 = (f32[3,72,128]{2,1,0:T(8,128)S(1)}, f32[3,72,128]{2,1,0:T(8,128)S(1)}, u32[]{:S(2)}, u32[]{:S(2)}) collective-permute-start(f32[3,72,128]{2,1,0:T(8,128)S(1)} %get-tuple-element.59), channel_id=1, source_target_pairs={{2,0},{4,2},{6,4},{3,1},{5,3},{7,5},{10,8},{12,10},{14,12},{11,9},... | collective-permute-start | bytes 331784 | tf_op jit(solution)/shard_map/ppermute | solution.py:474
  36.8 1.6 %weights.1.w_ref = bf16[480,896]{1,0:T(8,128)(2,1)S(1)} custom-call(f32[128,136]{1,0:T(8,128)S(1)} %pad.11.levels_ref, f32[2,136,80]{2,1,0:T(8,128)S(1)} %pad_maximum_fusion.modes_ref, f32[1,136]{1,0:T(1,128)S(1)} %bitcast.7), custom_call_target="tpu_custom_call" | custom-call | flops 1 | bytes 1 | tf_op jit(solution)/shard_map/weights/pallas_call | solution.py:27
  38.5 3.5 %mix_outer.1 = (f32[6,48,144,128]{3,2,1,0:T(8,128)S(1)}, f32[48,160,128]{2,1,0:T(8,128)S(1)}) custom-call(bf16[480,896]{1,0:T(8,128)(2,1)S(1)} %weights.1.w_ref, f32[8,72,128]{2,1,0:T(8,128)S(1)} %get-tuple-element.55.low_ref.low, f32[8,72,128]{2,1,0:T(8,128)S(1)} %get-tuple-element.56.high_ref.high, ...), custom_call_target="tpu_custom_call" | custom-call | flops 1 | bytes 1 | tf_op jit(solution)/shard_map/mix_outer/pallas_call | solution.py:27
  42.1 1.9 %collective-permute-start.11 = (f32[8,72,128]{2,1,0:T(8,128)S(1)}, f32[8,72,128]{2,1,0:T(8,128)S(1)}, u32[]{:S(2)}, u32[]{:S(2)}) collective-permute-start(f32[8,72,128]{2,1,0:T(8,128)S(1)} %get-tuple-element.75), channel_id=1, source_target_pairs={{8,0},{16,8},{24,16},{9,1},{17,9},{25,17},{10,2},{18,10},{26,18},{... | collective-permute-start | bytes 884744 | tf_op jit(solution)/shard_map/ppermute | solution.py:490
  44.0 4.8 %collective-permute-start.10 = (f32[8,72,128]{2,1,0:T(8,128)S(1)}, f32[8,72,128]{2,1,0:T(8,128)S(1)}, u32[]{:S(2)}, u32[]{:S(2)}) collective-permute-start(f32[8,72,128]{2,1,0:T(8,128)S(1)} %get-tuple-element.76), channel_id=1, source_target_pairs={{0,8},{8,16},{16,24},{1,9},{9,17},{17,25},{2,10},{10,18},{18,26},{... | collective-permute-start | bytes 884744 | tf_op jit(solution)/shard_map/ppermute | solution.py:489
  48.8 1.3 %collective-permute-start.12 = (f32[3,72,128]{2,1,0:T(8,128)S(1)}, f32[3,72,128]{2,1,0:T(8,128)S(1)}, u32[]{:S(2)}, u32[]{:S(2)}) collective-permute-start(f32[3,72,128]{2,1,0:T(8,128)S(1)} %collective-permute-done.8.refs_4_), channel_id=1, source_target_pairs={{1,0},{0,1},{3,2},{2,3},{5,4},{4,5},{7,6},{6,7},{9,8},{8,9},{11,10... | collective-permute-start | bytes 331784 | tf_op jit(solution)/shard_map/ppermute | solution.py:389
  50.3 6.1 %mix_inner.1 = (f32[6,48,144,128]{3,2,1,0:T(8,128)S(1)}, f32[48,160,128]{2,1,0:T(8,128)S(1)}) custom-call(bf16[480,896]{1,0:T(8,128)(2,1)S(1)} %weights.1.w_ref, f32[18,72,128]{2,1,0:T(8,128)S(1)} %get-tuple-element.65.refs_0_, f32[16,72,128]{2,1,0:T(8,128)S(1)} %get-tuple-element.66.mid_ref.refs_1_, ...), custom_call_target="tpu_custom_call", output_to_operand_aliasing={{0}: (7, {}), {1}: (8, {})} | custom-call | flops 1 | bytes 1 | tf_op jit(solution)/shard_map/mix_inner/pallas_call | solution.py:27
  56.5 13.6 %finish.1 = (f32[6,48,144,128]{3,2,1,0:T(8,128)S(1)}, f32[48,160,128]{2,1,0:T(8,128)S(1)}, f32[68,32,128]{2,1,0:T(8,128)}, f32[68,32,128]{2,1,0:T(8,128)}, f32[68,32,128]{2,1,0:T(8,128)}) custom-call(s32[2]{0:T(128)S(1)} %pad_add_fusion.place_ref, bf16[480,896]{1,0:T(8,128)(2,1)S(1)} %weights.1.w_ref, ...), custom_call_target="tpu_custom_call", output_to_operand_aliasing={{0}: (6, {}), {1}: (7, {})} | custom-call | flops 1 | bytes 1 | tf_op jit(solution)/shard_map/finish/pallas_call | solution.py:27
  (25 shorter events, 0.6 us)
Async XLA Ops:
  0.6 27.6 %copy-start = (f32[136,136]{1,0:T(8,128)S(1)}, f32[136,136]{1,0:T(8,128)}, u32[]{:S(2)}) copy-start(f32[136,136]{1,0:T(8,128)} %param.10) | copy-start | bytes 221956
  0.6 27.6 %copy-start.2 = (f32[136,136]{1,0:T(8,128)S(1)}, f32[136,136]{1,0:T(8,128)}, u32[]{:S(2)}) copy-start(f32[136,136]{1,0:T(8,128)} %param.9) | copy-start | bytes 221956
  4.3 32.6 %copy-start.1 = (f32[136]{0:T(256)S(1)}, f32[136]{0:T(256)}, u32[]{:S(2)}) copy-start(f32[136]{0:T(256)} %param.11) | copy-start | bytes 1636
  4.3 17.6 %collective-permute-start.4 = (f32[16,72,128]{2,1,0:T(8,128)S(1)}, f32[16,72,128]{2,1,0:T(8,128)S(1)}, u32[]{:S(2)}, u32[]{:S(2)}) collective-permute-start(f32[16,72,128]{2,1,0:T(8,128)S(1)} %get-tuple-element.66.mid_ref.refs_1_), channel_id=1, source_target_pairs={{1,0},{0,1},{3,2},{2,3},{5,4},{4,5},{7,6},{6,7},{9,8},{8,9},{11,10... | collective-permute-start | bytes 1769480 | tf_op jit(solution)/shard_map/ppermute | solution.py:389
  6.4 15.2 %collective-permute-start.3 = (f32[68,128]{1,0:T(8,128)S(1)}, f32[68,128]{1,0:T(8,128)S(1)}, u32[]{:S(2)}, u32[]{:S(2)}) collective-permute-start(f32[68,128]{1,0:T(8,128)S(1)} %get-tuple-element.41.own_ref), channel_id=1, source_target_pairs={{2,0},{4,2},{6,4},{3,1},{5,3},{7,5},{10,8},{12,10},{14,12},{11,9},... | collective-permute-start | bytes 104456 | tf_op jit(solution)/shard_map/ppermute | solution.py:412
  7.7 13.9 %collective-permute-start.2 = (f32[68,128]{1,0:T(8,128)S(1)}, f32[68,128]{1,0:T(8,128)S(1)}, u32[]{:S(2)}, u32[]{:S(2)}) collective-permute-start(f32[68,128]{1,0:T(8,128)S(1)} %get-tuple-element.41.own_ref), channel_id=1, source_target_pairs={{0,2},{2,4},{4,6},{1,3},{3,5},{5,7},{8,10},{10,12},{12,14},{9,11},... | collective-permute-start | bytes 104456 | tf_op jit(solution)/shard_map/ppermute | solution.py:411
  11.7 9.9 %collective-permute-start = (f32[2,68,128]{2,1,0:T(8,128)S(1)}, f32[2,68,128]{2,1,0:T(8,128)S(1)}, u32[]{:S(2)}, u32[]{:S(2)}) collective-permute-start(f32[2,68,128]{2,1,0:T(8,128)S(1)} %get-tuple-element.39), channel_id=1, source_target_pairs={{0,8},{8,16},{16,24},{1,9},{9,17},{17,25},{2,10},{10,18},{18,26},{... | collective-permute-start | bytes 208904 | tf_op jit(solution)/shard_map/ppermute | solution.py:409
  16.2 5.7 %collective-permute-start.1 = (f32[2,68,128]{2,1,0:T(8,128)S(1)}, f32[2,68,128]{2,1,0:T(8,128)S(1)}, u32[]{:S(2)}, u32[]{:S(2)}) collective-permute-start(f32[2,68,128]{2,1,0:T(8,128)S(1)} %get-tuple-element.40), channel_id=1, source_target_pairs={{8,0},{16,8},{24,16},{9,1},{17,9},{25,17},{10,2},{18,10},{26,18},{... | collective-permute-start | bytes 208904 | tf_op jit(solution)/shard_map/ppermute | solution.py:410
  22.3 19.7 %collective-permute-start.5 = (f32[18,72,128]{2,1,0:T(8,128)S(1)}, f32[18,72,128]{2,1,0:T(8,128)S(1)}, u32[]{:S(2)}, u32[]{:S(2)}) collective-permute-start(f32[18,72,128]{2,1,0:T(8,128)S(1)} %get-tuple-element.65.refs_0_), channel_id=1, source_target_pairs={{1,0},{0,1},{3,2},{2,3},{5,4},{4,5},{7,6},{6,7},{9,8},{8,9},{11,10... | collective-permute-start | bytes 1990664 | tf_op jit(solution)/shard_map/ppermute | solution.py:389
  22.6 8.3 %collective-permute-start.7 = (f32[8,72,128]{2,1,0:T(8,128)S(1)}, f32[8,72,128]{2,1,0:T(8,128)S(1)}, u32[]{:S(2)}, u32[]{:S(2)}) collective-permute-start(f32[8,72,128]{2,1,0:T(8,128)S(1)} %get-tuple-element.55.low_ref.low), channel_id=1, source_target_pairs={{8,0},{16,8},{24,16},{9,1},{17,9},{25,17},{10,2},{18,10},{26,18},{... | collective-permute-start | bytes 884744 | tf_op jit(solution)/shard_map/ppermute | solution.py:462
  24.8 7.1 %collective-permute-start.6 = (f32[8,72,128]{2,1,0:T(8,128)S(1)}, f32[8,72,128]{2,1,0:T(8,128)S(1)}, u32[]{:S(2)}, u32[]{:S(2)}) collective-permute-start(f32[8,72,128]{2,1,0:T(8,128)S(1)} %get-tuple-element.56.high_ref.high), channel_id=1, source_target_pairs={{0,8},{8,16},{16,24},{1,9},{9,17},{17,25},{2,10},{10,18},{18,26},{... | collective-permute-start | bytes 884744 | tf_op jit(solution)/shard_map/ppermute | solution.py:461
  32.3 9.7 %collective-permute-start.8 = (f32[3,72,128]{2,1,0:T(8,128)S(1)}, f32[3,72,128]{2,1,0:T(8,128)S(1)}, u32[]{:S(2)}, u32[]{:S(2)}) collective-permute-start(f32[3,72,128]{2,1,0:T(8,128)S(1)} %get-tuple-element.58), channel_id=1, source_target_pairs={{0,2},{2,4},{4,6},{1,3},{3,5},{5,7},{8,10},{10,12},{12,14},{9,11},... | collective-permute-start | bytes 331784 | tf_op jit(solution)/shard_map/ppermute | solution.py:473
  35.5 6.5 %collective-permute-start.9 = (f32[3,72,128]{2,1,0:T(8,128)S(1)}, f32[3,72,128]{2,1,0:T(8,128)S(1)}, u32[]{:S(2)}, u32[]{:S(2)}) collective-permute-start(f32[3,72,128]{2,1,0:T(8,128)S(1)} %get-tuple-element.59), channel_id=1, source_target_pairs={{2,0},{4,2},{6,4},{3,1},{5,3},{7,5},{10,8},{12,10},{14,12},{11,9},... | collective-permute-start | bytes 331784 | tf_op jit(solution)/shard_map/ppermute | solution.py:474
  42.1 14.4 %collective-permute-start.11 = (f32[8,72,128]{2,1,0:T(8,128)S(1)}, f32[8,72,128]{2,1,0:T(8,128)S(1)}, u32[]{:S(2)}, u32[]{:S(2)}) collective-permute-start(f32[8,72,128]{2,1,0:T(8,128)S(1)} %get-tuple-element.75), channel_id=1, source_target_pairs={{8,0},{16,8},{24,16},{9,1},{17,9},{25,17},{10,2},{18,10},{26,18},{... | collective-permute-start | bytes 884744 | tf_op jit(solution)/shard_map/ppermute | solution.py:490
  44.0 12.5 %collective-permute-start.10 = (f32[8,72,128]{2,1,0:T(8,128)S(1)}, f32[8,72,128]{2,1,0:T(8,128)S(1)}, u32[]{:S(2)}, u32[]{:S(2)}) collective-permute-start(f32[8,72,128]{2,1,0:T(8,128)S(1)} %get-tuple-element.76), channel_id=1, source_target_pairs={{0,8},{8,16},{16,24},{1,9},{9,17},{17,25},{2,10},{10,18},{18,26},{... | collective-permute-start | bytes 884744 | tf_op jit(solution)/shard_map/ppermute | solution.py:489
  48.8 7.7 %collective-permute-start.12 = (f32[3,72,128]{2,1,0:T(8,128)S(1)}, f32[3,72,128]{2,1,0:T(8,128)S(1)}, u32[]{:S(2)}, u32[]{:S(2)}) collective-permute-start(f32[3,72,128]{2,1,0:T(8,128)S(1)} %collective-permute-done.8.refs_4_), channel_id=1, source_target_pairs={{1,0},{0,1},{3,2},{2,3},{5,4},{4,5},{7,6},{6,7},{9,8},{8,9},{11,10... | collective-permute-start | bytes 331784 | tf_op jit(solution)/shard_map/ppermute | solution.py:389
  50.1 6.4 %collective-permute-start.13 = (f32[3,72,128]{2,1,0:T(8,128)S(1)}, f32[3,72,128]{2,1,0:T(8,128)S(1)}, u32[]{:S(2)}, u32[]{:S(2)}) collective-permute-start(f32[3,72,128]{2,1,0:T(8,128)S(1)} %collective-permute-done.9.refs_5_), channel_id=1, source_target_pairs={{1,0},{0,1},{3,2},{2,3},{5,4},{4,5},{7,6},{6,7},{9,8},{8,9},{11,10... | collective-permute-start | bytes 331784 | tf_op jit(solution)/shard_map/ppermute | solution.py:389

commit v6 on v5

--- a/solution.py
+++ b/solution.py
@@ -208,7 +208,7 @@
             s_ref[m, pl.ds((3 * g + i) * kp, kp), at] = part
         return _
 
-    lax.fori_loop(0, 8, stage, 0, unroll=4)
+    lax.fori_loop(0, 8, stage, 0, unroll=8)
 
 def stage_sides(z_ref, g, kp, left_ref, right_ref):
     slot = lanes_of() % 16
@@ -241,7 +241,7 @@
             put(t_ref, g_ref, row_of_block(m) + k, HALO, part[k * LANES : (k + 1) * LANES], add)
         return _
 
-    lax.fori_loop(0, s_ref.shape[0], block, 0)
+    lax.fori_loop(0, s_ref.shape[0], block, 0, unroll=2)
 
 def put_sides(t_ref, g_ref, z_ref, w_ref, add):
     part = mix(z_ref[...], w_ref)
@@ -323,7 +323,7 @@
                 nxt[x, here] = (total + t_ref[j, x, pl.ds(y - 8, 8)]) * mask
             return _
 
-        lax.fori_loop(HALO - reach, HALO + rows + reach, sweep, 0, unroll=4)
+        lax.fori_loop(HALO - reach, HALO + rows + reach, sweep, 0, unroll=8)
 
     done = (gb_ref, ga_ref)[(SWEEPS - 1) % 2]
     levels = u_rows.shape[1]
@@ -332,7 +332,7 @@
         h_rows[x] = done[x + HALO - 2, pl.ds(16, LANES)].T[:levels]
         return _
 
-    lax.fori_loop(0, rows + 4, turn, 0, unroll=2)
+    lax.fori_loop(0, rows + 4, turn, 0, unroll=12)
     for copy in loads:
         copy.wait()
 
@@ -356,7 +356,7 @@
             copy.start()
         return _
 
-    lax.fori_loop(0, rows, output, 0, unroll=2)
+    lax.fori_loop(0, rows, output, 0, unroll=8)
     for x in range(rows):
         for copy in stores(x):
             copy.wait()

time: 70.8 us -> 67.3 us (0.951)
  Pallas kernels: 32.6 us -> 28.4 us
    pallas_call x8, Pallas kernels: 32.6 us -> 28.4 us  [call(): pl.pallas_call(body, out_shape=outs, in_specs=specs or [VMEM] * len(args)...]
  transfers between devices with their start and end apart: 14 -> 14, of which waited for: 3 -> 3; matrix products, arithmetic and copies ran while one was open for 0% -> 0% of each run, Pallas kernels for 21% -> 19%
where the time goes in v6:
time: 67.3 us; the launch traced here: 66.7 us
  starting transfers between devices  33.1 us (49%)
  Pallas kernels  28.4 us (42%)
  waiting for transfers between devices  3.81 us (6%)
  between operations  1.1 us (2%)
    pallas_call x8, Pallas kernels, call(): pl.pallas_call(body, out_shape=outs, in_specs=specs or [VMEM] * len(args)...  28.4 us
    ppermute x1, starting transfers between devices, on_device(): belows = [lax.ppermute(e[HALO:2 * HALO], 'gx', x_up) for e in edges[1:]]  5.44 us
    ppermute x1, starting transfers between devices, on_device(): lax.ppermute(hi, 'gx', x_up)  4.55 us
    ppermute x1, starting transfers between devices, on_device(): lax.ppermute(packed, 'gy', y_up)  3.99 us
    ppermute x4, starting transfers between devices, to_others(): lax.ppermute(value, 'lev', [((i + d) % groups, i) for i in range(groups)])  3.96 us
    ppermute x1, starting transfers between devices, on_device(): below = lax.ppermute(high, 'gx', x_up)  3.4 us
    ppermute x1, starting transfers between devices, on_device(): from_left = lax.ppermute(right, 'gy', y_up)  3.21 us
    ppermute x1, waiting for transfers between devices, on_device(): above = lax.ppermute(low, 'gx', x_down)  2.56 us
  transfers between devices with their start and end apart: 14, of which 3 were waited for; matrix products, arithmetic and copies ran while one was open for 0% of the time, Pallas kernels for 19%

profile of v6, /device:TPU:1, one launch (start us, length us, event | category | flops | bytes accessed | tf_op | source)
XLA Modules:
  0.0 66.7 jit_solution(7007859499429558320)
XLA Ops:
  0.7 3.6 %inner_rows.1 = (f32[2,68,128]{2,1,0:T(8,128)S(1)}, f32[2,68,128]{2,1,0:T(8,128)S(1)}, f32[68,128]{1,0:T(8,128)S(1)}, f32[16,72,128]{2,1,0:T(8,128)S(1)}) custom-call(f32[68,32,128]{2,1,0:T(8,128)} %refs_6_.1, f32[68,32,128]{2,1,0:T(8,128)} %refs_7_.1, f32[68,32,128]{2,1,0:T(8,128)} %h_ref.3), custom_call_target="tpu_custom_call" | custom-call | flops 1 | bytes 1 | tf_op jit(solution)/shard_map/inner_rows/pallas_call | solution.py:27
  4.3 2.1 %collective-permute-start.4 = (f32[16,72,128]{2,1,0:T(8,128)S(1)}, f32[16,72,128]{2,1,0:T(8,128)S(1)}, u32[]{:S(2)}, u32[]{:S(2)}) collective-permute-start(f32[16,72,128]{2,1,0:T(8,128)S(1)} %get-tuple-element.66.mid_ref.refs_1_), channel_id=1, source_target_pairs={{1,0},{0,1},{3,2},{2,3},{5,4},{4,5},{7,6},{6,7},{9,8},{8,9},{11,10... | collective-permute-start | bytes 1769480 | tf_op jit(solution)/shard_map/ppermute | solution.py:389
  6.4 1.3 %collective-permute-start.3 = (f32[68,128]{1,0:T(8,128)S(1)}, f32[68,128]{1,0:T(8,128)S(1)}, u32[]{:S(2)}, u32[]{:S(2)}) collective-permute-start(f32[68,128]{1,0:T(8,128)S(1)} %get-tuple-element.41.own_ref), channel_id=1, source_target_pairs={{2,0},{4,2},{6,4},{3,1},{5,3},{7,5},{10,8},{12,10},{14,12},{11,9},... | collective-permute-start | bytes 104456 | tf_op jit(solution)/shard_map/ppermute | solution.py:412
  7.7 4.0 %collective-permute-start.2 = (f32[68,128]{1,0:T(8,128)S(1)}, f32[68,128]{1,0:T(8,128)S(1)}, u32[]{:S(2)}, u32[]{:S(2)}) collective-permute-start(f32[68,128]{1,0:T(8,128)S(1)} %get-tuple-element.41.own_ref), channel_id=1, source_target_pairs={{0,2},{2,4},{4,6},{1,3},{3,5},{5,7},{8,10},{10,12},{12,14},{9,11},... | collective-permute-start | bytes 104456 | tf_op jit(solution)/shard_map/ppermute | solution.py:411
  11.7 4.5 %collective-permute-start = (f32[2,68,128]{2,1,0:T(8,128)S(1)}, f32[2,68,128]{2,1,0:T(8,128)S(1)}, u32[]{:S(2)}, u32[]{:S(2)}) collective-permute-start(f32[2,68,128]{2,1,0:T(8,128)S(1)} %get-tuple-element.39), channel_id=1, source_target_pairs={{0,8},{8,16},{16,24},{1,9},{9,17},{17,25},{2,10},{10,18},{18,26},{... | collective-permute-start | bytes 208904 | tf_op jit(solution)/shard_map/ppermute | solution.py:409
  16.2 1.9 %collective-permute-start.1 = (f32[2,68,128]{2,1,0:T(8,128)S(1)}, f32[2,68,128]{2,1,0:T(8,128)S(1)}, u32[]{:S(2)}, u32[]{:S(2)}) collective-permute-start(f32[2,68,128]{2,1,0:T(8,128)S(1)} %get-tuple-element.40), channel_id=1, source_target_pairs={{8,0},{16,8},{24,16},{9,1},{17,9},{25,17},{10,2},{18,10},{26,18},{... | collective-permute-start | bytes 208904 | tf_op jit(solution)/shard_map/ppermute | solution.py:410
  18.2 3.3 %outer_rows.1 = (f32[8,72,128]{2,1,0:T(8,128)S(1)}, f32[8,72,128]{2,1,0:T(8,128)S(1)}, f32[2,72,128]{2,1,0:T(8,128)S(1)}) custom-call(f32[68,32,128]{2,1,0:T(8,128)} %refs_6_.1, f32[68,32,128]{2,1,0:T(8,128)} %refs_7_.1, f32[68,32,128]{2,1,0:T(8,128)} %h_ref.3, f32[16,72,128]{2,1,0:T(8,128)S(1)} %get-tuple-element.66.mid_ref.refs_1_), custom_call_target="tpu_custom_call" | custom-call | flops 1 | bytes 1 | tf_op jit(solution)/shard_map/outer_rows/pallas_call | solution.py:27
  21.6 0.3 collective-permute-done.1.uhi_ref
  21.9 0.4 outer_fix.1
  22.3 0.3 collective-permute-start.5
  22.6 2.1 %collective-permute-start.7 = (f32[8,72,128]{2,1,0:T(8,128)S(1)}, f32[8,72,128]{2,1,0:T(8,128)S(1)}, u32[]{:S(2)}, u32[]{:S(2)}) collective-permute-start(f32[8,72,128]{2,1,0:T(8,128)S(1)} %get-tuple-element.55.low_ref.low), channel_id=1, source_target_pairs={{8,0},{16,8},{24,16},{9,1},{17,9},{25,17},{10,2},{18,10},{26,18},{... | collective-permute-start | bytes 884744 | tf_op jit(solution)/shard_map/ppermute | solution.py:462
  24.8 3.4 %collective-permute-start.6 = (f32[8,72,128]{2,1,0:T(8,128)S(1)}, f32[8,72,128]{2,1,0:T(8,128)S(1)}, u32[]{:S(2)}, u32[]{:S(2)}) collective-permute-start(f32[8,72,128]{2,1,0:T(8,128)S(1)} %get-tuple-element.56.high_ref.high), channel_id=1, source_target_pairs={{0,8},{8,16},{16,24},{1,9},{9,17},{17,25},{2,10},{10,18},{18,26},{... | collective-permute-start | bytes 884744 | tf_op jit(solution)/shard_map/ppermute | solution.py:461
  28.4 2.6 %collective-permute-done.7.above_ref.above = f32[8,72,128]{2,1,0:T(8,128)S(1)} collective-permute-done((f32[8,72,128]{2,1,0:T(8,128)S(1)}, f32[8,72,128]{2,1,0:T(8,128)S(1)}, u32[]{:S(2)}, u32[]{:S(2)}) %collective-permute-start.7) | collective-permute-done | bytes 294944 | tf_op jit(solution)/shard_map/ppermute | solution.py:462
  30.9 0.9 %collective-permute-done.6.below_ref.below = f32[8,72,128]{2,1,0:T(8,128)S(1)} collective-permute-done((f32[8,72,128]{2,1,0:T(8,128)S(1)}, f32[8,72,128]{2,1,0:T(8,128)S(1)}, u32[]{:S(2)}, u32[]{:S(2)}) %collective-permute-start.6) | collective-permute-done | bytes 294944 | tf_op jit(solution)/shard_map/ppermute | solution.py:461
  31.8 0.4 column_messages.1
  32.3 3.2 %collective-permute-start.8 = (f32[3,72,128]{2,1,0:T(8,128)S(1)}, f32[3,72,128]{2,1,0:T(8,128)S(1)}, u32[]{:S(2)}, u32[]{:S(2)}) collective-permute-start(f32[3,72,128]{2,1,0:T(8,128)S(1)} %get-tuple-element.58), channel_id=1, source_target_pairs={{0,2},{2,4},{4,6},{1,3},{3,5},{5,7},{8,10},{10,12},{12,14},{9,11},... | collective-permute-start | bytes 331784 | tf_op jit(solution)/shard_map/ppermute | solution.py:473
  35.5 1.3 %collective-permute-start.9 = (f32[3,72,128]{2,1,0:T(8,128)S(1)}, f32[3,72,128]{2,1,0:T(8,128)S(1)}, u32[]{:S(2)}, u32[]{:S(2)}) collective-permute-start(f32[3,72,128]{2,1,0:T(8,128)S(1)} %get-tuple-element.59), channel_id=1, source_target_pairs={{2,0},{4,2},{6,4},{3,1},{5,3},{7,5},{10,8},{12,10},{14,12},{11,9},... | collective-permute-start | bytes 331784 | tf_op jit(solution)/shard_map/ppermute | solution.py:474
  36.8 1.6 %weights.1.w_ref = bf16[480,896]{1,0:T(8,128)(2,1)S(1)} custom-call(f32[128,136]{1,0:T(8,128)S(1)} %pad.11.levels_ref, f32[2,136,80]{2,1,0:T(8,128)S(1)} %pad_maximum_fusion.modes_ref, f32[1,136]{1,0:T(1,128)S(1)} %bitcast.7), custom_call_target="tpu_custom_call" | custom-call | flops 1 | bytes 1 | tf_op jit(solution)/shard_map/weights/pallas_call | solution.py:27
  38.5 3.0 %mix_outer.1 = (f32[6,48,144,128]{3,2,1,0:T(8,128)S(1)}, f32[48,160,128]{2,1,0:T(8,128)S(1)}) custom-call(bf16[480,896]{1,0:T(8,128)(2,1)S(1)} %weights.1.w_ref, f32[8,72,128]{2,1,0:T(8,128)S(1)} %get-tuple-element.55.low_ref.low, f32[8,72,128]{2,1,0:T(8,128)S(1)} %get-tuple-element.56.high_ref.high, ...), custom_call_target="tpu_custom_call" | custom-call | flops 1 | bytes 1 | tf_op jit(solution)/shard_map/mix_outer/pallas_call | solution.py:27
  41.6 1.9 %collective-permute-start.11 = (f32[8,72,128]{2,1,0:T(8,128)S(1)}, f32[8,72,128]{2,1,0:T(8,128)S(1)}, u32[]{:S(2)}, u32[]{:S(2)}) collective-permute-start(f32[8,72,128]{2,1,0:T(8,128)S(1)} %get-tuple-element.75), channel_id=1, source_target_pairs={{8,0},{16,8},{24,16},{9,1},{17,9},{25,17},{10,2},{18,10},{26,18},{... | collective-permute-start | bytes 884744 | tf_op jit(solution)/shard_map/ppermute | solution.py:490
  43.5 5.4 %collective-permute-start.10 = (f32[8,72,128]{2,1,0:T(8,128)S(1)}, f32[8,72,128]{2,1,0:T(8,128)S(1)}, u32[]{:S(2)}, u32[]{:S(2)}) collective-permute-start(f32[8,72,128]{2,1,0:T(8,128)S(1)} %get-tuple-element.76), channel_id=1, source_target_pairs={{0,8},{8,16},{16,24},{1,9},{9,17},{17,25},{2,10},{10,18},{18,26},{... | collective-permute-start | bytes 884744 | tf_op jit(solution)/shard_map/ppermute | solution.py:489
  49.0 1.3 %collective-permute-start.12 = (f32[3,72,128]{2,1,0:T(8,128)S(1)}, f32[3,72,128]{2,1,0:T(8,128)S(1)}, u32[]{:S(2)}, u32[]{:S(2)}) collective-permute-start(f32[3,72,128]{2,1,0:T(8,128)S(1)} %collective-permute-done.8.refs_4_), channel_id=1, source_target_pairs={{1,0},{0,1},{3,2},{2,3},{5,4},{4,5},{7,6},{6,7},{9,8},{8,9},{11,10... | collective-permute-start | bytes 331784 | tf_op jit(solution)/shard_map/ppermute | solution.py:389
  50.5 4.4 %mix_inner.1 = (f32[6,48,144,128]{3,2,1,0:T(8,128)S(1)}, f32[48,160,128]{2,1,0:T(8,128)S(1)}) custom-call(bf16[480,896]{1,0:T(8,128)(2,1)S(1)} %weights.1.w_ref, f32[18,72,128]{2,1,0:T(8,128)S(1)} %get-tuple-element.65.refs_0_, f32[16,72,128]{2,1,0:T(8,128)S(1)} %get-tuple-element.66.mid_ref.refs_1_, ...), custom_call_target="tpu_custom_call", output_to_operand_aliasing={{0}: (7, {}), {1}: (8, {})} | custom-call | flops 1 | bytes 1 | tf_op jit(solution)/shard_map/mix_inner/pallas_call | solution.py:27
  54.9 11.6 %finish.1 = (f32[6,48,144,128]{3,2,1,0:T(8,128)S(1)}, f32[48,160,128]{2,1,0:T(8,128)S(1)}, f32[68,32,128]{2,1,0:T(8,128)}, f32[68,32,128]{2,1,0:T(8,128)}, f32[68,32,128]{2,1,0:T(8,128)}) custom-call(s32[2]{0:T(128)S(1)} %pad_add_fusion.place_ref, bf16[480,896]{1,0:T(8,128)(2,1)S(1)} %weights.1.w_ref, ...), custom_call_target="tpu_custom_call", output_to_operand_aliasing={{0}: (6, {}), {1}: (7, {})} | custom-call | flops 1 | bytes 1 | tf_op jit(solution)/shard_map/finish/pallas_call | solution.py:27
  (25 shorter events, 0.6 us)
Async XLA Ops:
  0.6 27.6 %copy-start = (f32[136,136]{1,0:T(8,128)S(1)}, f32[136,136]{1,0:T(8,128)}, u32[]{:S(2)}) copy-start(f32[136,136]{1,0:T(8,128)} %param.10) | copy-start | bytes 221956
  0.6 27.6 %copy-start.2 = (f32[136,136]{1,0:T(8,128)S(1)}, f32[136,136]{1,0:T(8,128)}, u32[]{:S(2)}) copy-start(f32[136,136]{1,0:T(8,128)} %param.9) | copy-start | bytes 221956
  4.3 32.6 %copy-start.1 = (f32[136]{0:T(256)S(1)}, f32[136]{0:T(256)}, u32[]{:S(2)}) copy-start(f32[136]{0:T(256)} %param.11) | copy-start | bytes 1636
  4.3 17.6 %collective-permute-start.4 = (f32[16,72,128]{2,1,0:T(8,128)S(1)}, f32[16,72,128]{2,1,0:T(8,128)S(1)}, u32[]{:S(2)}, u32[]{:S(2)}) collective-permute-start(f32[16,72,128]{2,1,0:T(8,128)S(1)} %get-tuple-element.66.mid_ref.refs_1_), channel_id=1, source_target_pairs={{1,0},{0,1},{3,2},{2,3},{5,4},{4,5},{7,6},{6,7},{9,8},{8,9},{11,10... | collective-permute-start | bytes 1769480 | tf_op jit(solution)/shard_map/ppermute | solution.py:389
  6.4 15.2 %collective-permute-start.3 = (f32[68,128]{1,0:T(8,128)S(1)}, f32[68,128]{1,0:T(8,128)S(1)}, u32[]{:S(2)}, u32[]{:S(2)}) collective-permute-start(f32[68,128]{1,0:T(8,128)S(1)} %get-tuple-element.41.own_ref), channel_id=1, source_target_pairs={{2,0},{4,2},{6,4},{3,1},{5,3},{7,5},{10,8},{12,10},{14,12},{11,9},... | collective-permute-start | bytes 104456 | tf_op jit(solution)/shard_map/ppermute | solution.py:412
  7.7 13.9 %collective-permute-start.2 = (f32[68,128]{1,0:T(8,128)S(1)}, f32[68,128]{1,0:T(8,128)S(1)}, u32[]{:S(2)}, u32[]{:S(2)}) collective-permute-start(f32[68,128]{1,0:T(8,128)S(1)} %get-tuple-element.41.own_ref), channel_id=1, source_target_pairs={{0,2},{2,4},{4,6},{1,3},{3,5},{5,7},{8,10},{10,12},{12,14},{9,11},... | collective-permute-start | bytes 104456 | tf_op jit(solution)/shard_map/ppermute | solution.py:411
  11.7 9.9 %collective-permute-start = (f32[2,68,128]{2,1,0:T(8,128)S(1)}, f32[2,68,128]{2,1,0:T(8,128)S(1)}, u32[]{:S(2)}, u32[]{:S(2)}) collective-permute-start(f32[2,68,128]{2,1,0:T(8,128)S(1)} %get-tuple-element.39), channel_id=1, source_target_pairs={{0,8},{8,16},{16,24},{1,9},{9,17},{17,25},{2,10},{10,18},{18,26},{... | collective-permute-start | bytes 208904 | tf_op jit(solution)/shard_map/ppermute | solution.py:409
  16.2 5.7 %collective-permute-start.1 = (f32[2,68,128]{2,1,0:T(8,128)S(1)}, f32[2,68,128]{2,1,0:T(8,128)S(1)}, u32[]{:S(2)}, u32[]{:S(2)}) collective-permute-start(f32[2,68,128]{2,1,0:T(8,128)S(1)} %get-tuple-element.40), channel_id=1, source_target_pairs={{8,0},{16,8},{24,16},{9,1},{17,9},{25,17},{10,2},{18,10},{26,18},{... | collective-permute-start | bytes 208904 | tf_op jit(solution)/shard_map/ppermute | solution.py:410
  22.3 19.2 %collective-permute-start.5 = (f32[18,72,128]{2,1,0:T(8,128)S(1)}, f32[18,72,128]{2,1,0:T(8,128)S(1)}, u32[]{:S(2)}, u32[]{:S(2)}) collective-permute-start(f32[18,72,128]{2,1,0:T(8,128)S(1)} %get-tuple-element.65.refs_0_), channel_id=1, source_target_pairs={{1,0},{0,1},{3,2},{2,3},{5,4},{4,5},{7,6},{6,7},{9,8},{8,9},{11,10... | collective-permute-start | bytes 1990664 | tf_op jit(solution)/shard_map/ppermute | solution.py:389
  22.6 8.3 %collective-permute-start.7 = (f32[8,72,128]{2,1,0:T(8,128)S(1)}, f32[8,72,128]{2,1,0:T(8,128)S(1)}, u32[]{:S(2)}, u32[]{:S(2)}) collective-permute-start(f32[8,72,128]{2,1,0:T(8,128)S(1)} %get-tuple-element.55.low_ref.low), channel_id=1, source_target_pairs={{8,0},{16,8},{24,16},{9,1},{17,9},{25,17},{10,2},{18,10},{26,18},{... | collective-permute-start | bytes 884744 | tf_op jit(solution)/shard_map/ppermute | solution.py:462
  24.8 7.1 %collective-permute-start.6 = (f32[8,72,128]{2,1,0:T(8,128)S(1)}, f32[8,72,128]{2,1,0:T(8,128)S(1)}, u32[]{:S(2)}, u32[]{:S(2)}) collective-permute-start(f32[8,72,128]{2,1,0:T(8,128)S(1)} %get-tuple-element.56.high_ref.high), channel_id=1, source_target_pairs={{0,8},{8,16},{16,24},{1,9},{9,17},{17,25},{2,10},{10,18},{18,26},{... | collective-permute-start | bytes 884744 | tf_op jit(solution)/shard_map/ppermute | solution.py:461
  32.3 9.2 %collective-permute-start.8 = (f32[3,72,128]{2,1,0:T(8,128)S(1)}, f32[3,72,128]{2,1,0:T(8,128)S(1)}, u32[]{:S(2)}, u32[]{:S(2)}) collective-permute-start(f32[3,72,128]{2,1,0:T(8,128)S(1)} %get-tuple-element.58), channel_id=1, source_target_pairs={{0,2},{2,4},{4,6},{1,3},{3,5},{5,7},{8,10},{10,12},{12,14},{9,11},... | collective-permute-start | bytes 331784 | tf_op jit(solution)/shard_map/ppermute | solution.py:473
  35.5 6.0 %collective-permute-start.9 = (f32[3,72,128]{2,1,0:T(8,128)S(1)}, f32[3,72,128]{2,1,0:T(8,128)S(1)}, u32[]{:S(2)}, u32[]{:S(2)}) collective-permute-start(f32[3,72,128]{2,1,0:T(8,128)S(1)} %get-tuple-element.59), channel_id=1, source_target_pairs={{2,0},{4,2},{6,4},{3,1},{5,3},{7,5},{10,8},{12,10},{14,12},{11,9},... | collective-permute-start | bytes 331784 | tf_op jit(solution)/shard_map/ppermute | solution.py:474
  41.6 13.3 %collective-permute-start.11 = (f32[8,72,128]{2,1,0:T(8,128)S(1)}, f32[8,72,128]{2,1,0:T(8,128)S(1)}, u32[]{:S(2)}, u32[]{:S(2)}) collective-permute-start(f32[8,72,128]{2,1,0:T(8,128)S(1)} %get-tuple-element.75), channel_id=1, source_target_pairs={{8,0},{16,8},{24,16},{9,1},{17,9},{25,17},{10,2},{18,10},{26,18},{... | collective-permute-start | bytes 884744 | tf_op jit(solution)/shard_map/ppermute | solution.py:490
  43.5 11.4 %collective-permute-start.10 = (f32[8,72,128]{2,1,0:T(8,128)S(1)}, f32[8,72,128]{2,1,0:T(8,128)S(1)}, u32[]{:S(2)}, u32[]{:S(2)}) collective-permute-start(f32[8,72,128]{2,1,0:T(8,128)S(1)} %get-tuple-element.76), channel_id=1, source_target_pairs={{0,8},{8,16},{16,24},{1,9},{9,17},{17,25},{2,10},{10,18},{18,26},{... | collective-permute-start | bytes 884744 | tf_op jit(solution)/shard_map/ppermute | solution.py:489
  49.0 5.9 %collective-permute-start.12 = (f32[3,72,128]{2,1,0:T(8,128)S(1)}, f32[3,72,128]{2,1,0:T(8,128)S(1)}, u32[]{:S(2)}, u32[]{:S(2)}) collective-permute-start(f32[3,72,128]{2,1,0:T(8,128)S(1)} %collective-permute-done.8.refs_4_), channel_id=1, source_target_pairs={{1,0},{0,1},{3,2},{2,3},{5,4},{4,5},{7,6},{6,7},{9,8},{8,9},{11,10... | collective-permute-start | bytes 331784 | tf_op jit(solution)/shard_map/ppermute | solution.py:389
  50.2 4.6 %collective-permute-start.13 = (f32[3,72,128]{2,1,0:T(8,128)S(1)}, f32[3,72,128]{2,1,0:T(8,128)S(1)}, u32[]{:S(2)}, u32[]{:S(2)}) collective-permute-start(f32[3,72,128]{2,1,0:T(8,128)S(1)} %collective-permute-done.9.refs_5_), channel_id=1, source_target_pairs={{1,0},{0,1},{3,2},{2,3},{5,4},{4,5},{7,6},{6,7},{9,8},{8,9},{11,10... | collective-permute-start | bytes 331784 | tf_op jit(solution)/shard_map/ppermute | solution.py:389
